TPU v7x, 128 devices: a whole 4x4x4 slice. The times are simulated.
128 devices in a mesh: week: 4 (over x), row: 4 (over z), col: 8 (over y, core).
Axes of the slice: x: 4, y: 4, z: 4, core: 2. Of those that a mesh axis runs over, the one named last changes fastest.
Arguments:
- sensitivity: bfloat16 [4, 3, 1024, 4096], P('week', None, None, ('row', 'col')), may hold values from -0.1875 to 0.1875
- reach: int32 [4, 1024], P('week'), may hold values from 0 to 2, as said below
- obs_weight: float32 [4, 1024], P('week'), may hold values from 0.25 to 4
- prior_precision: float32 [4, 4096], P('week', ('row', 'col')), may hold values from 0.5 to 4
- pivot_solve: bfloat16 [4096, 4096], P('week', ('row', 'col')), may hold values from -0.09375 to 0.09375
Outputs:
- hessian_band: float32 [4, 3, 4096, 4096], P('week', None, ('row', 'col'))
- panel: bfloat16 [4096, 4096], P(('row', 'col'), 'week')
- schur: float32 [4096, 4096], P(('row', 'col'), 'week')
Inputs may be any that keep to these rules, and one draw needn't show every extreme that they name: The number of observations at each reach differs widely from week to week; in some week w >= 2 every observation has reach 2.
All inputs are finite; a program needn't handle non-finite values.
Results may differ from a plain program's by a relative error of at most 0.013.
Values may be sent and summed in bfloat16 or wider, within the bound.
No kernel may reach another device: no remote copies, remote signals or barrier semaphores. Data moves between devices by JAX's collectives and lax.ppermute only.
A program may use at most 128 MiB of HBM per device.

v0:
```python
import jax
import jax.numpy as jnp
from jax import lax
from jax.sharding import PartitionSpec as P


def from_behind(block, axis, distance):
    devices = range(lax.axis_size(axis))
    route = [(i - distance, i) for i in devices if i - distance in devices]
    return lax.ppermute(block, axis, route)


def picked(shard, axis, root):
    return lax.dynamic_index_in_dim(lax.all_gather(shard, axis), root, 0, keepdims=False)


def split_up(shard, dim, length):
    dims = shard.shape
    blocks = shard.reshape(*dims[:dim], length, dims[dim] // length, *dims[dim + 1 :])
    return jnp.moveaxis(blocks, dim, 0)


def sent_and_summed(shard, axis, dim):
    blocks = split_up(shard, dim, lax.axis_size(axis))
    arrived = lax.all_to_all(blocks, axis, split_axis=0, concat_axis=0, tiled=True)
    return arrived.astype(jnp.float32).sum(axis=0)


def contract_first(left, right):
    return lax.dot_general(
        left, right, (((0,), (0,)), ((), ())), preferred_element_type=jnp.float32
    )


def contract_last(left, right):
    return lax.dot_general(
        left, right, (((1,), (1,)), ((), ())), preferred_element_type=jnp.float32
    )


def lag_pairs(firsts, lags):
    return [(a, b) for a in firsts for b in range(a, lags)]


def weighted(source, offset, pairs, reach_here, weight_here, week_of):
    result = []
    for a, b in pairs:
        keep = jnp.where((reach_here >= b) & (week_of >= b), weight_here, 0.0)
        result.append((keep[:, None] * source[a - offset].astype(jnp.float32)).astype(jnp.bfloat16))
    return result


def products(lefts, right, offset, pairs):
    result = []
    for position in range(len(pairs)):
        result.append(contract_first(lefts[position], right[pairs[position][1] - offset]))
    return jnp.stack(result)


def body(sensitivity, reach, obs_weight, prior_precision, pivot_solve):
    week = lax.axis_index("week")
    n_row = lax.axis_size("row")
    n_col = lax.axis_size("col")
    local = sensitivity[0]
    lags = local.shape[0]
    slim = local.shape[2]
    regions = slim * n_row * n_col
    reach_here = reach[0]
    weight_here = obs_weight[0]
    starts = [sum((lags - k for k in range(a))) for a in range(lags)]
    local_pairs = lag_pairs(range(lags), lags)
    lefts = weighted(local, 0, local_pairs, reach_here, weight_here, week)
    partial_blocks = products(
        lefts, lax.all_gather(local, ("row", "col"), axis=2, tiled=True), 0, local_pairs
    )
    bands = partial_blocks[0:lags]
    for a in range(1, lags):
        received = from_behind(
            partial_blocks[starts[a] : starts[a] + lags - a].astype(jnp.bfloat16), "week", -a
        ).astype(jnp.float32)
        bands = bands.at[: lags - a].add(received)
    first_row = (lax.axis_index("row") * n_col + lax.axis_index("col")) * slim
    row_ids = lax.broadcasted_iota(jnp.int32, (slim, regions), 0)
    col_ids = lax.broadcasted_iota(jnp.int32, (slim, regions), 1)
    diagonal = jnp.where(col_ids == row_ids + first_row, prior_precision[0][:, None], 0.0)
    bands = bands.at[0].add(diagonal)
    coupling = picked(bands[1].astype(jnp.bfloat16), "week", 1)
    panel_sum = contract_last(
        coupling, lax.all_gather(pivot_solve, ("row", "col"), axis=1, tiled=True)
    )
    panel = panel_sum.astype(jnp.bfloat16)
    gram = contract_last(panel, lax.all_gather(panel, ("row", "col"), axis=0, tiled=True))
    term = jnp.where(week == 1, bands[0], 0.0) - gram
    schur = sent_and_summed(term.astype(jnp.bfloat16), "week", 1)
    return (bands[None], panel, schur)


def solution(mesh):
    placed = (
        P("week", None, None, ("row", "col")),
        P("week", None),
        P("week", None),
        P("week", ("row", "col")),
        P("week", ("row", "col")),
    )
    return jax.shard_map(
        body,
        mesh=mesh,
        in_specs=placed,
        out_specs=(
            P("week", None, ("row", "col"), None),
            P(("row", "col"), "week"),
            P(("row", "col"), "week"),
        ),
        check_vma=False,
    )
```

profile of v0, /device:TPU:2, one launch (start us, length us, event | category | flops | bytes accessed | tf_op | source)
XLA Modules:
  0.0 346.1 jit_solution(5114212472843733637)
XLA Ops:
  7.2 0.0 all-gather.12.cloned.1.call-start
  7.2 0.7 all-gather.12.cloned.1.call-update
  7.9 0.0 all-gather.8.cloned.1.call-start
  7.9 0.0 copy-start.3
  8.0 0.7 all-gather.8.cloned.1.call-update
  8.6 0.0 all-gather.6.cloned.1.call-start
  8.7 0.7 and_select_fusion.2
  9.5 106.4 %all-gather.12.cloned.1.call-done = bf16[1,3,1024,4096]{3,2,1,0:T(8,128)(2,1)} async-done(((bf16[1,3,1024,128]{3,2,1,0:T(8,128)(2,1)}), bf16[1,3,1024,4096]{3,2,1,0:T(8,128)(2,1)}) %all-gather.12.cloned.1.call-update) | async-done | bytes 25165840 | tf_op jit(solution)/shard_map/all_gather | solution.py:74
  115.9 0.0 copy-start
  115.9 5.0 %fusion.13 = bf16[1,128,4096]{2,1,0:T(8,128)(2,1)S(1)} fusion(bf16[1,3,1024,4096]{3,2,1,0:T(8,128)(2,1)} %all-gather.12.cloned.1.call-done, bf16[1,3,1024,128]{3,2,1,0:T(8,128)(2,1)} %param.11, f32[1024]{0:T(1024)S(1)} %bitcast.86), kind=kOutput, calls=%fused_computation.17 | convolution fusion | flops 1074659328 | bytes 9703424 | tf_op jit(solution)/shard_map/dot_general | solution.py:30
  120.9 1.6 collective-permute-start.1
  122.4 0.0 copy-done.3
  122.4 5.5 %fusion.14 = bf16[1,128,4096]{2,1,0:T(8,128)(2,1)S(1)} fusion(bf16[1,3,1024,4096]{3,2,1,0:T(8,128)(2,1)} %all-gather.12.cloned.1.call-done, f32[1024]{0:T(1024)S(1)} %bitcast.87, bf16[1,3,1024,128]{3,2,1,0:T(8,128)(2,1)S(1)} %copy-done.3), kind=kOutput, calls=%fused_computation.18 | convolution fusion | flops 1074659328 | bytes 9703424 | tf_op jit(solution)/shard_map/dot_general | solution.py:30
  127.9 5.0 %fusion.12 = bf16[1,128,4096]{2,1,0:T(8,128)(2,1)S(1)} fusion(bf16[1,3,1024,4096]{3,2,1,0:T(8,128)(2,1)} %all-gather.12.cloned.1.call-done, f32[1024]{0:T(1024)S(1)} %bitcast.89, bf16[1,3,1024,128]{3,2,1,0:T(8,128)(2,1)S(1)} %copy-done.3), kind=kOutput, calls=%fused_computation.16 | convolution fusion | flops 1074659328 | bytes 9703424 | tf_op jit(solution)/shard_map/dot_general | solution.py:30
  132.9 1.5 pad_maximum_fusion.1
  134.4 2.5 collective-permute-start
  136.9 0.0 copy-done
  136.9 1.4 fusion.7
  138.3 1.4 fusion.6
  139.7 1.4 fusion.8
  141.1 0.7 pad_maximum_fusion
  141.8 53.3 %collective-permute-done = bf16[2,128,4096]{2,1,0:T(8,128)(2,1)} collective-permute-done((bf16[2,128,4096]{2,1,0:T(8,128)(2,1)}, bf16[2,128,4096]{2,1,0:T(8,128)(2,1)}, u32[]{:S(2)}, u32[]{:S(2)}) %collective-permute-start) | collective-permute-done | bytes 2097184 | tf_op jit(solution)/shard_map/ppermute | solution.py:10
  195.0 2.8 constant_dynamic-update-slice_fusion
  197.8 0.0 copy-start.1
  197.8 0.0 copy-start.4
  197.9 0.0 collective-permute-done.1
  197.9 0.2 fusion.17
  198.1 0.4 copy-done.4
  198.5 0.4 fusion.16
  199.0 0.8 copy-done.1
  199.8 0.0 copy-start.2
  199.8 2.7 copy-done.2
  202.5 1.1 slice.180
  203.6 0.0 all-gather.6.cloned.1.call-update
  203.6 0.2 all-gather.10.cloned.1.call-start
  203.9 0.0 all-gather.8.cloned.1.call-done
  203.9 47.4 %all-gather.6.cloned.1.call-done = bf16[4,128,4096]{2,1,0:T(8,128)(2,1)} async-done(((bf16[1,128,4096]{2,1,0:T(8,128)(2,1)}), bf16[4,128,4096]{2,1,0:T(8,128)(2,1)}) %all-gather.6.cloned.1.call-update) | async-done | bytes 4194320 | tf_op jit(solution)/shard_map/all_gather | solution.py:14
  251.3 7.3 %convolution_convert_fusion = bf16[128,1024]{1,0:T(8,128)(2,1)} fusion(bf16[1024,4096]{1,0:T(8,128)(2,1)} %all-gather.8.cloned.1.call-done, bf16[4,128,4096]{2,1,0:T(8,128)(2,1)} %all-gather.6.cloned.1.call-done), kind=kOutput, calls=%fused_computation.29 | convolution fusion | flops 1073872896 | bytes 9699328 | tf_op jit(solution)/shard_map/dot_general | solution.py:36
  258.6 0.0 all-gather.10.cloned.1.call-update
  258.7 54.1 %all-gather.10.cloned.1.call-done = bf16[4096,1024]{1,0:T(8,128)(2,1)} async-done(((bf16[128,1024]{1,0:T(8,128)(2,1)}), bf16[4096,1024]{1,0:T(8,128)(2,1)}) %all-gather.10.cloned.1.call-update) | async-done | bytes 8388624 | tf_op jit(solution)/shard_map/all_gather | solution.py:92
  312.8 7.0 %fusion.15 = bf16[128,4096]{1,0:T(8,128)(2,1)S(1)} fusion(f32[128]{0:T(128)S(1)} %bitcast.92, s32[128]{0:T(128)S(1)} %iota_add_fusion, pred[]{:T(512)S(6)} %eq.12, bf16[1,128,4096]{2,1,0:T(8,128)(2,1)S(1)} %collective-permute-done.1, f32[2,128,4096]{2,1,0:T(8,128)} %copy-done.1, bf16[128,1024]{1,0:T(8,128)(2,1)} %convolution_convert_fusion, ...), kind=kOutput, calls=%fused_computation.24 | convolution fusion | flops 1077936128 | bytes 12846081 | tf_op jit(solution)/shard_map/dot_general | solution.py:36
  319.8 0.1 copy.11
  319.9 18.7 %all_to_all.5 = bf16[4,128,1024]{2,1,0:T(8,128)(2,1)S(1)} all-to-all(bf16[4,128,1024]{2,1,0:T(8,128)(2,1)S(1)} %bitcast.83), channel_id=1, replica_groups=mesh['week'=4,'row'=4,'col'=8] {'week'}, dimensions={0} | all-to-all | bytes 2097152 | tf_op jit(solution)/shard_map/all_to_all | solution.py:25
  338.6 1.0 convert_reduce_fusion
  (1 shorter events, 0.0 us)
Async XLA Ops:
  7.2 108.7 %all-gather.12.cloned.1.call-start = ((), (), s32[]{:S(2)}) async-start(), calls=%async_computation.4 | async-start | bytes 25952256 | tf_op jit(solution)/shard_map/all_gather | solution.py:74
  7.9 196.0 %all-gather.8.cloned.1.call-start = ((), (), s32[]{:S(2)}) async-start(), calls=%async_computation.2 | async-start | bytes 8650752 | tf_op jit(solution)/shard_map/all_gather | solution.py:89
  7.9 114.5 %copy-start.3 = (bf16[1,3,1024,128]{3,2,1,0:T(8,128)(2,1)S(1)}, bf16[1,3,1024,128]{3,2,1,0:T(8,128)(2,1)}, u32[]{:S(2)}) copy-start(bf16[1,3,1024,128]{3,2,1,0:T(8,128)(2,1)} %param.11) | copy-start | bytes 2359300
  8.6 242.7 %all-gather.6.cloned.1.call-start = ((), (), s32[]{:S(2)}) async-start(), calls=%async_computation.1 | async-start | bytes 5242880 | tf_op jit(solution)/shard_map/all_gather | solution.py:14
  115.9 21.0 %copy-start = (bf16[1,3,1024,4096]{3,2,1,0:T(8,128)(2,1)S(1)}, bf16[1,3,1024,4096]{3,2,1,0:T(8,128)(2,1)}, u32[]{:S(2)}) copy-start(bf16[1,3,1024,4096]{3,2,1,0:T(8,128)(2,1)} %all-gather.12.cloned.1.call-done) | copy-start | bytes 75497472
  120.9 77.0 %collective-permute-start.1 = (bf16[1,128,4096]{2,1,0:T(8,128)(2,1)S(1)}, bf16[1,128,4096]{2,1,0:T(8,128)(2,1)S(1)}, u32[]{:S(2)}, u32[]{:S(2)}) collective-permute-start(bf16[1,128,4096]{2,1,0:T(8,128)(2,1)S(1)} %fusion.13), channel_id=1, source_target_pairs={{64,0},{96,32},{65,1},{97,33},{66,2},{98,34},{67,3},{99,35},{68,4}... | collective-permute-start | bytes 3145736 | tf_op jit(solution)/shard_map/ppermute | solution.py:10
  134.4 60.6 %collective-permute-start = (bf16[2,128,4096]{2,1,0:T(8,128)(2,1)}, bf16[2,128,4096]{2,1,0:T(8,128)(2,1)}, u32[]{:S(2)}, u32[]{:S(2)}) collective-permute-start(bf16[2,128,4096]{2,1,0:T(8,128)(2,1)} %pad_maximum_fusion.1), channel_id=1, source_target_pairs={{32,0},{64,32},{96,64},{33,1},{65,33},{97,65},{34,2},{66,34},{98,6... | collective-permute-start | bytes 6291464 | tf_op jit(solution)/shard_map/ppermute | solution.py:10
  197.8 2.0 copy-start.1
  197.8 0.7 copy-start.4
  199.8 2.7 copy-start.2
  203.6 109.2 %all-gather.10.cloned.1.call-start = ((), (), s32[]{:S(2)}) async-start(), calls=%async_computation.3 | async-start | bytes 8650752 | tf_op jit(solution)/shard_map/all_gather | solution.py:92
Sparse Core Ops, SparseCore 0:
  10.2 105.6 all-gather.11
  118.0 60.4 all-gather.7
  203.8 47.5 all-gather.5
  258.8 53.9 all-gather.9
where the time goes:
time: 347 us; the launch traced here: 346 us
  waiting for transfers between devices  263 us (76%)
  matrix products  34 us (10%)
  blocking collectives  18.7 us (5%)
  between operations  13.9 us (4%)
  other arithmetic  7.36 us (2%)
  local copies, waits for them, and re-layouts  5.19 us (1%)
  starting transfers between devices  4.35 us (1%)
    all_gather x1, waiting for transfers between devices, body(): lax.all_gather(local, ('row', 'col'), axis=2, tiled=True)  106 us
    all_gather x1, waiting for transfers between devices, body(): lax.all_gather(panel, ('row', 'col'), axis=0, tiled=True)  54.1 us
    ppermute x2, waiting for transfers between devices, from_behind(): return lax.ppermute(block, axis, route)  53.3 us
    all_gather x1, waiting for transfers between devices, picked(): lax.all_gather(shard, axis)  47.4 us
    dot_general x6, matrix products, contract_first(): lax.dot_general(left, right, (((0,), (0,)), ((), ())), preferred_element_...  19.6 us
    all_to_all x1, blocking collectives, sent_and_summed(): lax.all_to_all(blocks, axis, split_axis=0, concat_axis=0, tiled=True)  18.7 us
    dot_general x2, matrix products, contract_last(): lax.dot_general(left, right, (((1,), (1,)), ((), ())), preferred_element_...  14.3 us
  transfers between devices with their start and end apart: 6, of which 4 were waited for; matrix products, arithmetic and copies ran while one was open for 8% of the time, Pallas kernels for 0%

commit v1 on v0

v1 whole, which is shorter than its diff:
```python
import jax
import jax.numpy as jnp
from jax import lax
from jax.experimental import pallas as pl
from jax.experimental.pallas import tpu as pltpu
from jax.sharding import PartitionSpec as P

AXES = ("week", "row", "col")


def moved(block, sizes, dw=0, dz=0, dy=0, dk=0, weeks=None):
    n_week, n_row, n_col = sizes
    n_y = n_col // 2
    route = []
    for w in range(n_week):
        if weeks is not None and w not in weeks:
            continue
        for z in range(n_row):
            for y in range(n_y):
                for k in range(2):
                    here = (w * n_row + z) * n_col + y * 2 + k
                    to = (((w + dw) % n_week) * n_row + (z + dz) % n_row) * n_col
                    to += ((y + dy) % n_y) * 2 + (k + dk) % 2
                    route.append((here, to))
    return lax.ppermute(block, AXES, route)


HBM = pl.BlockSpec(memory_space=pl.ANY)
VMEM = pl.BlockSpec(memory_space=pltpu.VMEM)
SMEM = pl.BlockSpec(memory_space=pltpu.SMEM)
LIMIT = pltpu.CompilerParams(vmem_limit_bytes=48 * 1024 * 1024)
bf = jnp.bfloat16
f32 = jnp.float32


def contract_first(left, right):
    return lax.dot_general(
        left, right, (((0,), (0,)), ((), ())), preferred_element_type=jnp.float32
    )


def dot_first(left, right):
    return lax.dot_general(
        left, right, (((0,), (0,)), ((), ())), preferred_element_type=jnp.float32
    )


def dot_last(left, right):
    return lax.dot_general(
        left, right, (((1,), (1,)), ((), ())), preferred_element_type=jnp.float32
    )


def brought(copies, sems):
    started = []
    for n, (source, target) in enumerate(copies):
        copy = pltpu.make_async_copy(source, target, sems.at[n])
        copy.start()
        started.append(copy)
    for copy in started:
        copy.wait()


def left_copies(pieces, scratch, a, obs, slim):
    rows = pl.ds(a * obs, obs)
    return [
        (ref, scratch.at[t // 2, rows, pl.ds((t % 2) * slim, slim)])
        for t, ref in enumerate(pieces)
    ]


def right_copies(pieces, scratch, a, obs, slim):
    rows = pl.ds(a * obs, obs)
    return [(ref, scratch.at[rows, pl.ds(n * slim, slim)]) for n, ref in enumerate(pieces)]


def cut(refs, *lengths):
    parts, at = [], 0
    for length in lengths:
        parts.append(refs[at : at + length])
        at += length
    return parts + [refs[at:]]


def coupling_and_parts(lefts, rights, pivots):
    n_a, obs, slim = rights[0].shape
    n_r, n_c, wide = len(lefts), len(rights), pivots[0].shape[0]
    pairs = n_r // 2

    def kernel(*refs):
        la, ra, pv, rest = cut(refs, n_r, n_c, n_c)
        parts, (l_s, r_s, p_s, sems) = rest[:n_r], rest[n_r:]
        copies = right_copies(pv, p_s, 0, wide, slim)
        for a in range(n_a):
            copies += left_copies([ref.at[a] for ref in la], l_s, a, obs, slim)
            copies += right_copies([ref.at[a] for ref in ra], r_s, a, obs, slim)
        brought(copies, sems)
        for n in range(pairs):
            block = dot_first(l_s[n], r_s[...]).astype(bf)
            part = dot_last(block, p_s[...])
            for m in range(2):
                out = parts[2 * n + m]
                out[...] = part[m * slim : (m + 1) * slim].astype(out.dtype)

    operands = [*lefts, *rights, *pivots]
    return pl.pallas_call(
        kernel,
        in_specs=[VMEM] * len(operands),
        out_specs=[VMEM] * n_r,
        out_shape=[jax.ShapeDtypeStruct((slim, wide), bf if t else f32) for t in range(n_r)],
        scratch_shapes=[
            pltpu.VMEM((pairs, n_a * obs, 2 * slim), bf),
            pltpu.VMEM((n_a * obs, n_c * slim), bf),
            pltpu.VMEM((wide, n_c * slim), bf),
            pltpu.SemaphoreType.DMA((n_a * (n_r + n_c) + n_c,)),
        ],
        compiler_params=LIMIT,
        name="coupling_and_parts",
    )(*operands)


def gram_terms(turn, rows_of, slots):
    slim, wide = slots[0].shape
    n_r, n_c = len(rows_of), len(slots)
    pairs, n_j = n_r // 2, n_c // 2

    def kernel(*refs):
        (turn_ref,), l_refs, r_refs, rest = cut(refs, 1, n_r, n_c)
        outs, (l_s, r_s, g_s, sems) = rest[:n_j], rest[n_j:]
        brought(
            [(ref, l_s.at[pl.ds(n * slim, slim)]) for n, ref in enumerate(l_refs)]
            + [(ref, r_s.at[pl.ds(n * slim, slim)]) for n, ref in enumerate(r_refs)],
            sems,
        )
        for n in range(pairs):
            gram = dot_last(l_s[pl.ds(n * 2 * slim, 2 * slim)], r_s[...])
            for e in range(2):
                for s in range(n_j):
                    at = (e * n_j + s) * slim
                    rows, lanes = pl.ds(n * 2 * slim, 2 * slim), pl.ds(e * slim, slim)
                    g_s[s, rows, lanes] = gram[:, at : at + slim]
        for j in range(n_j):
            outs[j][...] = g_s[(turn_ref[0] + n_j - j) % n_j].astype(outs[j].dtype)

    operands = [*rows_of, *slots]
    return pl.pallas_call(
        kernel,
        in_specs=[SMEM] + [VMEM] * len(operands),
        out_specs=[VMEM] * n_j,
        out_shape=[
            jax.ShapeDtypeStruct((n_r * slim, 2 * slim), bf if j else f32) for j in range(n_j)
        ],
        scratch_shapes=[
            pltpu.VMEM((n_r * slim, wide), bf),
            pltpu.VMEM((n_c * slim, wide), bf),
            pltpu.VMEM((n_j, n_r * slim, 2 * slim), f32),
            pltpu.SemaphoreType.DMA((len(operands),)),
        ],
        compiler_params=LIMIT,
        name="gram_terms",
    )(turn.reshape(1), *operands)


def week_sum(terms, n_r):
    rows, wide = terms[0].shape
    slim = rows // n_r

    def kernel(*refs):
        ins, outs = refs[: len(terms)], refs[len(terms) :]
        for n in range(n_r):
            at = pl.ds(n * slim, slim)
            total = ins[0][at].astype(f32)
            for ref in ins[1:]:
                total = total + ref[at].astype(f32)
            outs[n][...] = total.astype(bf)

    return pl.pallas_call(
        kernel,
        in_specs=[VMEM] * len(terms),
        out_specs=[VMEM] * n_r,
        out_shape=[jax.ShapeDtypeStruct((slim, wide), bf)] * n_r,
        name="week_sum",
    )(*terms)


def place_schur(ys, here, pieces):
    slim = pieces[0].shape[0]
    n = len(pieces)

    def kernel(ys_ref, here_ref, *refs):
        for t in range(n):
            for e in range(2):
                at = pl.ds(pl.multiple_of(ys_ref[2 * t + e] * slim, slim), slim)
                block = refs[t][:, e * slim : (e + 1) * slim]
                refs[-1][:, at] = here_ref[:, at] - block.astype(f32)

    return pl.pallas_call(
        kernel,
        in_specs=[SMEM] + [VMEM] * (1 + n),
        out_specs=VMEM,
        out_shape=jax.ShapeDtypeStruct((slim, 2 * n * slim), f32),
        name="place_schur",
    )(ys, here, *pieces)


def body(sensitivity, reach, obs_weight, prior_precision, pivot_solve):
    sizes = tuple(lax.axis_size(a) for a in AXES)
    n_week, n_row, n_col = sizes
    n_y = n_col // 2
    week = lax.axis_index("week")
    z = lax.axis_index("row")
    col = lax.axis_index("col")
    y, k = col // 2, col % 2
    local = sensitivity[0]
    lags, obs, slim = local.shape

    def move(block, **by):
        return moved(block, sizes, **by)

    def over_y(block):
        return [block] + [move(block, dy=t) for t in range(1, n_y)]

    def over_z(block):
        own = [block] + [move(block, dz=s) for s in range(1, n_row)]
        return own + [move(p, dk=1) for p in own]

    def to_rows(blocks):
        return [blocks[0]] + [move(blocks[t], dy=-t) for t in range(1, n_y)]

    def after(value, *events):
        return lax.optimization_barrier((value, *events))[0]

    def by_week(*choices):
        return lax.select_n(week, *choices)

    pivots = over_z(pivot_solve)

    root = jnp.sqrt(obs_weight[0])

    def scaled(lag):
        keep = jnp.where((reach[0] >= lag) & (week >= lag), root, 0.0)
        return (keep[:, None] * local[lag].astype(f32)).astype(bf)

    held = [scaled(lag) for lag in range(lags)]
    pair = jnp.stack(
        [by_week(held[1], held[0], held[1], held[1]), by_week(held[2], held[1], held[2], held[2])]
    )
    below = move(pair, dw=-1, weeks=(1, 2, 3))
    above = move(pair, dw=1, weeks=(1, 2))
    across = move(pair, dw=2, weeks=(1, 2))
    wide = [lax.all_gather(held[lag], ("row", "col"), axis=1, tiled=True) for lag in (2, 1, 0)]

    def both(n):
        first = by_week(below[n], pair[n], pair[n], above[n])
        return jnp.stack([first, by_week(across[n], below[n], above[n], across[n])])

    left_c, right_c = over_y(both(0)), over_z(both(1))
    parts = coupling_and_parts(left_c, right_c, pivots)

    panel = parts[0]
    for t in range(1, n_y):
        panel = panel + move(parts[t], dy=-t).astype(f32)
    panel = panel.astype(bf)
    rows_of = over_y(panel)
    slots = over_z(panel)

    terms = gram_terms((z - week + n_week) % n_week, rows_of, slots)
    terms = [terms[0]] + [move(terms[j], dw=j) for j in range(1, n_week)]
    totals = to_rows(week_sum(terms, n_y))

    mine = after(jnp.concatenate(held[::-1], axis=1), parts[0])
    from_2 = contract_first(mine, wide[0])
    near = move(from_2[slim : 2 * slim].astype(bf), dw=-1, weeks=(2, 3)).astype(f32)
    far = move(from_2[:slim].astype(bf), dw=-2, weeks=(2, 3)).astype(f32)
    from_1 = contract_first(after(mine[:, slim:], panel, near), wide[1])
    next_0 = move(from_1[:slim].astype(bf), dw=-1, weeks=(1, 2, 3)).astype(f32)
    band_2 = from_2[2 * slim :]
    band_1 = from_1[slim:] + near
    from_0 = contract_first(after(held[0], terms[0]), wide[2])
    first = (lax.axis_index("row") * n_col + col) * slim
    rows = lax.broadcasted_iota(jnp.int32, (slim, n_row * n_col * slim), 0)
    cols = lax.broadcasted_iota(jnp.int32, (slim, n_row * n_col * slim), 1)
    diagonal = jnp.where(cols == rows + first, prior_precision[0][:, None], 0.0)
    band_0 = from_0 + next_0 + far + diagonal
    bands = jnp.stack([band_0, band_1, band_2])

    span = n_col * slim
    here = jnp.where(week == 1, band_0[:, span : 2 * span], 0.0)
    for j in range(1, n_week):
        at = (1 + j) % n_week * span
        here = here + move(band_0[:, at : at + span].astype(bf), dw=j, weeks=(1,)).astype(f32)

    ys = [((y + t) % n_y) * 2 + (k + e) % 2 for t in range(n_y) for e in range(2)]
    schur = place_schur(jnp.stack(ys).astype(jnp.int32), here, totals)
    return (bands[None], panel, schur)


def solution(mesh):
    placed = (
        P("week", None, None, ("row", "col")),
        P("week", None),
        P("week", None),
        P("week", ("row", "col")),
        P("week", ("row", "col")),
    )
    return jax.shard_map(
        body,
        mesh=mesh,
        in_specs=placed,
        out_specs=(
            P("week", None, ("row", "col"), None),
            P(("row", "col"), "week"),
            P(("row", "col"), "week"),
        ),
        check_vma=False,
    )
```

time: 347 us -> 263 us (0.76)
  waiting for transfers between devices: 263 us -> 128 us
  starting transfers between devices: 4.35 us -> 60.7 us
  blocking collectives: 18.7 us -> 0 us
  Pallas kernels: 0 us -> 14.5 us
  matrix products: 34 us -> 21.4 us
  local copies, waits for them, and re-layouts: 5.19 us -> 10.9 us
  other arithmetic: 7.36 us -> 12.7 us
    all_gather x4 -> x3, waiting for transfers between devices: 208 us -> 35.9 us  [body(): lax.all_gather(held[lag], ('row', 'col'), axis=1, tiled=True)]
    ppermute x2 -> x45, starting transfers between devices: 4.01 us -> 60.6 us  [moved(): return lax.ppermute(block, AXES, route)]
    ppermute x2 -> x45, waiting for transfers between devices: 53.3 us -> 90.6 us  [moved(): return lax.ppermute(block, AXES, route)]
    all_to_all x1 -> x0, blocking collectives: 18.7 us -> none  [sent_and_summed(): lax.all_to_all(blocks, axis, split_axis=0, concat_axis=0, tiled=True)]
    pallas_call x0 -> x4, Pallas kernels: none -> 14.5 us  [the longest x1 7.95 us: coupling_and_parts(): pl.pallas_call(kernel, in_specs=[VMEM] * len(operands), out_specs=[VMEM]...]
    dot_general x2 -> x0, matrix products: 14.3 us -> none  [contract_last(): lax.dot_general(left, right, (((1,), (1,)), ((), ())), preferred_element_...]
    dot_general x6 -> x3, matrix products: 19.6 us -> 21.4 us  [contract_first(): lax.dot_general(left, right, (((0,), (0,)), ((), ())), preferred_element_...]
  transfers between devices with their start and end apart: 6 -> 48, of which waited for: 4 -> 18; matrix products, arithmetic and copies ran while one was open for 8% -> 14% of each run, Pallas kernels for 0% -> 5%
where the time goes in v1:
time: 263 us
  waiting for transfers between devices  128 us (49%)
  starting transfers between devices  60.7 us (23%)
  matrix products  21.4 us (8%)
  Pallas kernels  14.5 us (6%)
  between operations  14.3 us (5%)
  other arithmetic  12.7 us (5%)
  local copies, waits for them, and re-layouts  10.9 us (4%)
    ppermute x45, waiting for transfers between devices, moved(): return lax.ppermute(block, AXES, route)  90.6 us
    ppermute x45, starting transfers between devices, moved(): return lax.ppermute(block, AXES, route)  60.6 us
    all_gather x3, waiting for transfers between devices, body(): lax.all_gather(held[lag], ('row', 'col'), axis=1, tiled=True)  35.9 us
    dot_general x3, matrix products, contract_first(): lax.dot_general(left, right, (((0,), (0,)), ((), ())), preferred_element_...  21.4 us
    pallas_call x1, Pallas kernels, coupling_and_parts(): pl.pallas_call(kernel, in_specs=[VMEM] * len(operands), out_specs=[VMEM]...  7.95 us
    unnamed x44, local copies, waits for them, and re-layouts  5.85 us
  transfers between devices with their start and end apart: 48, of which 18 were waited for; matrix products, arithmetic and copies ran while one was open for 14% of the time, Pallas kernels for 5%

profile of v1, /device:TPU:2, one launch (start us, length us, event | category | flops | bytes accessed | tf_op | source)
XLA Modules:
  0.0 262.6 jit_solution(12351569125470356237)
XLA Ops:
  8.0 2.5 fusion.12
  12.0 2.0 collective-permute-start.13
  14.0 1.6 select_select_fusion.1
  16.4 4.0 %collective-permute-start.2 = (bf16[2,1024,128]{2,1,0:T(8,128)(2,1)}, bf16[2,1024,128]{2,1,0:T(8,128)(2,1)S(1)}, u32[]{:S(2)}, u32[]{:S(2)}) collective-permute-start(bf16[2,1024,128]{2,1,0:T(8,128)(2,1)} %pad_maximum_fusion.1), channel_id=1, source_target_pairs={{32,96},{33,97},{34,98},{35,99},{36,100},{37,101},{38,102},{39,103... | collective-permute-start | bytes 1572872 | tf_op jit(solution)/shard_map/ppermute | solution.py:25
  20.5 1.8 collective-permute-start.1
  22.3 1.9 collective-permute-start
  24.2 3.7 %collective-permute-start.14 = (bf16[1024,128]{1,0:T(8,128)(2,1)S(1)}, bf16[1024,128]{1,0:T(8,128)(2,1)S(1)}, u32[]{:S(2)}, u32[]{:S(2)}) collective-permute-start(bf16[1024,128]{1,0:T(8,128)(2,1)S(1)} %copy-done.2), channel_id=1, source_target_pairs={{0,16},{1,17},{2,18},{3,19},{4,20},{5,21},{6,22},{7,23},{8,24},{9,... | collective-permute-start | bytes 786440 | tf_op jit(solution)/shard_map/ppermute | solution.py:25
  28.9 7.0 %collective-permute-done.14.refs_14_ = bf16[1024,128]{1,0:T(8,128)(2,1)S(1)} collective-permute-done((bf16[1024,128]{1,0:T(8,128)(2,1)S(1)}, bf16[1024,128]{1,0:T(8,128)(2,1)S(1)}, u32[]{:S(2)}, u32[]{:S(2)}) %collective-permute-start.14) | collective-permute-done | bytes 262176 | tf_op jit(solution)/shard_map/ppermute | solution.py:25
  35.9 5.5 %collective-permute-done.15.refs_15_ = bf16[1024,128]{1,0:T(8,128)(2,1)S(1)} collective-permute-done((bf16[1024,128]{1,0:T(8,128)(2,1)S(1)}, bf16[1024,128]{1,0:T(8,128)(2,1)S(1)}, u32[]{:S(2)}, u32[]{:S(2)}) %collective-permute-start.15) | collective-permute-done | bytes 262176 | tf_op jit(solution)/shard_map/ppermute | solution.py:25
  43.1 1.6 collective-permute-start.3
  44.8 3.0 %collective-permute-start.4 = (bf16[2,1024,128]{2,1,0:T(8,128)(2,1)S(1)}, bf16[2,1024,128]{2,1,0:T(8,128)(2,1)S(1)}, u32[]{:S(2)}, u32[]{:S(2)}) collective-permute-start(bf16[2,1024,128]{2,1,0:T(8,128)(2,1)S(1)} %pad_maximum_fusion.2.refs_0_), channel_id=1, source_target_pairs={{0,4},{1,5},{2,6},{3,7},{4,0},{5,1},{6,2},{7,3},{8,12},{9,13},{10,... | collective-permute-start | bytes 1572872 | tf_op jit(solution)/shard_map/ppermute | solution.py:25
  47.7 1.9 collective-permute-start.6
  49.7 2.0 collective-permute-start.7
  51.6 2.3 collective-permute-start.8
  54.0 10.3 %collective-permute-done.3.refs_1_ = bf16[2,1024,128]{2,1,0:T(8,128)(2,1)S(1)} collective-permute-done((bf16[2,1024,128]{2,1,0:T(8,128)(2,1)S(1)}, bf16[2,1024,128]{2,1,0:T(8,128)(2,1)S(1)}, u32[]{:S(2)}, u32[]{:S(2)}) %collective-permute-start.3) | collective-permute-done | bytes 524320 | tf_op jit(solution)/shard_map/ppermute | solution.py:25
  64.3 2.3 collective-permute-start.5
  66.6 14.6 %collective-permute-done.4.refs_2_ = bf16[2,1024,128]{2,1,0:T(8,128)(2,1)S(1)} collective-permute-done((bf16[2,1024,128]{2,1,0:T(8,128)(2,1)S(1)}, bf16[2,1024,128]{2,1,0:T(8,128)(2,1)S(1)}, u32[]{:S(2)}, u32[]{:S(2)}) %collective-permute-start.4) | collective-permute-done | bytes 524320 | tf_op jit(solution)/shard_map/ppermute | solution.py:25
  81.7 8.8 %collective-permute-done.7.refs_6_ = bf16[2,1024,128]{2,1,0:T(8,128)(2,1)S(1)} collective-permute-done((bf16[2,1024,128]{2,1,0:T(8,128)(2,1)S(1)}, bf16[2,1024,128]{2,1,0:T(8,128)(2,1)S(1)}, u32[]{:S(2)}, u32[]{:S(2)}) %collective-permute-start.7) | collective-permute-done | bytes 524320 | tf_op jit(solution)/shard_map/ppermute | solution.py:25
  91.1 1.7 collective-permute-done.11.refs_10_
  94.4 8.0 %coupling_and_parts.1 = (f32[128,1024]{1,0:T(8,128)S(1)}, bf16[128,1024]{1,0:T(8,128)(2,1)S(1)}, bf16[128,1024]{1,0:T(8,128)(2,1)S(1)}, bf16[128,1024]{1,0:T(8,128)(2,1)S(1)}) custom-call(bf16[2,1024,128]{2,1,0:T(8,128)(2,1)S(1)} %pad_maximum_fusion.2.refs_0_, bf16[2,1024,128]{2,1,0:T(8,128)(2,1)S(1)} %collective-permute-done.3.refs_1_, ...), custom_call_target="tpu_custom_call" | custom-call | tf_op jit(solution)/shard_map/coupling_and_parts/pallas_call | solution.py:106
  102.4 1.7 collective-permute-start.21
  104.1 1.5 collective-permute-start.20
  105.6 14.0 %collective-permute-done.22 = bf16[128,1024]{1,0:T(8,128)(2,1)S(1)} collective-permute-done((bf16[128,1024]{1,0:T(8,128)(2,1)S(1)}, bf16[128,1024]{1,0:T(8,128)(2,1)S(1)}, u32[]{:S(2)}, u32[]{:S(2)}) %collective-permute-start.22) | collective-permute-done | bytes 262176 | tf_op jit(solution)/shard_map/ppermute | solution.py:25
  121.5 2.2 collective-permute-start.24
  125.1 2.6 %collective-permute-start.28 = (bf16[128,1024]{1,0:T(8,128)(2,1)S(1)}, bf16[128,1024]{1,0:T(8,128)(2,1)S(1)}, u32[]{:S(2)}, u32[]{:S(2)}) collective-permute-start(bf16[128,1024]{1,0:T(8,128)(2,1)S(1)} %add_convert_fusion.refs_1_.refs_5_), channel_id=1, source_target_pairs={{0,24},{1,25},{2,26},{3,27},{4,28},{5,29},{6,30},{7,31},{8,0},{9,1... | collective-permute-start | bytes 786440 | tf_op jit(solution)/shard_map/ppermute | solution.py:25
  127.7 7.6 %collective-permute-done.23.refs_2_ = bf16[128,1024]{1,0:T(8,128)(2,1)S(1)} collective-permute-done((bf16[128,1024]{1,0:T(8,128)(2,1)S(1)}, bf16[128,1024]{1,0:T(8,128)(2,1)S(1)}, u32[]{:S(2)}, u32[]{:S(2)}) %collective-permute-start.23) | collective-permute-done | bytes 262176 | tf_op jit(solution)/shard_map/ppermute | solution.py:25
  135.4 2.5 collective-permute-done.26.refs_6_
  138.3 1.7 collective-permute-done.28.refs_8_
  141.3 4.7 %collective-permute-done.25.refs_4_ = bf16[128,1024]{1,0:T(8,128)(2,1)S(1)} collective-permute-done((bf16[128,1024]{1,0:T(8,128)(2,1)S(1)}, bf16[128,1024]{1,0:T(8,128)(2,1)S(1)}, u32[]{:S(2)}, u32[]{:S(2)}) %collective-permute-start.25) | collective-permute-done | bytes 262176 | tf_op jit(solution)/shard_map/ppermute | solution.py:25
  146.0 2.5 gram_terms.1
  149.3 6.4 %collective-permute-start.40 = (bf16[512,256]{1,0:T(8,128)(2,1)S(1)}, bf16[512,256]{1,0:T(8,128)(2,1)S(1)}, u32[]{:S(2)}, u32[]{:S(2)}) collective-permute-start(bf16[512,256]{1,0:T(8,128)(2,1)S(1)} %get-tuple-element.27), channel_id=1, source_target_pairs={{0,64},{1,65},{2,66},{3,67},{4,68},{5,69},{6,70},{7,71},{8,72},{9,... | collective-permute-start | bytes 786440 | tf_op jit(solution)/shard_map/ppermute | solution.py:25
  155.7 9.9 %fusion.19 = (bf16[384,4096]{1,0:T(8,128)(2,1)S(1)}, f32[384,4096]{1,0:T(8,128)}) fusion(bf16[1024,384]{1,0:T(8,128)(2,1)} %copy-done.5, bf16[1024,4096]{1,0:T(8,128)(2,1)} %all-gather.6.cloned.1.call-done), kind=kOutput, calls=%fused_computation.47 | convolution fusion | flops 3222798336 | bytes 18612224 | tf_op jit(solution)/shard_map/dot_general | solution.py:37
  165.6 1.5 fusion.17
  167.2 1.5 collective-permute-start.35
  168.7 5.9 %fusion.20 = f32[256,4096]{1,0:T(8,128)S(1)} fusion(bf16[1024,256]{1,0:T(8,128)(2,1)S(1)} %slice-done, bf16[1024,4096]{1,0:T(8,128)(2,1)} %all-gather.8.cloned.1.call-done), kind=kOutput, calls=%fused_computation.48 | convolution fusion | flops 2147483648 | bytes 13107200 | tf_op jit(solution)/shard_map/dot_general | solution.py:37
  174.6 2.1 copy-done.3
  177.9 3.3 %collective-permute-start.34 = (bf16[128,4096]{1,0:T(8,128)(2,1)}, bf16[128,4096]{1,0:T(8,128)(2,1)}, u32[]{:S(2)}, u32[]{:S(2)}) collective-permute-start(bf16[128,4096]{1,0:T(8,128)(2,1)} %slice.138), channel_id=1, source_target_pairs={{32,0},{33,1},{34,2},{35,3},{36,4},{37,5},{38,6},{39,7},{40,8},{41... | collective-permute-start | bytes 3145736 | tf_op jit(solution)/shard_map/ppermute | solution.py:25
  183.4 2.0 week_sum.1
  188.1 1.7 slice_bitcast_fusion
  189.8 35.9 %all-gather.4.cloned.1.call-done = bf16[1024,4096]{1,0:T(8,128)(2,1)} async-done(((bf16[1024,128]{1,0:T(8,128)(2,1)}), bf16[1024,4096]{1,0:T(8,128)(2,1)}) %all-gather.4.cloned.1.call-update) | async-done | bytes 8388624 | tf_op jit(solution)/shard_map/all_gather | solution.py:251
  225.8 5.6 %fusion.16 = (bf16[128,4096]{1,0:T(8,128)(2,1)S(1)}, f32[128,4096]{1,0:T(8,128)S(1)}) fusion(f32[128]{0:T(128)S(1)} %bitcast.77, s32[128]{0:T(128)S(1)} %iota_add_fusion, bf16[128,4096]{1,0:T(8,128)(2,1)S(1)} %collective-permute-done.35, bf16[128,4096]{1,0:T(8,128)(2,1)} %collective-permute-done.34, bf16[1024,128]{1,0:T(8,128)(2,1)S(1)} %copy-done.6, ...), kind=kOutput, calls=%fused_computation.44 | convolution fusion | flops 1077936128 | bytes 13894656 | tf_op jit(solution)/shard_map/dot_general | solution.py:37
  231.4 2.5 collective-permute-start.38
  233.9 2.2 collective-permute-start.37
  236.1 4.7 %collective-permute-done.33 = bf16[128,4096]{1,0:T(8,128)(2,1)} collective-permute-done((bf16[128,4096]{1,0:T(8,128)(2,1)}, bf16[128,4096]{1,0:T(8,128)(2,1)}, u32[]{:S(2)}, u32[]{:S(2)}) %collective-permute-start.33) | collective-permute-done | bytes 1048608 | tf_op jit(solution)/shard_map/ppermute | solution.py:25
  240.8 2.5 collective-permute-start.36
  244.8 3.1 %maximum_bitcast_fusion = f32[1,3,128,4096]{3,2,1,0:T(8,128)} fusion(f32[1,128,4096]{2,1,0:T(8,128)S(1)} %slice_bitcast_fusion, f32[1,128,4096]{2,1,0:T(8,128)S(1)} %fusion, f32[1,128,4096]{2,1,0:T(8,128)S(1)} %bitcast.70), kind=kLoop, calls=%fused_computation | loop fusion | flops 3145728 | bytes 12582912 | tf_op jit(solution)/shard_map/broadcast_in_dim | solution.py:295
  249.0 4.3 %collective-permute-done.44.refs_3_ = bf16[128,256]{1,0:T(8,128)(2,1)S(1)} collective-permute-done((bf16[128,256]{1,0:T(8,128)(2,1)S(1)}, bf16[128,256]{1,0:T(8,128)(2,1)S(1)}, u32[]{:S(2)}, u32[]{:S(2)}) %collective-permute-start.44) | collective-permute-done | bytes 65568 | tf_op jit(solution)/shard_map/ppermute | solution.py:25
  254.0 2.0 place_schur.1
  (122 shorter events, 23.5 us)
Async XLA Ops:
  7.2 148.5 %all-gather.6.cloned.1.call-start = ((), (), s32[]{:S(2)}) async-start(), calls=%async_computation.1 | async-start | bytes 8650752 | tf_op jit(solution)/shard_map/all_gather | solution.py:251
  10.5 158.2 %all-gather.8.cloned.1.call-start = ((), (), s32[]{:S(2)}) async-start(), calls=%async_computation.2 | async-start | bytes 8650752 | tf_op jit(solution)/shard_map/all_gather | solution.py:251
  11.3 214.5 %all-gather.4.cloned.1.call-start = ((), (), s32[]{:S(2)}) async-start(), calls=%async_computation | async-start | bytes 8650752 | tf_op jit(solution)/shard_map/all_gather | solution.py:251
  12.0 15.9 %collective-permute-start.13 = (bf16[1024,128]{1,0:T(8,128)(2,1)}, bf16[1024,128]{1,0:T(8,128)(2,1)S(1)}, u32[]{:S(2)}, u32[]{:S(2)}) collective-permute-start(bf16[1024,128]{1,0:T(8,128)(2,1)} %refs_12_.1), channel_id=1, source_target_pairs={{0,8},{1,9},{2,10},{3,11},{4,12},{5,13},{6,14},{7,15},{8,16},{9,17... | collective-permute-start | bytes 786440 | tf_op jit(solution)/shard_map/ppermute | solution.py:25
  16.4 25.0 %collective-permute-start.2 = (bf16[2,1024,128]{2,1,0:T(8,128)(2,1)}, bf16[2,1024,128]{2,1,0:T(8,128)(2,1)S(1)}, u32[]{:S(2)}, u32[]{:S(2)}) collective-permute-start(bf16[2,1024,128]{2,1,0:T(8,128)(2,1)} %pad_maximum_fusion.1), channel_id=1, source_target_pairs={{32,96},{33,97},{34,98},{35,99},{36,100},{37,101},{38,102},{39,103... | collective-permute-start | bytes 1572872 | tf_op jit(solution)/shard_map/ppermute | solution.py:25
  20.5 21.4 %collective-permute-start.1 = (bf16[2,1024,128]{2,1,0:T(8,128)(2,1)}, bf16[2,1024,128]{2,1,0:T(8,128)(2,1)S(1)}, u32[]{:S(2)}, u32[]{:S(2)}) collective-permute-start(bf16[2,1024,128]{2,1,0:T(8,128)(2,1)} %pad_maximum_fusion.1), channel_id=1, source_target_pairs={{32,64},{33,65},{34,66},{35,67},{36,68},{37,69},{38,70},{39,71},{4... | collective-permute-start | bytes 1572872 | tf_op jit(solution)/shard_map/ppermute | solution.py:25
  22.3 20.6 %collective-permute-start = (bf16[2,1024,128]{2,1,0:T(8,128)(2,1)}, bf16[2,1024,128]{2,1,0:T(8,128)(2,1)S(1)}, u32[]{:S(2)}, u32[]{:S(2)}) collective-permute-start(bf16[2,1024,128]{2,1,0:T(8,128)(2,1)} %pad_maximum_fusion.1), channel_id=1, source_target_pairs={{32,0},{33,1},{34,2},{35,3},{36,4},{37,5},{38,6},{39,7},{40,8},{41... | collective-permute-start | bytes 1572872 | tf_op jit(solution)/shard_map/ppermute | solution.py:25
  24.2 11.6 %collective-permute-start.14 = (bf16[1024,128]{1,0:T(8,128)(2,1)S(1)}, bf16[1024,128]{1,0:T(8,128)(2,1)S(1)}, u32[]{:S(2)}, u32[]{:S(2)}) collective-permute-start(bf16[1024,128]{1,0:T(8,128)(2,1)S(1)} %copy-done.2), channel_id=1, source_target_pairs={{0,16},{1,17},{2,18},{3,19},{4,20},{5,21},{6,22},{7,23},{8,24},{9,... | collective-permute-start | bytes 786440 | tf_op jit(solution)/shard_map/ppermute | solution.py:25
  27.9 13.5 %collective-permute-start.15 = (bf16[1024,128]{1,0:T(8,128)(2,1)S(1)}, bf16[1024,128]{1,0:T(8,128)(2,1)S(1)}, u32[]{:S(2)}, u32[]{:S(2)}) collective-permute-start(bf16[1024,128]{1,0:T(8,128)(2,1)S(1)} %copy-done.2), channel_id=1, source_target_pairs={{0,24},{1,25},{2,26},{3,27},{4,28},{5,29},{6,30},{7,31},{8,0},{9,1... | collective-permute-start | bytes 786440 | tf_op jit(solution)/shard_map/ppermute | solution.py:25
  35.9 8.9 %collective-permute-start.16 = (bf16[1024,128]{1,0:T(8,128)(2,1)S(1)}, bf16[1024,128]{1,0:T(8,128)(2,1)S(1)}, u32[]{:S(2)}, u32[]{:S(2)}) collective-permute-start(bf16[1024,128]{1,0:T(8,128)(2,1)S(1)} %copy-done.2), channel_id=1, source_target_pairs={{0,1},{1,0},{2,3},{3,2},{4,5},{5,4},{6,7},{7,6},{8,9},{9,8},{10,11... | collective-permute-start | bytes 786440 | tf_op jit(solution)/shard_map/ppermute | solution.py:25
  41.4 6.3 %collective-permute-start.17 = (bf16[1024,128]{1,0:T(8,128)(2,1)S(1)}, bf16[1024,128]{1,0:T(8,128)(2,1)S(1)}, u32[]{:S(2)}, u32[]{:S(2)}) collective-permute-start(bf16[1024,128]{1,0:T(8,128)(2,1)S(1)} %collective-permute-done.13.refs_13_), channel_id=1, source_target_pairs={{0,1},{1,0},{2,3},{3,2},{4,5},{5,4},{6,7},{7,6},{8,9},{9,8},{10,11... | collective-permute-start | bytes 786440 | tf_op jit(solution)/shard_map/ppermute | solution.py:25
  41.4 8.3 %collective-permute-start.18 = (bf16[1024,128]{1,0:T(8,128)(2,1)S(1)}, bf16[1024,128]{1,0:T(8,128)(2,1)S(1)}, u32[]{:S(2)}, u32[]{:S(2)}) collective-permute-start(bf16[1024,128]{1,0:T(8,128)(2,1)S(1)} %collective-permute-done.14.refs_14_), channel_id=1, source_target_pairs={{0,1},{1,0},{2,3},{3,2},{4,5},{5,4},{6,7},{7,6},{8,9},{9,8},{10,11... | collective-permute-start | bytes 786440 | tf_op jit(solution)/shard_map/ppermute | solution.py:25
  41.9 9.7 %collective-permute-start.19 = (bf16[1024,128]{1,0:T(8,128)(2,1)S(1)}, bf16[1024,128]{1,0:T(8,128)(2,1)S(1)}, u32[]{:S(2)}, u32[]{:S(2)}) collective-permute-start(bf16[1024,128]{1,0:T(8,128)(2,1)S(1)} %collective-permute-done.15.refs_15_), channel_id=1, source_target_pairs={{0,1},{1,0},{2,3},{3,2},{4,5},{5,4},{6,7},{7,6},{8,9},{9,8},{10,11... | collective-permute-start | bytes 786440 | tf_op jit(solution)/shard_map/ppermute | solution.py:25
  43.1 21.2 %collective-permute-start.3 = (bf16[2,1024,128]{2,1,0:T(8,128)(2,1)S(1)}, bf16[2,1024,128]{2,1,0:T(8,128)(2,1)S(1)}, u32[]{:S(2)}, u32[]{:S(2)}) collective-permute-start(bf16[2,1024,128]{2,1,0:T(8,128)(2,1)S(1)} %pad_maximum_fusion.2.refs_0_), channel_id=1, source_target_pairs={{0,2},{1,3},{2,4},{3,5},{4,6},{5,7},{6,0},{7,1},{8,10},{9,11},{10,... | collective-permute-start | bytes 1572872 | tf_op jit(solution)/shard_map/ppermute | solution.py:25
  44.8 36.5 %collective-permute-start.4 = (bf16[2,1024,128]{2,1,0:T(8,128)(2,1)S(1)}, bf16[2,1024,128]{2,1,0:T(8,128)(2,1)S(1)}, u32[]{:S(2)}, u32[]{:S(2)}) collective-permute-start(bf16[2,1024,128]{2,1,0:T(8,128)(2,1)S(1)} %pad_maximum_fusion.2.refs_0_), channel_id=1, source_target_pairs={{0,4},{1,5},{2,6},{3,7},{4,0},{5,1},{6,2},{7,3},{8,12},{9,13},{10,... | collective-permute-start | bytes 1572872 | tf_op jit(solution)/shard_map/ppermute | solution.py:25
  47.7 33.5 %collective-permute-start.6 = (bf16[2,1024,128]{2,1,0:T(8,128)(2,1)S(1)}, bf16[2,1024,128]{2,1,0:T(8,128)(2,1)S(1)}, u32[]{:S(2)}, u32[]{:S(2)}) collective-permute-start(bf16[2,1024,128]{2,1,0:T(8,128)(2,1)S(1)} %pad_maximum_fusion.3.refs_4_), channel_id=1, source_target_pairs={{0,8},{1,9},{2,10},{3,11},{4,12},{5,13},{6,14},{7,15},{8,16},{9,17... | collective-permute-start | bytes 1572872 | tf_op jit(solution)/shard_map/ppermute | solution.py:25
  49.7 40.9 %collective-permute-start.7 = (bf16[2,1024,128]{2,1,0:T(8,128)(2,1)S(1)}, bf16[2,1024,128]{2,1,0:T(8,128)(2,1)S(1)}, u32[]{:S(2)}, u32[]{:S(2)}) collective-permute-start(bf16[2,1024,128]{2,1,0:T(8,128)(2,1)S(1)} %pad_maximum_fusion.3.refs_4_), channel_id=1, source_target_pairs={{0,16},{1,17},{2,18},{3,19},{4,20},{5,21},{6,22},{7,23},{8,24},{9,... | collective-permute-start | bytes 1572872 | tf_op jit(solution)/shard_map/ppermute | solution.py:25
  51.6 38.9 %collective-permute-start.8 = (bf16[2,1024,128]{2,1,0:T(8,128)(2,1)S(1)}, bf16[2,1024,128]{2,1,0:T(8,128)(2,1)S(1)}, u32[]{:S(2)}, u32[]{:S(2)}) collective-permute-start(bf16[2,1024,128]{2,1,0:T(8,128)(2,1)S(1)} %pad_maximum_fusion.3.refs_4_), channel_id=1, source_target_pairs={{0,24},{1,25},{2,26},{3,27},{4,28},{5,29},{6,30},{7,31},{8,0},{9,1... | collective-permute-start | bytes 1572872 | tf_op jit(solution)/shard_map/ppermute | solution.py:25
  64.3 26.8 %collective-permute-start.5 = (bf16[2,1024,128]{2,1,0:T(8,128)(2,1)S(1)}, bf16[2,1024,128]{2,1,0:T(8,128)(2,1)S(1)}, u32[]{:S(2)}, u32[]{:S(2)}) collective-permute-start(bf16[2,1024,128]{2,1,0:T(8,128)(2,1)S(1)} %pad_maximum_fusion.2.refs_0_), channel_id=1, source_target_pairs={{0,6},{1,7},{2,0},{3,1},{4,2},{5,3},{6,4},{7,5},{8,14},{9,15},{10,... | collective-permute-start | bytes 1572872 | tf_op jit(solution)/shard_map/ppermute | solution.py:25
  81.2 9.9 %collective-permute-start.9 = (bf16[2,1024,128]{2,1,0:T(8,128)(2,1)S(1)}, bf16[2,1024,128]{2,1,0:T(8,128)(2,1)S(1)}, u32[]{:S(2)}, u32[]{:S(2)}) collective-permute-start(bf16[2,1024,128]{2,1,0:T(8,128)(2,1)S(1)} %pad_maximum_fusion.3.refs_4_), channel_id=1, source_target_pairs={{0,1},{1,0},{2,3},{3,2},{4,5},{5,4},{6,7},{7,6},{8,9},{9,8},{10,11... | collective-permute-start | bytes 1572872 | tf_op jit(solution)/shard_map/ppermute | solution.py:25
  81.2 9.9 %collective-permute-start.10 = (bf16[2,1024,128]{2,1,0:T(8,128)(2,1)S(1)}, bf16[2,1024,128]{2,1,0:T(8,128)(2,1)S(1)}, u32[]{:S(2)}, u32[]{:S(2)}) collective-permute-start(bf16[2,1024,128]{2,1,0:T(8,128)(2,1)S(1)} %collective-permute-done.6.refs_5_), channel_id=1, source_target_pairs={{0,1},{1,0},{2,3},{3,2},{4,5},{5,4},{6,7},{7,6},{8,9},{9,8},{10,11... | collective-permute-start | bytes 1572872 | tf_op jit(solution)/shard_map/ppermute | solution.py:25
  90.6 2.2 collective-permute-start.11
  90.6 2.9 %collective-permute-start.12 = (bf16[2,1024,128]{2,1,0:T(8,128)(2,1)S(1)}, bf16[2,1024,128]{2,1,0:T(8,128)(2,1)S(1)}, u32[]{:S(2)}, u32[]{:S(2)}) collective-permute-start(bf16[2,1024,128]{2,1,0:T(8,128)(2,1)S(1)} %collective-permute-done.8.refs_7_), channel_id=1, source_target_pairs={{0,1},{1,0},{2,3},{3,2},{4,5},{5,4},{6,7},{7,6},{8,9},{9,8},{10,11... | collective-permute-start | bytes 1572872 | tf_op jit(solution)/shard_map/ppermute | solution.py:25
  102.3 17.3 %collective-permute-start.22 = (bf16[128,1024]{1,0:T(8,128)(2,1)S(1)}, bf16[128,1024]{1,0:T(8,128)(2,1)S(1)}, u32[]{:S(2)}, u32[]{:S(2)}) collective-permute-start(bf16[128,1024]{1,0:T(8,128)(2,1)S(1)} %get-tuple-element.21), channel_id=1, source_target_pairs={{0,2},{1,3},{2,4},{3,5},{4,6},{5,7},{6,0},{7,1},{8,10},{9,11},{10,... | collective-permute-start | bytes 786440 | tf_op jit(solution)/shard_map/ppermute | solution.py:25
  102.4 17.2 %collective-permute-start.21 = (bf16[128,1024]{1,0:T(8,128)(2,1)S(1)}, bf16[128,1024]{1,0:T(8,128)(2,1)S(1)}, u32[]{:S(2)}, u32[]{:S(2)}) collective-permute-start(bf16[128,1024]{1,0:T(8,128)(2,1)S(1)} %get-tuple-element.20), channel_id=1, source_target_pairs={{0,4},{1,5},{2,6},{3,7},{4,0},{5,1},{6,2},{7,3},{8,12},{9,13},{10,... | collective-permute-start | bytes 786440 | tf_op jit(solution)/shard_map/ppermute | solution.py:25
  104.1 16.9 %collective-permute-start.20 = (bf16[128,1024]{1,0:T(8,128)(2,1)S(1)}, bf16[128,1024]{1,0:T(8,128)(2,1)S(1)}, u32[]{:S(2)}, u32[]{:S(2)}) collective-permute-start(bf16[128,1024]{1,0:T(8,128)(2,1)S(1)} %get-tuple-element.19), channel_id=1, source_target_pairs={{0,6},{1,7},{2,0},{3,1},{4,2},{5,3},{6,4},{7,5},{8,14},{9,15},{10,... | collective-permute-start | bytes 786440 | tf_op jit(solution)/shard_map/ppermute | solution.py:25
  121.2 14.2 %collective-permute-start.23 = (bf16[128,1024]{1,0:T(8,128)(2,1)S(1)}, bf16[128,1024]{1,0:T(8,128)(2,1)S(1)}, u32[]{:S(2)}, u32[]{:S(2)}) collective-permute-start(bf16[128,1024]{1,0:T(8,128)(2,1)S(1)} %add_convert_fusion.refs_1_.refs_5_), channel_id=1, source_target_pairs={{0,2},{1,3},{2,4},{3,5},{4,6},{5,7},{6,0},{7,1},{8,10},{9,11},{10,... | collective-permute-start | bytes 786440 | tf_op jit(solution)/shard_map/ppermute | solution.py:25
  121.5 13.9 %collective-permute-start.24 = (bf16[128,1024]{1,0:T(8,128)(2,1)S(1)}, bf16[128,1024]{1,0:T(8,128)(2,1)S(1)}, u32[]{:S(2)}, u32[]{:S(2)}) collective-permute-start(bf16[128,1024]{1,0:T(8,128)(2,1)S(1)} %add_convert_fusion.refs_1_.refs_5_), channel_id=1, source_target_pairs={{0,4},{1,5},{2,6},{3,7},{4,0},{5,1},{6,2},{7,3},{8,12},{9,13},{10,... | collective-permute-start | bytes 786440 | tf_op jit(solution)/shard_map/ppermute | solution.py:25
  123.6 14.2 %collective-permute-start.26 = (bf16[128,1024]{1,0:T(8,128)(2,1)S(1)}, bf16[128,1024]{1,0:T(8,128)(2,1)S(1)}, u32[]{:S(2)}, u32[]{:S(2)}) collective-permute-start(bf16[128,1024]{1,0:T(8,128)(2,1)S(1)} %add_convert_fusion.refs_1_.refs_5_), channel_id=1, source_target_pairs={{0,8},{1,9},{2,10},{3,11},{4,12},{5,13},{6,14},{7,15},{8,16},{9,17... | collective-permute-start | bytes 786440 | tf_op jit(solution)/shard_map/ppermute | solution.py:25
  123.6 14.2 %collective-permute-start.27 = (bf16[128,1024]{1,0:T(8,128)(2,1)S(1)}, bf16[128,1024]{1,0:T(8,128)(2,1)S(1)}, u32[]{:S(2)}, u32[]{:S(2)}) collective-permute-start(bf16[128,1024]{1,0:T(8,128)(2,1)S(1)} %add_convert_fusion.refs_1_.refs_5_), channel_id=1, source_target_pairs={{0,16},{1,17},{2,18},{3,19},{4,20},{5,21},{6,22},{7,23},{8,24},{9,... | collective-permute-start | bytes 786440 | tf_op jit(solution)/shard_map/ppermute | solution.py:25
  125.1 14.9 %collective-permute-start.28 = (bf16[128,1024]{1,0:T(8,128)(2,1)S(1)}, bf16[128,1024]{1,0:T(8,128)(2,1)S(1)}, u32[]{:S(2)}, u32[]{:S(2)}) collective-permute-start(bf16[128,1024]{1,0:T(8,128)(2,1)S(1)} %add_convert_fusion.refs_1_.refs_5_), channel_id=1, source_target_pairs={{0,24},{1,25},{2,26},{3,27},{4,28},{5,29},{6,30},{7,31},{8,0},{9,1... | collective-permute-start | bytes 786440 | tf_op jit(solution)/shard_map/ppermute | solution.py:25
  135.3 10.6 %collective-permute-start.25 = (bf16[128,1024]{1,0:T(8,128)(2,1)S(1)}, bf16[128,1024]{1,0:T(8,128)(2,1)S(1)}, u32[]{:S(2)}, u32[]{:S(2)}) collective-permute-start(bf16[128,1024]{1,0:T(8,128)(2,1)S(1)} %add_convert_fusion.refs_1_.refs_5_), channel_id=1, source_target_pairs={{0,6},{1,7},{2,0},{3,1},{4,2},{5,3},{6,4},{7,5},{8,14},{9,15},{10,... | collective-permute-start | bytes 786440 | tf_op jit(solution)/shard_map/ppermute | solution.py:25
  135.3 10.6 %collective-permute-start.29 = (bf16[128,1024]{1,0:T(8,128)(2,1)S(1)}, bf16[128,1024]{1,0:T(8,128)(2,1)S(1)}, u32[]{:S(2)}, u32[]{:S(2)}) collective-permute-start(bf16[128,1024]{1,0:T(8,128)(2,1)S(1)} %add_convert_fusion.refs_1_.refs_5_), channel_id=1, source_target_pairs={{0,1},{1,0},{2,3},{3,2},{4,5},{5,4},{6,7},{7,6},{8,9},{9,8},{10,11... | collective-permute-start | bytes 786440 | tf_op jit(solution)/shard_map/ppermute | solution.py:25
  137.8 8.2 %collective-permute-start.30 = (bf16[128,1024]{1,0:T(8,128)(2,1)S(1)}, bf16[128,1024]{1,0:T(8,128)(2,1)S(1)}, u32[]{:S(2)}, u32[]{:S(2)}) collective-permute-start(bf16[128,1024]{1,0:T(8,128)(2,1)S(1)} %collective-permute-done.26.refs_6_), channel_id=1, source_target_pairs={{0,1},{1,0},{2,3},{3,2},{4,5},{5,4},{6,7},{7,6},{8,9},{9,8},{10,11... | collective-permute-start | bytes 786440 | tf_op jit(solution)/shard_map/ppermute | solution.py:25
  137.8 8.1 %collective-permute-start.31 = (bf16[128,1024]{1,0:T(8,128)(2,1)S(1)}, bf16[128,1024]{1,0:T(8,128)(2,1)S(1)}, u32[]{:S(2)}, u32[]{:S(2)}) collective-permute-start(bf16[128,1024]{1,0:T(8,128)(2,1)S(1)} %collective-permute-done.27.refs_7_), channel_id=1, source_target_pairs={{0,1},{1,0},{2,3},{3,2},{4,5},{5,4},{6,7},{7,6},{8,9},{9,8},{10,11... | collective-permute-start | bytes 786440 | tf_op jit(solution)/shard_map/ppermute | solution.py:25
  140.0 6.0 %collective-permute-start.32 = (bf16[128,1024]{1,0:T(8,128)(2,1)S(1)}, bf16[128,1024]{1,0:T(8,128)(2,1)S(1)}, u32[]{:S(2)}, u32[]{:S(2)}) collective-permute-start(bf16[128,1024]{1,0:T(8,128)(2,1)S(1)} %collective-permute-done.28.refs_8_), channel_id=1, source_target_pairs={{0,1},{1,0},{2,3},{3,2},{4,5},{5,4},{6,7},{7,6},{8,9},{9,8},{10,11... | collective-permute-start | bytes 786440 | tf_op jit(solution)/shard_map/ppermute | solution.py:25
  149.3 32.6 %collective-permute-start.39 = (bf16[512,256]{1,0:T(8,128)(2,1)}, bf16[512,256]{1,0:T(8,128)(2,1)S(1)}, u32[]{:S(2)}, u32[]{:S(2)}) collective-permute-start(bf16[512,256]{1,0:T(8,128)(2,1)} %get-tuple-element.26), channel_id=1, source_target_pairs={{0,32},{1,33},{2,34},{3,35},{4,36},{5,37},{6,38},{7,39},{8,40},{9,... | collective-permute-start | bytes 786440 | tf_op jit(solution)/shard_map/ppermute | solution.py:25
  149.3 32.6 %collective-permute-start.40 = (bf16[512,256]{1,0:T(8,128)(2,1)S(1)}, bf16[512,256]{1,0:T(8,128)(2,1)S(1)}, u32[]{:S(2)}, u32[]{:S(2)}) collective-permute-start(bf16[512,256]{1,0:T(8,128)(2,1)S(1)} %get-tuple-element.27), channel_id=1, source_target_pairs={{0,64},{1,65},{2,66},{3,67},{4,68},{5,69},{6,70},{7,71},{8,72},{9,... | collective-permute-start | bytes 786440 | tf_op jit(solution)/shard_map/ppermute | solution.py:25
  155.7 26.2 %collective-permute-start.41 = (bf16[512,256]{1,0:T(8,128)(2,1)S(1)}, bf16[512,256]{1,0:T(8,128)(2,1)S(1)}, u32[]{:S(2)}, u32[]{:S(2)}) collective-permute-start(bf16[512,256]{1,0:T(8,128)(2,1)S(1)} %get-tuple-element.28), channel_id=1, source_target_pairs={{0,96},{1,97},{2,98},{3,99},{4,100},{5,101},{6,102},{7,103},{8,104... | collective-permute-start | bytes 786440 | tf_op jit(solution)/shard_map/ppermute | solution.py:25
  167.2 58.6 %collective-permute-start.35 = (bf16[128,4096]{1,0:T(8,128)(2,1)}, bf16[128,4096]{1,0:T(8,128)(2,1)S(1)}, u32[]{:S(2)}, u32[]{:S(2)}) collective-permute-start(bf16[128,4096]{1,0:T(8,128)(2,1)} %get-tuple-element.35), channel_id=1, source_target_pairs={{64,0},{65,1},{66,2},{67,3},{68,4},{69,5},{70,6},{71,7},{72,8},{73... | collective-permute-start | bytes 3145736 | tf_op jit(solution)/shard_map/ppermute | solution.py:25
  177.9 47.9 %collective-permute-start.34 = (bf16[128,4096]{1,0:T(8,128)(2,1)}, bf16[128,4096]{1,0:T(8,128)(2,1)}, u32[]{:S(2)}, u32[]{:S(2)}) collective-permute-start(bf16[128,4096]{1,0:T(8,128)(2,1)} %slice.138), channel_id=1, source_target_pairs={{32,0},{33,1},{34,2},{35,3},{36,4},{37,5},{38,6},{39,7},{40,8},{41... | collective-permute-start | bytes 3145736 | tf_op jit(solution)/shard_map/ppermute | solution.py:25
  185.4 63.6 %collective-permute-start.42 = (bf16[128,256]{1,0:T(8,128)(2,1)}, bf16[128,256]{1,0:T(8,128)(2,1)S(1)}, u32[]{:S(2)}, u32[]{:S(2)}) collective-permute-start(bf16[128,256]{1,0:T(8,128)(2,1)} %get-tuple-element.30), channel_id=1, source_target_pairs={{0,6},{1,7},{2,0},{3,1},{4,2},{5,3},{6,4},{7,5},{8,14},{9,15},{10,... | collective-permute-start | bytes 196616 | tf_op jit(solution)/shard_map/ppermute | solution.py:25
  185.4 63.6 %collective-permute-start.43 = (bf16[128,256]{1,0:T(8,128)(2,1)}, bf16[128,256]{1,0:T(8,128)(2,1)S(1)}, u32[]{:S(2)}, u32[]{:S(2)}) collective-permute-start(bf16[128,256]{1,0:T(8,128)(2,1)} %get-tuple-element.31), channel_id=1, source_target_pairs={{0,4},{1,5},{2,6},{3,7},{4,0},{5,1},{6,2},{7,3},{8,12},{9,13},{10,... | collective-permute-start | bytes 196616 | tf_op jit(solution)/shard_map/ppermute | solution.py:25
  186.8 54.0 %collective-permute-start.33 = (bf16[128,4096]{1,0:T(8,128)(2,1)}, bf16[128,4096]{1,0:T(8,128)(2,1)}, u32[]{:S(2)}, u32[]{:S(2)}) collective-permute-start(bf16[128,4096]{1,0:T(8,128)(2,1)} %get-tuple-element.36), channel_id=1, source_target_pairs={{64,32},{65,33},{66,34},{67,35},{68,36},{69,37},{70,38},{71,39},{7... | collective-permute-start | bytes 3145736 | tf_op jit(solution)/shard_map/ppermute | solution.py:25
  231.4 16.5 %collective-permute-start.38 = (bf16[128,1024]{1,0:T(8,128)(2,1)S(1)}, bf16[128,1024]{1,0:T(8,128)(2,1)S(1)}, u32[]{:S(2)}, u32[]{:S(2)}) collective-permute-start(bf16[128,1024]{1,0:T(8,128)(2,1)S(1)} %get-tuple-element.40), channel_id=1, source_target_pairs={{32,0},{33,1},{34,2},{35,3},{36,4},{37,5},{38,6},{39,7},{40,8},{41... | collective-permute-start | bytes 786440 | tf_op jit(solution)/shard_map/ppermute | solution.py:25
  233.9 14.0 %collective-permute-start.37 = (bf16[128,1024]{1,0:T(8,128)(2,1)S(1)}, bf16[128,1024]{1,0:T(8,128)(2,1)S(1)}, u32[]{:S(2)}, u32[]{:S(2)}) collective-permute-start(bf16[128,1024]{1,0:T(8,128)(2,1)S(1)} %get-tuple-element.41), channel_id=1, source_target_pairs={{32,96},{33,97},{34,98},{35,99},{36,100},{37,101},{38,102},{39,103... | collective-permute-start | bytes 786440 | tf_op jit(solution)/shard_map/ppermute | solution.py:25
  240.8 7.3 %collective-permute-start.36 = (bf16[128,1024]{1,0:T(8,128)(2,1)S(1)}, bf16[128,1024]{1,0:T(8,128)(2,1)S(1)}, u32[]{:S(2)}, u32[]{:S(2)}) collective-permute-start(bf16[128,1024]{1,0:T(8,128)(2,1)S(1)} %get-tuple-element.39), channel_id=1, source_target_pairs={{32,64},{33,65},{34,66},{35,67},{36,68},{37,69},{38,70},{39,71},{4... | collective-permute-start | bytes 786440 | tf_op jit(solution)/shard_map/ppermute | solution.py:25
  247.9 5.5 %collective-permute-start.44 = (bf16[128,256]{1,0:T(8,128)(2,1)S(1)}, bf16[128,256]{1,0:T(8,128)(2,1)S(1)}, u32[]{:S(2)}, u32[]{:S(2)}) collective-permute-start(bf16[128,256]{1,0:T(8,128)(2,1)S(1)} %copy-done.21), channel_id=1, source_target_pairs={{0,2},{1,3},{2,4},{3,5},{4,6},{5,7},{6,0},{7,1},{8,10},{9,11},{10,... | collective-permute-start | bytes 196616 | tf_op jit(solution)/shard_map/ppermute | solution.py:25
  (23 other events, 224.9 us)
Sparse Core Ops, SparseCore 0:
  10.6 85.0 all-gather.5
  97.9 65.5 all-gather.7
  165.7 60.0 all-gather.3

commit v2 on v1

--- a/solution.py
+++ b/solution.py
@@ -33,12 +33,6 @@
 f32 = jnp.float32
 
 
-def contract_first(left, right):
-    return lax.dot_general(
-        left, right, (((0,), (0,)), ((), ())), preferred_element_type=jnp.float32
-    )
-
-
 def dot_first(left, right):
     return lax.dot_general(
         left, right, (((0,), (0,)), ((), ())), preferred_element_type=jnp.float32
@@ -83,17 +77,22 @@
 
 
 def coupling_and_parts(lefts, rights, pivots):
-    n_a, obs, slim = rights[0].shape
+    obs, slim = rights[0].shape[1:]
     n_r, n_c, wide = len(lefts), len(rights), pivots[0].shape[0]
     pairs = n_r // 2
+    operands, places = list(pivots), []
+    for piece in [*lefts, *rights]:
+        places.append((len(operands), isinstance(piece, tuple)))
+        operands += piece if isinstance(piece, tuple) else [piece]
+    n_in = len(operands)
 
     def kernel(*refs):
-        la, ra, pv, rest = cut(refs, n_r, n_c, n_c)
-        parts, (l_s, r_s, p_s, sems) = rest[:n_r], rest[n_r:]
-        copies = right_copies(pv, p_s, 0, wide, slim)
-        for a in range(n_a):
-            copies += left_copies([ref.at[a] for ref in la], l_s, a, obs, slim)
-            copies += right_copies([ref.at[a] for ref in ra], r_s, a, obs, slim)
+        parts, (l_s, r_s, p_s, sems) = refs[n_in : n_in + n_r], refs[n_in + n_r :]
+        copies = right_copies(refs[:n_c], p_s, 0, wide, slim)
+        for a in range(2):
+            blocks = [refs[at + a] if two else refs[at].at[a] for at, two in places]
+            copies += left_copies(blocks[:n_r], l_s, a, obs, slim)
+            copies += right_copies(blocks[n_r:], r_s, a, obs, slim)
         brought(copies, sems)
         for n in range(pairs):
             block = dot_first(l_s[n], r_s[...]).astype(bf)
@@ -102,17 +101,16 @@
                 out = parts[2 * n + m]
                 out[...] = part[m * slim : (m + 1) * slim].astype(out.dtype)
 
-    operands = [*lefts, *rights, *pivots]
-    return pl.pallas_call(
-        kernel,
-        in_specs=[VMEM] * len(operands),
+    return pl.pallas_call(
+        kernel,
+        in_specs=[VMEM] * n_in,
         out_specs=[VMEM] * n_r,
         out_shape=[jax.ShapeDtypeStruct((slim, wide), bf if t else f32) for t in range(n_r)],
         scratch_shapes=[
-            pltpu.VMEM((pairs, n_a * obs, 2 * slim), bf),
-            pltpu.VMEM((n_a * obs, n_c * slim), bf),
+            pltpu.VMEM((pairs, 2 * obs, 2 * slim), bf),
+            pltpu.VMEM((2 * obs, n_c * slim), bf),
             pltpu.VMEM((wide, n_c * slim), bf),
-            pltpu.SemaphoreType.DMA((n_a * (n_r + n_c) + n_c,)),
+            pltpu.SemaphoreType.DMA((2 * (n_r + n_c) + n_c,)),
         ],
         compiler_params=LIMIT,
         name="coupling_and_parts",
@@ -183,24 +181,132 @@
     )(*terms)
 
 
-def place_schur(ys, here, pieces):
+def band_products(week, left, wide):
+    n_b, obs, regions = wide.shape
+    slim = left.shape[1] // 2
+    tile = min(512, regions // 4)
+
+    def kernel(week_ref, left_ref, wide_ref, band_ref, send_a, send_b, turned):
+        @pl.when(pl.program_id(0) == 0)
+        def _():
+            turned[...] = left_ref[...].T
+
+        from_a = jnp.dot(turned[...], wide_ref[0], preferred_element_type=f32)
+        from_b = jnp.dot(turned[...], wide_ref[1], preferred_element_type=f32)
+        late = week_ref[0] >= 2
+        band_ref[0] = jnp.where(late, 0.0, from_a[:slim])
+        band_ref[1] = from_b[:slim]
+        band_ref[2] = jnp.where(late, from_a[:slim], 0.0)
+        send_a[...] = from_a[slim:].astype(bf)
+        send_b[...] = from_b[slim:].astype(bf)
+
+    return pl.pallas_call(
+        kernel,
+        grid=(regions // tile,),
+        in_specs=[SMEM, VMEM, pl.BlockSpec((n_b, obs, tile), lambda i: (0, 0, i))],
+        out_specs=[
+            pl.BlockSpec((3, slim, tile), lambda i: (0, 0, i)),
+            pl.BlockSpec((slim, tile), lambda i: (0, i)),
+            pl.BlockSpec((slim, tile), lambda i: (0, i)),
+        ],
+        out_shape=[
+            jax.ShapeDtypeStruct((3, slim, regions), f32),
+            jax.ShapeDtypeStruct((slim, regions), bf),
+            jax.ShapeDtypeStruct((slim, regions), bf),
+        ],
+        scratch_shapes=[pltpu.VMEM((2 * slim, obs), bf)],
+        compiler_params=LIMIT,
+        name="band_products",
+    )(week.reshape(1), left, wide)
+
+
+def add_lag_1(bands, arrived):
+    _, slim, regions = bands.shape
+    tile = min(2048, regions)
+
+    def kernel(band_ref, arrived_ref, out_ref):
+        out_ref[0] = band_ref[0] + arrived_ref[...].astype(f32)
+
+    band = pl.BlockSpec((1, slim, tile), lambda i: (1, 0, i))
+    return pl.pallas_call(
+        kernel,
+        grid=(regions // tile,),
+        in_specs=[band, pl.BlockSpec((slim, tile), lambda i: (0, i))],
+        out_specs=band,
+        out_shape=jax.ShapeDtypeStruct(bands.shape, f32),
+        input_output_aliases={0: 0},
+        name="add_lag_1",
+    )(bands, arrived)
+
+
+def finish_lag_0(first, left, wide, bands, arrived, prior, spans):
+    obs, slim = left.shape
+    regions = wide.shape[1]
+    tile = min(512, regions // 4)
+    span = regions // spans
+    each = span // tile
+
+    def kernel(first_ref, left_ref, wide_ref, band_ref, arrived_ref, prior_ref, out_ref, cut_ref, turned):
+        step = pl.program_id(0)
+
+        @pl.when(step == 0)
+        def _():
+            turned[...] = left_ref[...].T
+
+        last = jnp.dot(turned[...], wide_ref[...], preferred_element_type=f32)
+        rows = lax.broadcasted_iota(jnp.int32, (slim, tile), 0) + first_ref[0]
+        cols = lax.broadcasted_iota(jnp.int32, (slim, tile), 1) + step * tile
+        total = band_ref[0] + arrived_ref[...].astype(f32) + last
+        total = total + jnp.where(rows == cols, prior_ref[...], 0.0)
+        out_ref[0] = total
+        cut_ref[0] = total.astype(bf)
+
+    band = pl.BlockSpec((1, slim, tile), lambda i: (0, 0, i))
+    return pl.pallas_call(
+        kernel,
+        grid=(regions // tile,),
+        in_specs=[
+            SMEM,
+            VMEM,
+            pl.BlockSpec((obs, tile), lambda i: (0, i)),
+            band,
+            pl.BlockSpec((slim, tile), lambda i: (0, i)),
+            VMEM,
+        ],
+        out_specs=[band, pl.BlockSpec((1, slim, tile), lambda i: (i // each, 0, i % each))],
+        out_shape=[
+            jax.ShapeDtypeStruct(bands.shape, f32),
+            jax.ShapeDtypeStruct((spans, slim, span), bf),
+        ],
+        scratch_shapes=[pltpu.VMEM((slim, obs), bf)],
+        input_output_aliases={3: 0},
+        compiler_params=LIMIT,
+        name="finish_lag_0",
+    )(first.reshape(1), left, wide, bands, arrived, prior.reshape(slim, 1))
+
+
+def place_schur(ys, week, here, arrived, pieces):
     slim = pieces[0].shape[0]
-    n = len(pieces)
-
-    def kernel(ys_ref, here_ref, *refs):
+    n, m = len(pieces), len(arrived)
+
+    def kernel(ys_ref, week_ref, here_ref, *refs):
+        own = week_ref[0] == 1
         for t in range(n):
             for e in range(2):
                 at = pl.ds(pl.multiple_of(ys_ref[2 * t + e] * slim, slim), slim)
-                block = refs[t][:, e * slim : (e + 1) * slim]
-                refs[-1][:, at] = here_ref[:, at] - block.astype(f32)
-
-    return pl.pallas_call(
-        kernel,
-        in_specs=[SMEM] + [VMEM] * (1 + n),
+                total = -refs[m + t][:, e * slim : (e + 1) * slim].astype(f32)
+                total = total + jnp.where(own, here_ref[1, :, at].astype(f32), 0.0)
+                for ref in refs[:m]:
+                    total = total + ref[:, at].astype(f32)
+                refs[-1][:, at] = total
+
+    return pl.pallas_call(
+        kernel,
+        in_specs=[SMEM, SMEM] + [VMEM] * (1 + m + n),
         out_specs=VMEM,
         out_shape=jax.ShapeDtypeStruct((slim, 2 * n * slim), f32),
         name="place_schur",
-    )(ys, here, *pieces)
+    )(ys, week.reshape(1), here, *arrived, *pieces)
 
 
 def body(sensitivity, reach, obs_weight, prior_precision, pivot_solve):
@@ -222,7 +328,7 @@
 
     def over_z(block):
         own = [block] + [move(block, dz=s) for s in range(1, n_row)]
-        return own + [move(p, dk=1) for p in own]
+        return own + [move(p, dk=1) for p in [after(block, own[1])] + own[1:]]
 
     def to_rows(blocks):
         return [blocks[0]] + [move(blocks[t], dy=-t) for t in range(1, n_y)]
@@ -247,15 +353,19 @@
     )
     below = move(pair, dw=-1, weeks=(1, 2, 3))
     above = move(pair, dw=1, weeks=(1, 2))
-    across = move(pair, dw=2, weeks=(1, 2))
-    wide = [lax.all_gather(held[lag], ("row", "col"), axis=1, tiled=True) for lag in (2, 1, 0)]
-
+    across = move(pair, dw=2, weeks=(1, 2, 3))
+    wide = jnp.stack([by_week(held[0], held[0], held[2], held[2]), held[1]])
+    wide = lax.all_gather(wide, ("row", "col"), axis=2, tiled=True)
     def both(n):
         first = by_week(below[n], pair[n], pair[n], above[n])
         return jnp.stack([first, by_week(across[n], below[n], above[n], across[n])])
 
     left_c, right_c = over_y(both(0)), over_z(both(1))
     parts = coupling_and_parts(left_c, right_c, pivots)
+
+    last = by_week(across[1], across[1], held[0], held[0])
+    last = after(last, parts[0])
+    wide_last = lax.all_gather(last, ("row", "col"), axis=1, tiled=True)
 
     panel = parts[0]
     for t in range(1, n_y):
@@ -264,34 +374,27 @@
     rows_of = over_y(panel)
     slots = over_z(panel)
 
+    left = after(jnp.concatenate(held[:2], axis=1), panel)
+    bands, send_a, send_b = band_products(week, left, wide)
+
     terms = gram_terms((z - week + n_week) % n_week, rows_of, slots)
     terms = [terms[0]] + [move(terms[j], dw=j) for j in range(1, n_week)]
-    totals = to_rows(week_sum(terms, n_y))
-
-    mine = after(jnp.concatenate(held[::-1], axis=1), parts[0])
-    from_2 = contract_first(mine, wide[0])
-    near = move(from_2[slim : 2 * slim].astype(bf), dw=-1, weeks=(2, 3)).astype(f32)
-    far = move(from_2[:slim].astype(bf), dw=-2, weeks=(2, 3)).astype(f32)
-    from_1 = contract_first(after(mine[:, slim:], panel, near), wide[1])
-    next_0 = move(from_1[:slim].astype(bf), dw=-1, weeks=(1, 2, 3)).astype(f32)
-    band_2 = from_2[2 * slim :]
-    band_1 = from_1[slim:] + near
-    from_0 = contract_first(after(held[0], terms[0]), wide[2])
+    got_b = move(after(send_b, *terms[1:]), dw=-1, weeks=(1, 2, 3))
+    summed = week_sum(terms, n_y)
+    totals = to_rows(summed)
+    got_a = move(after(send_a, summed[0]), dw=-1, weeks=(2, 3))
+
     first = (lax.axis_index("row") * n_col + col) * slim
-    rows = lax.broadcasted_iota(jnp.int32, (slim, n_row * n_col * slim), 0)
-    cols = lax.broadcasted_iota(jnp.int32, (slim, n_row * n_col * slim), 1)
-    diagonal = jnp.where(cols == rows + first, prior_precision[0][:, None], 0.0)
-    band_0 = from_0 + next_0 + far + diagonal
-    bands = jnp.stack([band_0, band_1, band_2])
-
-    span = n_col * slim
-    here = jnp.where(week == 1, band_0[:, span : 2 * span], 0.0)
-    for j in range(1, n_week):
-        at = (1 + j) % n_week * span
-        here = here + move(band_0[:, at : at + span].astype(bf), dw=j, weeks=(1,)).astype(f32)
+    last = after(last, *totals)
+    bands, here = finish_lag_0(first, last, wide_last, bands, got_b, prior_precision, n_week)
+
+    arrived = [move(here[(1 + j) % n_week], dw=j, weeks=(1,)) for j in range(1, n_week)]
+    bands = add_lag_1(bands, got_a)
 
     ys = [((y + t) % n_y) * 2 + (k + e) % 2 for t in range(n_y) for e in range(2)]
-    schur = place_schur(jnp.stack(ys).astype(jnp.int32), here, totals)
+    ys = jnp.stack(ys).astype(jnp.int32)
+    schur = place_schur(ys, week, here, arrived, totals)
+
     return (bands[None], panel, schur)
 
 

time: 263 us -> 234 us (0.89); the launches traced: 263 us -> 231 us
  waiting for transfers between devices: 128 us -> 90.8 us
  Pallas kernels: 14.5 us -> 39.6 us
  matrix products: 21.4 us -> 0 us
  starting transfers between devices: 60.7 us -> 72.2 us
  local copies, waits for them, and re-layouts: 10.9 us -> 5.66 us
  other arithmetic: 12.7 us -> 7.83 us
    pallas_call x2 -> x5, Pallas kernels: 9.97 us -> 35 us  [the longest x1 13.1 us: band_products(): pl.pallas_call(kernel, grid=(regions // tile,), in_specs=[SMEM, VMEM, pl....]
    dot_general x3 -> x0, matrix products: 21.4 us -> none  [contract_first(): lax.dot_general(left, right, (((0,), (0,)), ((), ())), preferred_element_...]
    all_gather x3 -> x2, waiting for transfers between devices: 35.9 us -> 16.8 us  [the longest x1 16.8 us: body(): wide_last = lax.all_gather(last, ('row', 'col'), axis=1, tiled=True)]
    ppermute x45 -> x44, waiting for transfers between devices: 90.6 us -> 74 us  [moved(): return lax.ppermute(block, AXES, route)]
    ppermute x45 -> x44, starting transfers between devices: 60.6 us -> 72.1 us  [moved(): return lax.ppermute(block, AXES, route)]
    broadcast_in_dim x1 -> x0, other arithmetic: 3.11 us -> none  [body(): return (bands[None], panel, schur)]
    select_n x2 -> x4, other arithmetic: 1.69 us -> 4.7 us  [by_week(): return lax.select_n(week, *choices)]
    slice x5 -> x0, local copies, waits for them, and re-layouts: 2.7 us -> none  [the longest x1 1.52 us: body(): far = move(from_2[:slim].astype(bf), dw=-2, weeks=(2, 3)).astype(f32)]
  transfers between devices with their start and end apart: 48 -> 46, of which waited for: 18 -> 19; matrix products, arithmetic and copies ran while one was open for 14% -> 2% of each run, Pallas kernels for 5% -> 16%
where the time goes in v2:
time: 234 us; the launch traced here: 231 us
  waiting for transfers between devices  90.8 us (39%)
  starting transfers between devices  72.2 us (31%)
  Pallas kernels  39.6 us (17%)
  between operations  14.5 us (6%)
  other arithmetic  7.83 us (3%)
  local copies, waits for them, and re-layouts  5.66 us (2%)
    ppermute x44, waiting for transfers between devices, moved(): return lax.ppermute(block, AXES, route)  74 us
    ppermute x44, starting transfers between devices, moved(): return lax.ppermute(block, AXES, route)  72.1 us
    all_gather x1, waiting for transfers between devices, body(): wide_last = lax.all_gather(last, ('row', 'col'), axis=1, tiled=True)  16.8 us
    pallas_call x1, Pallas kernels, band_products(): pl.pallas_call(kernel, grid=(regions // tile,), in_specs=[SMEM, VMEM, pl....  13.1 us
    pallas_call x1, Pallas kernels, finish_lag_0(): pl.pallas_call(kernel, grid=(regions // tile,), in_specs=[SMEM, VMEM, pl....  8.44 us
    pallas_call x1, Pallas kernels, coupling_and_parts(): pl.pallas_call(kernel, in_specs=[VMEM] * n_in, out_specs=[VMEM] * n_r, ou...  8.02 us
    select_n x4, other arithmetic, by_week(): return lax.select_n(week, *choices)  4.7 us
  transfers between devices with their start and end apart: 46, of which 19 were waited for; matrix products, arithmetic and copies ran while one was open for 2% of the time, Pallas kernels for 16%

profile of v2, /device:TPU:2, one launch (start us, length us, event | category | flops | bytes accessed | tf_op | source)
XLA Modules:
  0.0 230.6 jit_solution(1854621850990258896)
XLA Ops:
  8.0 1.4 select_select_fusion.1
  9.4 1.4 broadcast_select_fusion
  11.7 4.0 %collective-permute-start = (bf16[2,1024,128]{2,1,0:T(8,128)(2,1)S(1)}, bf16[2,1024,128]{2,1,0:T(8,128)(2,1)S(1)}, u32[]{:S(2)}, u32[]{:S(2)}) collective-permute-start(bf16[2,1024,128]{2,1,0:T(8,128)(2,1)S(1)} %pad_maximum_fusion), channel_id=1, source_target_pairs={{32,96},{33,97},{34,98},{35,99},{36,100},{37,101},{38,102},{39,103... | collective-permute-start | bytes 1572872 | tf_op jit(solution)/shard_map/ppermute | solution.py:25
  15.8 1.9 collective-permute-start.8
  17.7 4.0 %collective-permute-start.9 = (bf16[2,1024,128]{2,1,0:T(8,128)(2,1)S(1)}, bf16[2,1024,128]{2,1,0:T(8,128)(2,1)S(1)}, u32[]{:S(2)}, u32[]{:S(2)}) collective-permute-start(bf16[2,1024,128]{2,1,0:T(8,128)(2,1)S(1)} %pad_maximum_fusion), channel_id=1, source_target_pairs={{32,64},{33,65},{34,66},{35,67},{36,68},{37,69},{38,70},{39,71},{4... | collective-permute-start | bytes 1572872 | tf_op jit(solution)/shard_map/ppermute | solution.py:25
  21.7 2.0 collective-permute-start.1
  23.6 3.6 %collective-permute-start.2 = (bf16[1024,128]{1,0:T(8,128)(2,1)}, bf16[1024,128]{1,0:T(8,128)(2,1)S(1)}, u32[]{:S(2)}, u32[]{:S(2)}) collective-permute-start(bf16[1024,128]{1,0:T(8,128)(2,1)} %refs_0_.1), channel_id=1, source_target_pairs={{0,16},{1,17},{2,18},{3,19},{4,20},{5,21},{6,22},{7,23},{8,24},{9,... | collective-permute-start | bytes 786440 | tf_op jit(solution)/shard_map/ppermute | solution.py:25
  27.2 2.8 %collective-permute-done = bf16[2,1024,128]{2,1,0:T(8,128)(2,1)S(1)} collective-permute-done((bf16[2,1024,128]{2,1,0:T(8,128)(2,1)S(1)}, bf16[2,1024,128]{2,1,0:T(8,128)(2,1)S(1)}, u32[]{:S(2)}, u32[]{:S(2)}) %collective-permute-start) | collective-permute-done | bytes 524320 | tf_op jit(solution)/shard_map/ppermute | solution.py:25
  30.0 4.0 %collective-permute-start.3 = (bf16[1024,128]{1,0:T(8,128)(2,1)}, bf16[1024,128]{1,0:T(8,128)(2,1)S(1)}, u32[]{:S(2)}, u32[]{:S(2)}) collective-permute-start(bf16[1024,128]{1,0:T(8,128)(2,1)} %refs_0_.1), channel_id=1, source_target_pairs={{0,24},{1,25},{2,26},{3,27},{4,28},{5,29},{6,30},{7,31},{8,0},{9,1... | collective-permute-start | bytes 786440 | tf_op jit(solution)/shard_map/ppermute | solution.py:25
  34.0 6.0 %collective-permute-done.8 = bf16[2,1024,128]{2,1,0:T(8,128)(2,1)S(1)} collective-permute-done((bf16[2,1024,128]{2,1,0:T(8,128)(2,1)S(1)}, bf16[2,1024,128]{2,1,0:T(8,128)(2,1)S(1)}, u32[]{:S(2)}, u32[]{:S(2)}) %collective-permute-start.8) | collective-permute-done | bytes 524320 | tf_op jit(solution)/shard_map/ppermute | solution.py:25
  40.2 2.0 collective-permute-start.13
  43.9 2.5 %collective-permute-start.14 = (bf16[2,1024,128]{2,1,0:T(8,128)(2,1)S(1)}, bf16[2,1024,128]{2,1,0:T(8,128)(2,1)S(1)}, u32[]{:S(2)}, u32[]{:S(2)}) collective-permute-start(bf16[2,1024,128]{2,1,0:T(8,128)(2,1)S(1)} %pad_maximum_fusion.2.refs_12_), channel_id=1, source_target_pairs={{0,16},{1,17},{2,18},{3,19},{4,20},{5,21},{6,22},{7,23},{8,24},{9,... | collective-permute-start | bytes 1572872 | tf_op jit(solution)/shard_map/ppermute | solution.py:25
  46.4 1.8 collective-permute-start.15
  48.2 1.6 collective-permute-start.10
  49.8 2.9 %collective-permute-start.11 = (bf16[2,1024,128]{2,1,0:T(8,128)(2,1)S(1)}, bf16[2,1024,128]{2,1,0:T(8,128)(2,1)S(1)}, u32[]{:S(2)}, u32[]{:S(2)}) collective-permute-start(bf16[2,1024,128]{2,1,0:T(8,128)(2,1)S(1)} %pad_maximum_fusion.1.refs_8_), channel_id=1, source_target_pairs={{0,4},{1,5},{2,6},{3,7},{4,0},{5,1},{6,2},{7,3},{8,12},{9,13},{10,... | collective-permute-start | bytes 1572872 | tf_op jit(solution)/shard_map/ppermute | solution.py:25
  52.7 5.5 %collective-permute-done.13.refs_13_ = bf16[2,1024,128]{2,1,0:T(8,128)(2,1)S(1)} collective-permute-done((bf16[2,1024,128]{2,1,0:T(8,128)(2,1)S(1)}, bf16[2,1024,128]{2,1,0:T(8,128)(2,1)S(1)}, u32[]{:S(2)}, u32[]{:S(2)}) %collective-permute-start.13) | collective-permute-done | bytes 524320 | tf_op jit(solution)/shard_map/ppermute | solution.py:25
  58.2 1.5 collective-permute-done.7.refs_7_
  59.7 3.1 %collective-permute-start.12 = (bf16[2,1024,128]{2,1,0:T(8,128)(2,1)S(1)}, bf16[2,1024,128]{2,1,0:T(8,128)(2,1)S(1)}, u32[]{:S(2)}, u32[]{:S(2)}) collective-permute-start(bf16[2,1024,128]{2,1,0:T(8,128)(2,1)S(1)} %pad_maximum_fusion.1.refs_8_), channel_id=1, source_target_pairs={{0,6},{1,7},{2,0},{3,1},{4,2},{5,3},{6,4},{7,5},{8,14},{9,15},{10,... | collective-permute-start | bytes 1572872 | tf_op jit(solution)/shard_map/ppermute | solution.py:25
  62.8 8.0 %collective-permute-done.14.refs_14_ = bf16[2,1024,128]{2,1,0:T(8,128)(2,1)S(1)} collective-permute-done((bf16[2,1024,128]{2,1,0:T(8,128)(2,1)S(1)}, bf16[2,1024,128]{2,1,0:T(8,128)(2,1)S(1)}, u32[]{:S(2)}, u32[]{:S(2)}) %collective-permute-start.14) | collective-permute-done | bytes 524320 | tf_op jit(solution)/shard_map/ppermute | solution.py:25
  71.5 9.0 %collective-permute-done.11.refs_10_ = bf16[2,1024,128]{2,1,0:T(8,128)(2,1)S(1)} collective-permute-done((bf16[2,1024,128]{2,1,0:T(8,128)(2,1)S(1)}, bf16[2,1024,128]{2,1,0:T(8,128)(2,1)S(1)}, u32[]{:S(2)}, u32[]{:S(2)}) %collective-permute-start.11) | collective-permute-done | bytes 524320 | tf_op jit(solution)/shard_map/ppermute | solution.py:25
  80.5 1.9 bitcast_select_fusion
  84.3 8.0 %coupling_and_parts.1 = (f32[128,1024]{1,0:T(8,128)S(1)}, bf16[128,1024]{1,0:T(8,128)(2,1)S(1)}, bf16[128,1024]{1,0:T(8,128)(2,1)S(1)}, bf16[128,1024]{1,0:T(8,128)(2,1)S(1)}) custom-call(bf16[1024,128]{1,0:T(8,128)(2,1)S(1)} %copy-done.4, bf16[1024,128]{1,0:T(8,128)(2,1)S(1)} %collective-permute-done.1.refs_1_, ...), custom_call_target="tpu_custom_call" | custom-call | tf_op jit(solution)/shard_map/coupling_and_parts/pallas_call | solution.py:104
  92.3 3.2 %collective-permute-start.20 = (bf16[128,1024]{1,0:T(8,128)(2,1)S(1)}, bf16[128,1024]{1,0:T(8,128)(2,1)S(1)}, u32[]{:S(2)}, u32[]{:S(2)}) collective-permute-start(bf16[128,1024]{1,0:T(8,128)(2,1)S(1)} %get-tuple-element.32), channel_id=1, source_target_pairs={{0,6},{1,7},{2,0},{3,1},{4,2},{5,3},{6,4},{7,5},{8,14},{9,15},{10,... | collective-permute-start | bytes 786440 | tf_op jit(solution)/shard_map/ppermute | solution.py:25
  96.7 9.7 %collective-permute-done.20 = bf16[128,1024]{1,0:T(8,128)(2,1)S(1)} collective-permute-done((bf16[128,1024]{1,0:T(8,128)(2,1)S(1)}, bf16[128,1024]{1,0:T(8,128)(2,1)S(1)}, u32[]{:S(2)}, u32[]{:S(2)}) %collective-permute-start.20) | collective-permute-done | bytes 262176 | tf_op jit(solution)/shard_map/ppermute | solution.py:25
  106.5 3.5 %collective-permute-done.21 = bf16[128,1024]{1,0:T(8,128)(2,1)S(1)} collective-permute-done((bf16[128,1024]{1,0:T(8,128)(2,1)S(1)}, bf16[128,1024]{1,0:T(8,128)(2,1)S(1)}, u32[]{:S(2)}, u32[]{:S(2)}) %collective-permute-start.21) | collective-permute-done | bytes 262176 | tf_op jit(solution)/shard_map/ppermute | solution.py:25
  110.0 5.6 %collective-permute-done.22 = bf16[128,1024]{1,0:T(8,128)(2,1)S(1)} collective-permute-done((bf16[128,1024]{1,0:T(8,128)(2,1)S(1)}, bf16[128,1024]{1,0:T(8,128)(2,1)S(1)}, u32[]{:S(2)}, u32[]{:S(2)}) %collective-permute-start.22) | collective-permute-done | bytes 262176 | tf_op jit(solution)/shard_map/ppermute | solution.py:25
  115.9 2.1 collective-permute-start.27
  119.1 4.2 %collective-permute-start.23 = (bf16[128,1024]{1,0:T(8,128)(2,1)S(1)}, bf16[128,1024]{1,0:T(8,128)(2,1)S(1)}, u32[]{:S(2)}, u32[]{:S(2)}) collective-permute-start(bf16[128,1024]{1,0:T(8,128)(2,1)S(1)} %add_convert_fusion.refs_1_.refs_5_), channel_id=1, source_target_pairs={{0,2},{1,3},{2,4},{3,5},{4,6},{5,7},{6,0},{7,1},{8,10},{9,11},{10,... | collective-permute-start | bytes 786440 | tf_op jit(solution)/shard_map/ppermute | solution.py:25
  123.2 2.3 collective-permute-start.24
  125.5 4.1 %collective-permute-done.26.refs_6_ = bf16[128,1024]{1,0:T(8,128)(2,1)S(1)} collective-permute-done((bf16[128,1024]{1,0:T(8,128)(2,1)S(1)}, bf16[128,1024]{1,0:T(8,128)(2,1)S(1)}, u32[]{:S(2)}, u32[]{:S(2)}) %collective-permute-start.26) | collective-permute-done | bytes 262176 | tf_op jit(solution)/shard_map/ppermute | solution.py:25
  129.7 4.1 %collective-permute-start.25 = (bf16[128,1024]{1,0:T(8,128)(2,1)S(1)}, bf16[128,1024]{1,0:T(8,128)(2,1)S(1)}, u32[]{:S(2)}, u32[]{:S(2)}) collective-permute-start(bf16[128,1024]{1,0:T(8,128)(2,1)S(1)} %add_convert_fusion.refs_1_.refs_5_), channel_id=1, source_target_pairs={{0,6},{1,7},{2,0},{3,1},{4,2},{5,3},{6,4},{7,5},{8,14},{9,15},{10,... | collective-permute-start | bytes 786440 | tf_op jit(solution)/shard_map/ppermute | solution.py:25
  134.8 4.1 %collective-permute-done.25.refs_4_ = bf16[128,1024]{1,0:T(8,128)(2,1)S(1)} collective-permute-done((bf16[128,1024]{1,0:T(8,128)(2,1)S(1)}, bf16[128,1024]{1,0:T(8,128)(2,1)S(1)}, u32[]{:S(2)}, u32[]{:S(2)}) %collective-permute-start.25) | collective-permute-done | bytes 262176 | tf_op jit(solution)/shard_map/ppermute | solution.py:25
  139.0 2.6 %gram_terms.1 = (f32[512,256]{1,0:T(8,128)S(1)}, bf16[512,256]{1,0:T(8,128)(2,1)}, bf16[512,256]{1,0:T(8,128)(2,1)}, bf16[512,256]{1,0:T(8,128)(2,1)}) custom-call(s32[1]{0:T(128)} %bitcast.9.refs_0_, bf16[128,1024]{1,0:T(8,128)(2,1)S(1)} %add_convert_fusion.refs_1_.refs_5_, bf16[128,1024]{1,0:T(8,128)(2,1)S(1)} %collective-permute-done.23.refs_2_, ...), custom_call_target="tpu_custom_call" | custom-call | tf_op jit(solution)/shard_map/gram_terms/pallas_call | solution.py:144
  141.7 2.0 collective-permute-start.34
  145.0 13.1 %band_products.1 = (f32[3,128,4096]{2,1,0:T(8,128)}, bf16[128,4096]{1,0:T(8,128)(2,1)S(1)}, bf16[128,4096]{1,0:T(8,128)(2,1)}) custom-call(s32[1]{0:T(128)} %bitcast.10.week_ref, bf16[1024,256]{1,0:T(8,128)(2,1)S(1)} %pad_maximum_fusion.3.left_ref, bf16[2,1024,4096]{2,1,0:T(8,128)(2,1)} %all-gather.5.cloned.1.call-done.wide_ref), custom_call_target="tpu_custom_call" | custom-call | tf_op jit(solution)/shard_map/band_products/pallas_call | solution.py:203
  159.6 4.6 %collective-permute-start.39 = (bf16[128,4096]{1,0:T(8,128)(2,1)}, bf16[128,4096]{1,0:T(8,128)(2,1)S(1)}, u32[]{:S(2)}, u32[]{:S(2)}) collective-permute-start(bf16[128,4096]{1,0:T(8,128)(2,1)} %get-tuple-element.48), channel_id=1, source_target_pairs={{32,0},{33,1},{34,2},{35,3},{36,4},{37,5},{38,6},{39,7},{40,8},{41... | collective-permute-start | bytes 3145736 | tf_op jit(solution)/shard_map/ppermute | solution.py:25
  164.2 2.0 week_sum.1
  167.5 3.8 %collective-permute-start.36 = (bf16[128,256]{1,0:T(8,128)(2,1)}, bf16[128,256]{1,0:T(8,128)(2,1)S(1)}, u32[]{:S(2)}, u32[]{:S(2)}) collective-permute-start(bf16[128,256]{1,0:T(8,128)(2,1)} %get-tuple-element.41), channel_id=1, source_target_pairs={{0,6},{1,7},{2,0},{3,1},{4,2},{5,3},{6,4},{7,5},{8,14},{9,15},{10,... | collective-permute-start | bytes 196616 | tf_op jit(solution)/shard_map/ppermute | solution.py:25
  172.4 2.7 %collective-permute-done.36.refs_4_ = bf16[128,256]{1,0:T(8,128)(2,1)S(1)} collective-permute-done((bf16[128,256]{1,0:T(8,128)(2,1)}, bf16[128,256]{1,0:T(8,128)(2,1)S(1)}, u32[]{:S(2)}, u32[]{:S(2)}) %collective-permute-start.36) | collective-permute-done | bytes 65568 | tf_op jit(solution)/shard_map/ppermute | solution.py:25
  175.1 2.8 %collective-permute-done.37.refs_5_ = bf16[128,256]{1,0:T(8,128)(2,1)S(1)} collective-permute-done((bf16[128,256]{1,0:T(8,128)(2,1)}, bf16[128,256]{1,0:T(8,128)(2,1)S(1)}, u32[]{:S(2)}, u32[]{:S(2)}) %collective-permute-start.37) | collective-permute-done | bytes 65568 | tf_op jit(solution)/shard_map/ppermute | solution.py:25
  178.2 16.8 %all-gather.3.cloned.1.call-done.wide_ref = bf16[1024,4096]{1,0:T(8,128)(2,1)} async-done(((bf16[1024,128]{1,0:T(8,128)(2,1)}), bf16[1024,4096]{1,0:T(8,128)(2,1)}) %all-gather.3.cloned.1.call-update) | async-done | bytes 8388624 | tf_op jit(solution)/shard_map/all_gather | solution.py:368
  195.0 8.4 %finish_lag_0.1 = (f32[3,128,4096]{2,1,0:T(8,128)}, bf16[4,128,1024]{2,1,0:T(8,128)(2,1)S(1)}) custom-call(s32[1]{0:T(128)} %bitcast.first_ref, bf16[1024,128]{1,0:T(8,128)(2,1)S(1)} %copy-done.1, bf16[1024,4096]{1,0:T(8,128)(2,1)} %all-gather.3.cloned.1.call-done.wide_ref, ...), custom_call_target="tpu_custom_call", output_to_operand_aliasing={{0}: (3, {})} | custom-call | tf_op jit(solution)/shard_map/finish_lag_0/pallas_call | solution.py:265
  204.3 2.9 %collective-permute-start.41 = (bf16[128,1024]{1,0:T(8,128)(2,1)}, bf16[128,1024]{1,0:T(8,128)(2,1)S(1)}, u32[]{:S(2)}, u32[]{:S(2)}) collective-permute-start(bf16[128,1024]{1,0:T(8,128)(2,1)} %get-tuple-element.61), channel_id=1, source_target_pairs={{32,64},{33,65},{34,66},{35,67},{36,68},{37,69},{38,70},{39,71},{4... | collective-permute-start | bytes 786440 | tf_op jit(solution)/shard_map/ppermute | solution.py:25
  207.2 1.8 collective-permute-start.42
  211.0 2.9 %add_lag_1.1 = f32[3,128,4096]{2,1,0:T(8,128)} custom-call(f32[3,128,4096]{2,1,0:T(8,128)} %get-tuple-element.49.band_ref, bf16[128,4096]{1,0:T(8,128)(2,1)} %collective-permute-done.40.arrived_ref), custom_call_target="tpu_custom_call", output_to_operand_aliasing={{}: (0, {})} | custom-call | tf_op jit(solution)/shard_map/add_lag_1/pallas_call | solution.py:231
  214.0 1.7 collective-permute-done.42.refs_1_
  215.6 5.0 %collective-permute-done.43.refs_2_ = bf16[128,1024]{1,0:T(8,128)(2,1)S(1)} collective-permute-done((bf16[128,1024]{1,0:T(8,128)(2,1)S(1)}, bf16[128,1024]{1,0:T(8,128)(2,1)S(1)}, u32[]{:S(2)}, u32[]{:S(2)}) %collective-permute-start.43) | collective-permute-done | bytes 262176 | tf_op jit(solution)/shard_map/ppermute | solution.py:25
  221.3 2.5 %place_schur.1 = f32[128,1024]{1,0:T(8,128)} custom-call(s32[8]{0:T(128)} %stack.59.ys_ref, s32[1]{0:T(128)} %bitcast.10.week_ref, bf16[4,128,1024]{2,1,0:T(8,128)(2,1)} %copy-done, bf16[128,1024]{1,0:T(8,128)(2,1)} %copy-done.12, bf16[128,1024]{1,0:T(8,128)(2,1)} %copy-done.13, bf16[128,1024]{1,0:T(8,128)(2,1)} %copy-done.14, ...), custom_call_target="tpu_custom_call" | custom-call | tf_op jit(solution)/shard_map/place_schur/pallas_call | solution.py:303
  (112 shorter events, 18.7 us)
Async XLA Ops:
  7.2 137.8 %all-gather.5.cloned.1.call-start = ((), (), s32[]{:S(2)}) async-start(), calls=%async_computation.1 | async-start | bytes 17301504 | tf_op jit(solution)/shard_map/all_gather | solution.py:358
  11.6 183.4 %all-gather.3.cloned.1.call-start = ((), (), s32[]{:S(2)}) async-start(), calls=%async_computation | async-start | bytes 8650752 | tf_op jit(solution)/shard_map/all_gather | solution.py:368
  11.7 18.3 %collective-permute-start = (bf16[2,1024,128]{2,1,0:T(8,128)(2,1)S(1)}, bf16[2,1024,128]{2,1,0:T(8,128)(2,1)S(1)}, u32[]{:S(2)}, u32[]{:S(2)}) collective-permute-start(bf16[2,1024,128]{2,1,0:T(8,128)(2,1)S(1)} %pad_maximum_fusion), channel_id=1, source_target_pairs={{32,96},{33,97},{34,98},{35,99},{36,100},{37,101},{38,102},{39,103... | collective-permute-start | bytes 1572872 | tf_op jit(solution)/shard_map/ppermute | solution.py:25
  15.8 24.3 %collective-permute-start.8 = (bf16[2,1024,128]{2,1,0:T(8,128)(2,1)S(1)}, bf16[2,1024,128]{2,1,0:T(8,128)(2,1)S(1)}, u32[]{:S(2)}, u32[]{:S(2)}) collective-permute-start(bf16[2,1024,128]{2,1,0:T(8,128)(2,1)S(1)} %pad_maximum_fusion), channel_id=1, source_target_pairs={{32,0},{33,1},{34,2},{35,3},{36,4},{37,5},{38,6},{39,7},{40,8},{41... | collective-permute-start | bytes 1572872 | tf_op jit(solution)/shard_map/ppermute | solution.py:25
  17.7 22.3 %collective-permute-start.9 = (bf16[2,1024,128]{2,1,0:T(8,128)(2,1)S(1)}, bf16[2,1024,128]{2,1,0:T(8,128)(2,1)S(1)}, u32[]{:S(2)}, u32[]{:S(2)}) collective-permute-start(bf16[2,1024,128]{2,1,0:T(8,128)(2,1)S(1)} %pad_maximum_fusion), channel_id=1, source_target_pairs={{32,64},{33,65},{34,66},{35,67},{36,68},{37,69},{38,70},{39,71},{4... | collective-permute-start | bytes 1572872 | tf_op jit(solution)/shard_map/ppermute | solution.py:25
  21.7 20.5 %collective-permute-start.1 = (bf16[1024,128]{1,0:T(8,128)(2,1)}, bf16[1024,128]{1,0:T(8,128)(2,1)S(1)}, u32[]{:S(2)}, u32[]{:S(2)}) collective-permute-start(bf16[1024,128]{1,0:T(8,128)(2,1)} %refs_0_.1), channel_id=1, source_target_pairs={{0,8},{1,9},{2,10},{3,11},{4,12},{5,13},{6,14},{7,15},{8,16},{9,17... | collective-permute-start | bytes 786440 | tf_op jit(solution)/shard_map/ppermute | solution.py:25
  23.6 20.2 %collective-permute-start.2 = (bf16[1024,128]{1,0:T(8,128)(2,1)}, bf16[1024,128]{1,0:T(8,128)(2,1)S(1)}, u32[]{:S(2)}, u32[]{:S(2)}) collective-permute-start(bf16[1024,128]{1,0:T(8,128)(2,1)} %refs_0_.1), channel_id=1, source_target_pairs={{0,16},{1,17},{2,18},{3,19},{4,20},{5,21},{6,22},{7,23},{8,24},{9,... | collective-permute-start | bytes 786440 | tf_op jit(solution)/shard_map/ppermute | solution.py:25
  30.0 13.9 %collective-permute-start.3 = (bf16[1024,128]{1,0:T(8,128)(2,1)}, bf16[1024,128]{1,0:T(8,128)(2,1)S(1)}, u32[]{:S(2)}, u32[]{:S(2)}) collective-permute-start(bf16[1024,128]{1,0:T(8,128)(2,1)} %refs_0_.1), channel_id=1, source_target_pairs={{0,24},{1,25},{2,26},{3,27},{4,28},{5,29},{6,30},{7,31},{8,0},{9,1... | collective-permute-start | bytes 786440 | tf_op jit(solution)/shard_map/ppermute | solution.py:25
  40.2 18.0 %collective-permute-start.13 = (bf16[2,1024,128]{2,1,0:T(8,128)(2,1)S(1)}, bf16[2,1024,128]{2,1,0:T(8,128)(2,1)S(1)}, u32[]{:S(2)}, u32[]{:S(2)}) collective-permute-start(bf16[2,1024,128]{2,1,0:T(8,128)(2,1)S(1)} %pad_maximum_fusion.2.refs_12_), channel_id=1, source_target_pairs={{0,8},{1,9},{2,10},{3,11},{4,12},{5,13},{6,14},{7,15},{8,16},{9,17... | collective-permute-start | bytes 1572872 | tf_op jit(solution)/shard_map/ppermute | solution.py:25
  42.2 4.2 %collective-permute-start.4 = (bf16[1024,128]{1,0:T(8,128)(2,1)S(1)}, bf16[1024,128]{1,0:T(8,128)(2,1)S(1)}, u32[]{:S(2)}, u32[]{:S(2)}) collective-permute-start(bf16[1024,128]{1,0:T(8,128)(2,1)S(1)} %copy-done.4), channel_id=1, source_target_pairs={{0,1},{1,0},{2,3},{3,2},{4,5},{5,4},{6,7},{7,6},{8,9},{9,8},{10,11... | collective-permute-start | bytes 786440 | tf_op jit(solution)/shard_map/ppermute | solution.py:25
  42.2 6.0 %collective-permute-start.5 = (bf16[1024,128]{1,0:T(8,128)(2,1)S(1)}, bf16[1024,128]{1,0:T(8,128)(2,1)S(1)}, u32[]{:S(2)}, u32[]{:S(2)}) collective-permute-start(bf16[1024,128]{1,0:T(8,128)(2,1)S(1)} %collective-permute-done.1.refs_1_), channel_id=1, source_target_pairs={{0,1},{1,0},{2,3},{3,2},{4,5},{5,4},{6,7},{7,6},{8,9},{9,8},{10,11... | collective-permute-start | bytes 786440 | tf_op jit(solution)/shard_map/ppermute | solution.py:25
  43.8 6.0 %collective-permute-start.6 = (bf16[1024,128]{1,0:T(8,128)(2,1)S(1)}, bf16[1024,128]{1,0:T(8,128)(2,1)S(1)}, u32[]{:S(2)}, u32[]{:S(2)}) collective-permute-start(bf16[1024,128]{1,0:T(8,128)(2,1)S(1)} %collective-permute-done.2.refs_2_), channel_id=1, source_target_pairs={{0,1},{1,0},{2,3},{3,2},{4,5},{5,4},{6,7},{7,6},{8,9},{9,8},{10,11... | collective-permute-start | bytes 786440 | tf_op jit(solution)/shard_map/ppermute | solution.py:25
  43.9 27.0 %collective-permute-start.14 = (bf16[2,1024,128]{2,1,0:T(8,128)(2,1)S(1)}, bf16[2,1024,128]{2,1,0:T(8,128)(2,1)S(1)}, u32[]{:S(2)}, u32[]{:S(2)}) collective-permute-start(bf16[2,1024,128]{2,1,0:T(8,128)(2,1)S(1)} %pad_maximum_fusion.2.refs_12_), channel_id=1, source_target_pairs={{0,16},{1,17},{2,18},{3,19},{4,20},{5,21},{6,22},{7,23},{8,24},{9,... | collective-permute-start | bytes 1572872 | tf_op jit(solution)/shard_map/ppermute | solution.py:25
  46.4 24.5 %collective-permute-start.15 = (bf16[2,1024,128]{2,1,0:T(8,128)(2,1)S(1)}, bf16[2,1024,128]{2,1,0:T(8,128)(2,1)S(1)}, u32[]{:S(2)}, u32[]{:S(2)}) collective-permute-start(bf16[2,1024,128]{2,1,0:T(8,128)(2,1)S(1)} %pad_maximum_fusion.2.refs_12_), channel_id=1, source_target_pairs={{0,24},{1,25},{2,26},{3,27},{4,28},{5,29},{6,30},{7,31},{8,0},{9,1... | collective-permute-start | bytes 1572872 | tf_op jit(solution)/shard_map/ppermute | solution.py:25
  48.2 23.1 %collective-permute-start.10 = (bf16[2,1024,128]{2,1,0:T(8,128)(2,1)S(1)}, bf16[2,1024,128]{2,1,0:T(8,128)(2,1)S(1)}, u32[]{:S(2)}, u32[]{:S(2)}) collective-permute-start(bf16[2,1024,128]{2,1,0:T(8,128)(2,1)S(1)} %pad_maximum_fusion.1.refs_8_), channel_id=1, source_target_pairs={{0,2},{1,3},{2,4},{3,5},{4,6},{5,7},{6,0},{7,1},{8,10},{9,11},{10,... | collective-permute-start | bytes 1572872 | tf_op jit(solution)/shard_map/ppermute | solution.py:25
  49.8 30.6 %collective-permute-start.11 = (bf16[2,1024,128]{2,1,0:T(8,128)(2,1)S(1)}, bf16[2,1024,128]{2,1,0:T(8,128)(2,1)S(1)}, u32[]{:S(2)}, u32[]{:S(2)}) collective-permute-start(bf16[2,1024,128]{2,1,0:T(8,128)(2,1)S(1)} %pad_maximum_fusion.1.refs_8_), channel_id=1, source_target_pairs={{0,4},{1,5},{2,6},{3,7},{4,0},{5,1},{6,2},{7,3},{8,12},{9,13},{10,... | collective-permute-start | bytes 1572872 | tf_op jit(solution)/shard_map/ppermute | solution.py:25
  58.2 1.5 collective-permute-start.7
  59.7 22.6 %collective-permute-start.12 = (bf16[2,1024,128]{2,1,0:T(8,128)(2,1)S(1)}, bf16[2,1024,128]{2,1,0:T(8,128)(2,1)S(1)}, u32[]{:S(2)}, u32[]{:S(2)}) collective-permute-start(bf16[2,1024,128]{2,1,0:T(8,128)(2,1)S(1)} %pad_maximum_fusion.1.refs_8_), channel_id=1, source_target_pairs={{0,6},{1,7},{2,0},{3,1},{4,2},{5,3},{6,4},{7,5},{8,14},{9,15},{10,... | collective-permute-start | bytes 1572872 | tf_op jit(solution)/shard_map/ppermute | solution.py:25
  70.9 11.5 %collective-permute-start.16 = (bf16[2,1024,128]{2,1,0:T(8,128)(2,1)S(1)}, bf16[2,1024,128]{2,1,0:T(8,128)(2,1)S(1)}, u32[]{:S(2)}, u32[]{:S(2)}) collective-permute-start(bf16[2,1024,128]{2,1,0:T(8,128)(2,1)S(1)} %pad_maximum_fusion.2.refs_12_), channel_id=1, source_target_pairs={{0,1},{1,0},{2,3},{3,2},{4,5},{5,4},{6,7},{7,6},{8,9},{9,8},{10,11... | collective-permute-start | bytes 1572872 | tf_op jit(solution)/shard_map/ppermute | solution.py:25
  70.9 11.4 %collective-permute-start.17 = (bf16[2,1024,128]{2,1,0:T(8,128)(2,1)S(1)}, bf16[2,1024,128]{2,1,0:T(8,128)(2,1)S(1)}, u32[]{:S(2)}, u32[]{:S(2)}) collective-permute-start(bf16[2,1024,128]{2,1,0:T(8,128)(2,1)S(1)} %collective-permute-done.13.refs_13_), channel_id=1, source_target_pairs={{0,1},{1,0},{2,3},{3,2},{4,5},{5,4},{6,7},{7,6},{8,9},{9,8},{10,11... | collective-permute-start | bytes 1572872 | tf_op jit(solution)/shard_map/ppermute | solution.py:25
  71.4 11.0 %collective-permute-start.18 = (bf16[2,1024,128]{2,1,0:T(8,128)(2,1)S(1)}, bf16[2,1024,128]{2,1,0:T(8,128)(2,1)S(1)}, u32[]{:S(2)}, u32[]{:S(2)}) collective-permute-start(bf16[2,1024,128]{2,1,0:T(8,128)(2,1)S(1)} %collective-permute-done.14.refs_14_), channel_id=1, source_target_pairs={{0,1},{1,0},{2,3},{3,2},{4,5},{5,4},{6,7},{7,6},{8,9},{9,8},{10,11... | collective-permute-start | bytes 1572872 | tf_op jit(solution)/shard_map/ppermute | solution.py:25
  80.5 1.9 collective-permute-start.19
  92.3 14.1 %collective-permute-start.20 = (bf16[128,1024]{1,0:T(8,128)(2,1)S(1)}, bf16[128,1024]{1,0:T(8,128)(2,1)S(1)}, u32[]{:S(2)}, u32[]{:S(2)}) collective-permute-start(bf16[128,1024]{1,0:T(8,128)(2,1)S(1)} %get-tuple-element.32), channel_id=1, source_target_pairs={{0,6},{1,7},{2,0},{3,1},{4,2},{5,3},{6,4},{7,5},{8,14},{9,15},{10,... | collective-permute-start | bytes 786440 | tf_op jit(solution)/shard_map/ppermute | solution.py:25
  95.6 14.4 %collective-permute-start.21 = (bf16[128,1024]{1,0:T(8,128)(2,1)S(1)}, bf16[128,1024]{1,0:T(8,128)(2,1)S(1)}, u32[]{:S(2)}, u32[]{:S(2)}) collective-permute-start(bf16[128,1024]{1,0:T(8,128)(2,1)S(1)} %get-tuple-element.33), channel_id=1, source_target_pairs={{0,4},{1,5},{2,6},{3,7},{4,0},{5,1},{6,2},{7,3},{8,12},{9,13},{10,... | collective-permute-start | bytes 786440 | tf_op jit(solution)/shard_map/ppermute | solution.py:25
  95.6 20.0 %collective-permute-start.22 = (bf16[128,1024]{1,0:T(8,128)(2,1)S(1)}, bf16[128,1024]{1,0:T(8,128)(2,1)S(1)}, u32[]{:S(2)}, u32[]{:S(2)}) collective-permute-start(bf16[128,1024]{1,0:T(8,128)(2,1)S(1)} %get-tuple-element.34), channel_id=1, source_target_pairs={{0,2},{1,3},{2,4},{3,5},{4,6},{5,7},{6,0},{7,1},{8,10},{9,11},{10,... | collective-permute-start | bytes 786440 | tf_op jit(solution)/shard_map/ppermute | solution.py:25
  115.8 42.4 %copy-start.2 = (bf16[128,1024]{1,0:T(8,128)(2,1)}, bf16[128,1024]{1,0:T(8,128)(2,1)S(1)}, u32[]{:S(2)}) copy-start(bf16[128,1024]{1,0:T(8,128)(2,1)S(1)} %add_convert_fusion.refs_1_.refs_5_) | copy-start | bytes 786436
  115.8 13.9 %collective-permute-start.26 = (bf16[128,1024]{1,0:T(8,128)(2,1)S(1)}, bf16[128,1024]{1,0:T(8,128)(2,1)S(1)}, u32[]{:S(2)}, u32[]{:S(2)}) collective-permute-start(bf16[128,1024]{1,0:T(8,128)(2,1)S(1)} %add_convert_fusion.refs_1_.refs_5_), channel_id=1, source_target_pairs={{0,8},{1,9},{2,10},{3,11},{4,12},{5,13},{6,14},{7,15},{8,16},{9,17... | collective-permute-start | bytes 786440 | tf_op jit(solution)/shard_map/ppermute | solution.py:25
  115.9 17.9 %collective-permute-start.27 = (bf16[128,1024]{1,0:T(8,128)(2,1)S(1)}, bf16[128,1024]{1,0:T(8,128)(2,1)S(1)}, u32[]{:S(2)}, u32[]{:S(2)}) collective-permute-start(bf16[128,1024]{1,0:T(8,128)(2,1)S(1)} %add_convert_fusion.refs_1_.refs_5_), channel_id=1, source_target_pairs={{0,16},{1,17},{2,18},{3,19},{4,20},{5,21},{6,22},{7,23},{8,24},{9,... | collective-permute-start | bytes 786440 | tf_op jit(solution)/shard_map/ppermute | solution.py:25
  118.0 15.8 %collective-permute-start.28 = (bf16[128,1024]{1,0:T(8,128)(2,1)S(1)}, bf16[128,1024]{1,0:T(8,128)(2,1)S(1)}, u32[]{:S(2)}, u32[]{:S(2)}) collective-permute-start(bf16[128,1024]{1,0:T(8,128)(2,1)S(1)} %add_convert_fusion.refs_1_.refs_5_), channel_id=1, source_target_pairs={{0,24},{1,25},{2,26},{3,27},{4,28},{5,29},{6,30},{7,31},{8,0},{9,1... | collective-permute-start | bytes 786440 | tf_op jit(solution)/shard_map/ppermute | solution.py:25
  119.1 15.2 %collective-permute-start.23 = (bf16[128,1024]{1,0:T(8,128)(2,1)S(1)}, bf16[128,1024]{1,0:T(8,128)(2,1)S(1)}, u32[]{:S(2)}, u32[]{:S(2)}) collective-permute-start(bf16[128,1024]{1,0:T(8,128)(2,1)S(1)} %add_convert_fusion.refs_1_.refs_5_), channel_id=1, source_target_pairs={{0,2},{1,3},{2,4},{3,5},{4,6},{5,7},{6,0},{7,1},{8,10},{9,11},{10,... | collective-permute-start | bytes 786440 | tf_op jit(solution)/shard_map/ppermute | solution.py:25
  123.2 11.4 %collective-permute-start.24 = (bf16[128,1024]{1,0:T(8,128)(2,1)S(1)}, bf16[128,1024]{1,0:T(8,128)(2,1)S(1)}, u32[]{:S(2)}, u32[]{:S(2)}) collective-permute-start(bf16[128,1024]{1,0:T(8,128)(2,1)S(1)} %add_convert_fusion.refs_1_.refs_5_), channel_id=1, source_target_pairs={{0,4},{1,5},{2,6},{3,7},{4,0},{5,1},{6,2},{7,3},{8,12},{9,13},{10,... | collective-permute-start | bytes 786440 | tf_op jit(solution)/shard_map/ppermute | solution.py:25
  129.7 9.3 %collective-permute-start.25 = (bf16[128,1024]{1,0:T(8,128)(2,1)S(1)}, bf16[128,1024]{1,0:T(8,128)(2,1)S(1)}, u32[]{:S(2)}, u32[]{:S(2)}) collective-permute-start(bf16[128,1024]{1,0:T(8,128)(2,1)S(1)} %add_convert_fusion.refs_1_.refs_5_), channel_id=1, source_target_pairs={{0,6},{1,7},{2,0},{3,1},{4,2},{5,3},{6,4},{7,5},{8,14},{9,15},{10,... | collective-permute-start | bytes 786440 | tf_op jit(solution)/shard_map/ppermute | solution.py:25
  133.8 5.2 %collective-permute-start.29 = (bf16[128,1024]{1,0:T(8,128)(2,1)S(1)}, bf16[128,1024]{1,0:T(8,128)(2,1)S(1)}, u32[]{:S(2)}, u32[]{:S(2)}) collective-permute-start(bf16[128,1024]{1,0:T(8,128)(2,1)S(1)} %add_convert_fusion.refs_1_.refs_5_), channel_id=1, source_target_pairs={{0,1},{1,0},{2,3},{3,2},{4,5},{5,4},{6,7},{7,6},{8,9},{9,8},{10,11... | collective-permute-start | bytes 786440 | tf_op jit(solution)/shard_map/ppermute | solution.py:25
  133.8 5.2 %collective-permute-start.30 = (bf16[128,1024]{1,0:T(8,128)(2,1)S(1)}, bf16[128,1024]{1,0:T(8,128)(2,1)S(1)}, u32[]{:S(2)}, u32[]{:S(2)}) collective-permute-start(bf16[128,1024]{1,0:T(8,128)(2,1)S(1)} %collective-permute-done.26.refs_6_), channel_id=1, source_target_pairs={{0,1},{1,0},{2,3},{3,2},{4,5},{5,4},{6,7},{7,6},{8,9},{9,8},{10,11... | collective-permute-start | bytes 786440 | tf_op jit(solution)/shard_map/ppermute | solution.py:25
  134.3 4.7 %collective-permute-start.31 = (bf16[128,1024]{1,0:T(8,128)(2,1)S(1)}, bf16[128,1024]{1,0:T(8,128)(2,1)S(1)}, u32[]{:S(2)}, u32[]{:S(2)}) collective-permute-start(bf16[128,1024]{1,0:T(8,128)(2,1)S(1)} %collective-permute-done.27.refs_7_), channel_id=1, source_target_pairs={{0,1},{1,0},{2,3},{3,2},{4,5},{5,4},{6,7},{7,6},{8,9},{9,8},{10,11... | collective-permute-start | bytes 786440 | tf_op jit(solution)/shard_map/ppermute | solution.py:25
  134.7 4.3 %collective-permute-start.32 = (bf16[128,1024]{1,0:T(8,128)(2,1)S(1)}, bf16[128,1024]{1,0:T(8,128)(2,1)S(1)}, u32[]{:S(2)}, u32[]{:S(2)}) collective-permute-start(bf16[128,1024]{1,0:T(8,128)(2,1)S(1)} %collective-permute-done.28.refs_8_), channel_id=1, source_target_pairs={{0,1},{1,0},{2,3},{3,2},{4,5},{5,4},{6,7},{7,6},{8,9},{9,8},{10,11... | collective-permute-start | bytes 786440 | tf_op jit(solution)/shard_map/ppermute | solution.py:25
  141.6 16.5 %collective-permute-start.33 = (bf16[512,256]{1,0:T(8,128)(2,1)}, bf16[512,256]{1,0:T(8,128)(2,1)S(1)}, u32[]{:S(2)}, u32[]{:S(2)}) collective-permute-start(bf16[512,256]{1,0:T(8,128)(2,1)} %get-tuple-element.37), channel_id=1, source_target_pairs={{0,32},{1,33},{2,34},{3,35},{4,36},{5,37},{6,38},{7,39},{8,40},{9,... | collective-permute-start | bytes 786440 | tf_op jit(solution)/shard_map/ppermute | solution.py:25
  141.7 16.5 %collective-permute-start.34 = (bf16[512,256]{1,0:T(8,128)(2,1)}, bf16[512,256]{1,0:T(8,128)(2,1)S(1)}, u32[]{:S(2)}, u32[]{:S(2)}) collective-permute-start(bf16[512,256]{1,0:T(8,128)(2,1)} %get-tuple-element.38), channel_id=1, source_target_pairs={{0,64},{1,65},{2,66},{3,67},{4,68},{5,69},{6,70},{7,71},{8,72},{9,... | collective-permute-start | bytes 786440 | tf_op jit(solution)/shard_map/ppermute | solution.py:25
  143.7 14.5 %collective-permute-start.35 = (bf16[512,256]{1,0:T(8,128)(2,1)}, bf16[512,256]{1,0:T(8,128)(2,1)S(1)}, u32[]{:S(2)}, u32[]{:S(2)}) collective-permute-start(bf16[512,256]{1,0:T(8,128)(2,1)} %get-tuple-element.39), channel_id=1, source_target_pairs={{0,96},{1,97},{2,98},{3,99},{4,100},{5,101},{6,102},{7,103},{8,104... | collective-permute-start | bytes 786440 | tf_op jit(solution)/shard_map/ppermute | solution.py:25
  145.0 50.0 %copy-start.1 = (bf16[1024,128]{1,0:T(8,128)(2,1)S(1)}, bf16[1024,128]{1,0:T(8,128)(2,1)}, u32[]{:S(2)}) copy-start(bf16[1024,128]{1,0:T(8,128)(2,1)} %get-tuple-element.44.left_ref) | copy-start | bytes 786436
  159.6 35.4 %collective-permute-start.39 = (bf16[128,4096]{1,0:T(8,128)(2,1)}, bf16[128,4096]{1,0:T(8,128)(2,1)S(1)}, u32[]{:S(2)}, u32[]{:S(2)}) collective-permute-start(bf16[128,4096]{1,0:T(8,128)(2,1)} %get-tuple-element.48), channel_id=1, source_target_pairs={{32,0},{33,1},{34,2},{35,3},{36,4},{37,5},{38,6},{39,7},{40,8},{41... | collective-permute-start | bytes 3145736 | tf_op jit(solution)/shard_map/ppermute | solution.py:25
  166.2 44.8 %collective-permute-start.40 = (bf16[128,4096]{1,0:T(8,128)(2,1)S(1)}, bf16[128,4096]{1,0:T(8,128)(2,1)}, u32[]{:S(2)}, u32[]{:S(2)}) collective-permute-start(bf16[128,4096]{1,0:T(8,128)(2,1)S(1)} %get-tuple-element.51), channel_id=1, source_target_pairs={{64,32},{65,33},{66,34},{67,35},{68,36},{69,37},{70,38},{71,39},{7... | collective-permute-start | bytes 3145736 | tf_op jit(solution)/shard_map/ppermute | solution.py:25
  167.5 7.6 %collective-permute-start.36 = (bf16[128,256]{1,0:T(8,128)(2,1)}, bf16[128,256]{1,0:T(8,128)(2,1)S(1)}, u32[]{:S(2)}, u32[]{:S(2)}) collective-permute-start(bf16[128,256]{1,0:T(8,128)(2,1)} %get-tuple-element.41), channel_id=1, source_target_pairs={{0,6},{1,7},{2,0},{3,1},{4,2},{5,3},{6,4},{7,5},{8,14},{9,15},{10,... | collective-permute-start | bytes 196616 | tf_op jit(solution)/shard_map/ppermute | solution.py:25
  171.3 6.6 %collective-permute-start.37 = (bf16[128,256]{1,0:T(8,128)(2,1)}, bf16[128,256]{1,0:T(8,128)(2,1)S(1)}, u32[]{:S(2)}, u32[]{:S(2)}) collective-permute-start(bf16[128,256]{1,0:T(8,128)(2,1)} %get-tuple-element.42), channel_id=1, source_target_pairs={{0,4},{1,5},{2,6},{3,7},{4,0},{5,1},{6,2},{7,3},{8,12},{9,13},{10,... | collective-permute-start | bytes 196616 | tf_op jit(solution)/shard_map/ppermute | solution.py:25
  171.3 6.9 %collective-permute-start.38 = (bf16[128,256]{1,0:T(8,128)(2,1)}, bf16[128,256]{1,0:T(8,128)(2,1)S(1)}, u32[]{:S(2)}, u32[]{:S(2)}) collective-permute-start(bf16[128,256]{1,0:T(8,128)(2,1)} %get-tuple-element.43), channel_id=1, source_target_pairs={{0,2},{1,3},{2,4},{3,5},{4,6},{5,7},{6,0},{7,1},{8,10},{9,11},{10,... | collective-permute-start | bytes 196616 | tf_op jit(solution)/shard_map/ppermute | solution.py:25
  204.3 9.6 %collective-permute-start.41 = (bf16[128,1024]{1,0:T(8,128)(2,1)}, bf16[128,1024]{1,0:T(8,128)(2,1)S(1)}, u32[]{:S(2)}, u32[]{:S(2)}) collective-permute-start(bf16[128,1024]{1,0:T(8,128)(2,1)} %get-tuple-element.61), channel_id=1, source_target_pairs={{32,64},{33,65},{34,66},{35,67},{36,68},{37,69},{38,70},{39,71},{4... | collective-permute-start | bytes 786440 | tf_op jit(solution)/shard_map/ppermute | solution.py:25
  207.2 8.4 %collective-permute-start.42 = (bf16[128,1024]{1,0:T(8,128)(2,1)S(1)}, bf16[128,1024]{1,0:T(8,128)(2,1)S(1)}, u32[]{:S(2)}, u32[]{:S(2)}) collective-permute-start(bf16[128,1024]{1,0:T(8,128)(2,1)S(1)} %get-tuple-element.60), channel_id=1, source_target_pairs={{32,96},{33,97},{34,98},{35,99},{36,100},{37,101},{38,102},{39,103... | collective-permute-start | bytes 786440 | tf_op jit(solution)/shard_map/ppermute | solution.py:25
  209.0 11.6 %collective-permute-start.43 = (bf16[128,1024]{1,0:T(8,128)(2,1)S(1)}, bf16[128,1024]{1,0:T(8,128)(2,1)S(1)}, u32[]{:S(2)}, u32[]{:S(2)}) collective-permute-start(bf16[128,1024]{1,0:T(8,128)(2,1)S(1)} %get-tuple-element.59), channel_id=1, source_target_pairs={{32,0},{33,1},{34,2},{35,3},{36,4},{37,5},{38,6},{39,7},{40,8},{41... | collective-permute-start | bytes 786440 | tf_op jit(solution)/shard_map/ppermute | solution.py:25
  (20 other events, 203.8 us)
Sparse Core Ops, SparseCore 0:
  11.7 113.9 all-gather.4
  127.9 67.0 all-gather.2

commit v3 on v2

--- a/solution.py
+++ b/solution.py
@@ -183,16 +183,16 @@
 
 def band_products(week, left, wide):
     n_b, obs, regions = wide.shape
-    slim = left.shape[1] // 2
-    tile = min(512, regions // 4)
+    slim = left.shape[1] // 4
+    tile = min(1024, regions // 4)
 
     def kernel(week_ref, left_ref, wide_ref, band_ref, send_a, send_b, turned):
         @pl.when(pl.program_id(0) == 0)
         def _():
             turned[...] = left_ref[...].T
 
-        from_a = jnp.dot(turned[...], wide_ref[0], preferred_element_type=f32)
-        from_b = jnp.dot(turned[...], wide_ref[1], preferred_element_type=f32)
+        from_a = jnp.dot(turned[: 2 * slim], wide_ref[0], preferred_element_type=f32)
+        from_b = jnp.dot(turned[2 * slim :], wide_ref[1], preferred_element_type=f32)
         late = week_ref[0] >= 2
         band_ref[0] = jnp.where(late, 0.0, from_a[:slim])
         band_ref[1] = from_b[:slim]
@@ -214,7 +214,7 @@
             jax.ShapeDtypeStruct((slim, regions), bf),
             jax.ShapeDtypeStruct((slim, regions), bf),
         ],
-        scratch_shapes=[pltpu.VMEM((2 * slim, obs), bf)],
+        scratch_shapes=[pltpu.VMEM((4 * slim, obs), bf)],
         compiler_params=LIMIT,
         name="band_products",
     )(week.reshape(1), left, wide)
@@ -242,11 +242,12 @@
 def finish_lag_0(first, left, wide, bands, arrived, prior, spans):
     obs, slim = left.shape
     regions = wide.shape[1]
-    tile = min(512, regions // 4)
+    tile = min(1024, regions // 4)
     span = regions // spans
     each = span // tile
 
-    def kernel(first_ref, left_ref, wide_ref, band_ref, arrived_ref, prior_ref, out_ref, cut_ref, turned):
+    def kernel(first_ref, left_ref, wide_ref, band_ref, arrived_ref, prior_ref, out_ref, *rest):
+        cuts, turned = rest[:spans], rest[spans]
         step = pl.program_id(0)
 
         @pl.when(step == 0)
@@ -259,7 +260,14 @@
         total = band_ref[0] + arrived_ref[...].astype(f32) + last
         total = total + jnp.where(rows == cols, prior_ref[...], 0.0)
         out_ref[0] = total
-        cut_ref[0] = total.astype(bf)
+        for n in range(spans):
+
+            @pl.when(step // each == n)
+            def _():
+                cuts[n][...] = total.astype(bf)
+
+    def cut_spec(n):
+        return pl.BlockSpec((slim, tile), lambda i: (0, jnp.clip(i - n * each, 0, each - 1)))
 
     band = pl.BlockSpec((1, slim, tile), lambda i: (0, 0, i))
     return pl.pallas_call(
@@ -273,11 +281,9 @@
             pl.BlockSpec((slim, tile), lambda i: (0, i)),
             VMEM,
         ],
-        out_specs=[band, pl.BlockSpec((1, slim, tile), lambda i: (i // each, 0, i % each))],
-        out_shape=[
-            jax.ShapeDtypeStruct(bands.shape, f32),
-            jax.ShapeDtypeStruct((spans, slim, span), bf),
-        ],
+        out_specs=[band] + [cut_spec(n) for n in range(spans)],
+        out_shape=[jax.ShapeDtypeStruct(bands.shape, f32)]
+        + [jax.ShapeDtypeStruct((slim, span), bf)] * spans,
         scratch_shapes=[pltpu.VMEM((slim, obs), bf)],
         input_output_aliases={3: 0},
         compiler_params=LIMIT,
@@ -295,7 +301,7 @@
             for e in range(2):
                 at = pl.ds(pl.multiple_of(ys_ref[2 * t + e] * slim, slim), slim)
                 total = -refs[m + t][:, e * slim : (e + 1) * slim].astype(f32)
-                total = total + jnp.where(own, here_ref[1, :, at].astype(f32), 0.0)
+                total = total + jnp.where(own, here_ref[:, at].astype(f32), 0.0)
                 for ref in refs[:m]:
                     total = total + ref[:, at].astype(f32)
                 refs[-1][:, at] = total
@@ -339,6 +345,8 @@
     def by_week(*choices):
         return lax.select_n(week, *choices)
 
+    wide = jnp.stack([by_week(local[0], local[0], local[2], local[2]), local[1]])
+    wide = lax.all_gather(wide, ("row", "col"), axis=2, tiled=True)
     pivots = over_z(pivot_solve)
 
     root = jnp.sqrt(obs_weight[0])
@@ -354,8 +362,6 @@
     below = move(pair, dw=-1, weeks=(1, 2, 3))
     above = move(pair, dw=1, weeks=(1, 2))
     across = move(pair, dw=2, weeks=(1, 2, 3))
-    wide = jnp.stack([by_week(held[0], held[0], held[2], held[2]), held[1]])
-    wide = lax.all_gather(wide, ("row", "col"), axis=2, tiled=True)
     def both(n):
         first = by_week(below[n], pair[n], pair[n], above[n])
         return jnp.stack([first, by_week(across[n], below[n], above[n], across[n])])
@@ -374,7 +380,14 @@
     rows_of = over_y(panel)
     slots = over_z(panel)
 
-    left = after(jnp.concatenate(held[:2], axis=1), panel)
+    weight = [
+        jnp.where((reach[0] >= lag) & (week >= lag), obs_weight[0], 0.0) for lag in range(lags)
+    ]
+    weight = (by_week(weight[0], weight[0], weight[2], weight[2]), weight[1])
+    left = [
+        (weight[b][:, None] * local[a].astype(f32)).astype(bf) for b in range(2) for a in range(2)
+    ]
+    left = after(jnp.concatenate(left, axis=1), panel)
     bands, send_a, send_b = band_products(week, left, wide)
 
     terms = gram_terms((z - week + n_week) % n_week, rows_of, slots)
@@ -386,14 +399,14 @@
 
     first = (lax.axis_index("row") * n_col + col) * slim
     last = after(last, *totals)
-    bands, here = finish_lag_0(first, last, wide_last, bands, got_b, prior_precision, n_week)
+    bands, *here = finish_lag_0(first, last, wide_last, bands, got_b, prior_precision, n_week)
 
     arrived = [move(here[(1 + j) % n_week], dw=j, weeks=(1,)) for j in range(1, n_week)]
     bands = add_lag_1(bands, got_a)
 
     ys = [((y + t) % n_y) * 2 + (k + e) % 2 for t in range(n_y) for e in range(2)]
     ys = jnp.stack(ys).astype(jnp.int32)
-    schur = place_schur(ys, week, here, arrived, totals)
+    schur = place_schur(ys, week, here[1], arrived, totals)
 
     return (bands[None], panel, schur)
 

time: 234 us -> 230 us (0.983); the launches traced: 231 us -> 229 us
  local copies, waits for them, and re-layouts: 5.66 us -> 13.9 us
  Pallas kernels: 39.6 us -> 35.4 us
  starting transfers between devices: 72.2 us -> 68.8 us
    all_gather x1, waiting for transfers between devices: 16.8 us -> 4.03 us  [body(): wide_last = lax.all_gather(last, ('row', 'col'), axis=1, tiled=True)]
    ppermute x44, waiting for transfers between devices: 74 us -> 85.4 us  [moved(): return lax.ppermute(block, AXES, route)]
    unnamed x44 -> x62, local copies, waits for them, and re-layouts: 4.08 us -> 13.2 us
    ppermute x44, starting transfers between devices: 72.1 us -> 68.7 us  [moved(): return lax.ppermute(block, AXES, route)]
    select_n x4 -> x5, other arithmetic: 4.7 us -> 4.7 us  [by_week(): return lax.select_n(week, *choices)]
  transfers between devices with their start and end apart: 46 -> 46, of which waited for: 19 -> 21; matrix products, arithmetic and copies ran while one was open for 2% -> 3% of each run, Pallas kernels for 16% -> 14%
where the time goes in v3:
time: 230 us; the launch traced here: 229 us
  waiting for transfers between devices  89.5 us (39%)
  starting transfers between devices  68.8 us (30%)
  Pallas kernels  35.4 us (15%)
  between operations  14.5 us (6%)
  local copies, waits for them, and re-layouts  13.9 us (6%)
  other arithmetic  7.16 us (3%)
    ppermute x44, waiting for transfers between devices, moved(): return lax.ppermute(block, AXES, route)  85.4 us
    ppermute x44, starting transfers between devices, moved(): return lax.ppermute(block, AXES, route)  68.7 us
    unnamed x62, local copies, waits for them, and re-layouts  13.2 us
    pallas_call x1, Pallas kernels, band_products(): pl.pallas_call(kernel, grid=(regions // tile,), in_specs=[SMEM, VMEM, pl....  10.9 us
    pallas_call x1, Pallas kernels, coupling_and_parts(): pl.pallas_call(kernel, in_specs=[VMEM] * n_in, out_specs=[VMEM] * n_r, ou...  8.03 us
    pallas_call x1, Pallas kernels, finish_lag_0(): pl.pallas_call(kernel, grid=(regions // tile,), in_specs=[SMEM, VMEM, pl....  6.56 us
    select_n x5, other arithmetic, by_week(): return lax.select_n(week, *choices)  4.7 us
  transfers between devices with their start and end apart: 46, of which 21 were waited for; matrix products, arithmetic and copies ran while one was open for 3% of the time, Pallas kernels for 14%

profile of v3, /device:TPU:2, one launch (start us, length us, event | category | flops | bytes accessed | tf_op | source)
XLA Modules:
  0.0 229.2 jit_solution(9612463590949127644)
XLA Ops:
  7.3 1.2 select_bitcast_fusion
  10.8 4.0 %collective-permute-start = (bf16[2,1024,128]{2,1,0:T(8,128)(2,1)}, bf16[2,1024,128]{2,1,0:T(8,128)(2,1)S(1)}, u32[]{:S(2)}, u32[]{:S(2)}) collective-permute-start(bf16[2,1024,128]{2,1,0:T(8,128)(2,1)} %pad_maximum_fusion.1), channel_id=1, source_target_pairs={{32,96},{33,97},{34,98},{35,99},{36,100},{37,101},{38,102},{39,103... | collective-permute-start | bytes 1572872 | tf_op jit(solution)/shard_map/ppermute | solution.py:25
  14.9 1.9 collective-permute-start.8
  16.8 4.7 %collective-permute-start.9 = (bf16[2,1024,128]{2,1,0:T(8,128)(2,1)}, bf16[2,1024,128]{2,1,0:T(8,128)(2,1)}, u32[]{:S(2)}, u32[]{:S(2)}) collective-permute-start(bf16[2,1024,128]{2,1,0:T(8,128)(2,1)} %pad_maximum_fusion.1), channel_id=1, source_target_pairs={{32,64},{33,65},{34,66},{35,67},{36,68},{37,69},{38,70},{39,71},{4... | collective-permute-start | bytes 1572872 | tf_op jit(solution)/shard_map/ppermute | solution.py:25
  21.5 1.9 collective-permute-start.1
  23.4 3.6 %collective-permute-start.2 = (bf16[1024,128]{1,0:T(8,128)(2,1)S(1)}, bf16[1024,128]{1,0:T(8,128)(2,1)S(1)}, u32[]{:S(2)}, u32[]{:S(2)}) collective-permute-start(bf16[1024,128]{1,0:T(8,128)(2,1)S(1)} %copy-done.3), channel_id=1, source_target_pairs={{0,16},{1,17},{2,18},{3,19},{4,20},{5,21},{6,22},{7,23},{8,24},{9,... | collective-permute-start | bytes 786440 | tf_op jit(solution)/shard_map/ppermute | solution.py:25
  27.0 2.2 collective-permute-done
  29.3 4.0 %collective-permute-start.3 = (bf16[1024,128]{1,0:T(8,128)(2,1)S(1)}, bf16[1024,128]{1,0:T(8,128)(2,1)S(1)}, u32[]{:S(2)}, u32[]{:S(2)}) collective-permute-start(bf16[1024,128]{1,0:T(8,128)(2,1)S(1)} %copy-done.3), channel_id=1, source_target_pairs={{0,24},{1,25},{2,26},{3,27},{4,28},{5,29},{6,30},{7,31},{8,0},{9,1... | collective-permute-start | bytes 786440 | tf_op jit(solution)/shard_map/ppermute | solution.py:25
  33.3 6.0 %collective-permute-done.8 = bf16[2,1024,128]{2,1,0:T(8,128)(2,1)S(1)} collective-permute-done((bf16[2,1024,128]{2,1,0:T(8,128)(2,1)}, bf16[2,1024,128]{2,1,0:T(8,128)(2,1)S(1)}, u32[]{:S(2)}, u32[]{:S(2)}) %collective-permute-start.8) | collective-permute-done | bytes 524320 | tf_op jit(solution)/shard_map/ppermute | solution.py:25
  40.5 2.0 collective-permute-start.13
  43.5 3.3 %collective-permute-start.14 = (bf16[2,1024,128]{2,1,0:T(8,128)(2,1)S(1)}, bf16[2,1024,128]{2,1,0:T(8,128)(2,1)}, u32[]{:S(2)}, u32[]{:S(2)}) collective-permute-start(bf16[2,1024,128]{2,1,0:T(8,128)(2,1)S(1)} %pad_maximum_fusion.3.refs_12_), channel_id=1, source_target_pairs={{0,16},{1,17},{2,18},{3,19},{4,20},{5,21},{6,22},{7,23},{8,24},{9,... | collective-permute-start | bytes 1572872 | tf_op jit(solution)/shard_map/ppermute | solution.py:25
  49.2 1.6 collective-permute-start.10
  51.5 2.9 %collective-permute-start.11 = (bf16[2,1024,128]{2,1,0:T(8,128)(2,1)S(1)}, bf16[2,1024,128]{2,1,0:T(8,128)(2,1)S(1)}, u32[]{:S(2)}, u32[]{:S(2)}) collective-permute-start(bf16[2,1024,128]{2,1,0:T(8,128)(2,1)S(1)} %pad_maximum_fusion.2.refs_8_), channel_id=1, source_target_pairs={{0,4},{1,5},{2,6},{3,7},{4,0},{5,1},{6,2},{7,3},{8,12},{9,13},{10,... | collective-permute-start | bytes 1572872 | tf_op jit(solution)/shard_map/ppermute | solution.py:25
  54.4 3.4 %collective-permute-done.13.refs_13_ = bf16[2,1024,128]{2,1,0:T(8,128)(2,1)} collective-permute-done((bf16[2,1024,128]{2,1,0:T(8,128)(2,1)S(1)}, bf16[2,1024,128]{2,1,0:T(8,128)(2,1)}, u32[]{:S(2)}, u32[]{:S(2)}) %collective-permute-start.13) | collective-permute-done | bytes 524320 | tf_op jit(solution)/shard_map/ppermute | solution.py:25
  57.8 1.6 collective-permute-done.7.refs_7_
  60.1 2.7 %collective-permute-start.12 = (bf16[2,1024,128]{2,1,0:T(8,128)(2,1)S(1)}, bf16[2,1024,128]{2,1,0:T(8,128)(2,1)S(1)}, u32[]{:S(2)}, u32[]{:S(2)}) collective-permute-start(bf16[2,1024,128]{2,1,0:T(8,128)(2,1)S(1)} %pad_maximum_fusion.2.refs_8_), channel_id=1, source_target_pairs={{0,6},{1,7},{2,0},{3,1},{4,2},{5,3},{6,4},{7,5},{8,14},{9,15},{10,... | collective-permute-start | bytes 1572872 | tf_op jit(solution)/shard_map/ppermute | solution.py:25
  62.9 18.9 %collective-permute-done.14.refs_14_ = bf16[2,1024,128]{2,1,0:T(8,128)(2,1)} collective-permute-done((bf16[2,1024,128]{2,1,0:T(8,128)(2,1)S(1)}, bf16[2,1024,128]{2,1,0:T(8,128)(2,1)}, u32[]{:S(2)}, u32[]{:S(2)}) %collective-permute-start.14) | collective-permute-done | bytes 524320 | tf_op jit(solution)/shard_map/ppermute | solution.py:25
  82.4 5.5 %collective-permute-done.11.refs_10_ = bf16[2,1024,128]{2,1,0:T(8,128)(2,1)S(1)} collective-permute-done((bf16[2,1024,128]{2,1,0:T(8,128)(2,1)S(1)}, bf16[2,1024,128]{2,1,0:T(8,128)(2,1)S(1)}, u32[]{:S(2)}, u32[]{:S(2)}) %collective-permute-start.11) | collective-permute-done | bytes 524320 | tf_op jit(solution)/shard_map/ppermute | solution.py:25
  87.9 1.9 fusion.11.left_ref
  97.0 8.0 %coupling_and_parts.1 = (f32[128,1024]{1,0:T(8,128)S(1)}, bf16[128,1024]{1,0:T(8,128)(2,1)S(1)}, bf16[128,1024]{1,0:T(8,128)(2,1)S(1)}, bf16[128,1024]{1,0:T(8,128)(2,1)S(1)}) custom-call(bf16[1024,128]{1,0:T(8,128)(2,1)S(1)} %copy-done.3, bf16[1024,128]{1,0:T(8,128)(2,1)S(1)} %copy-done.6, bf16[1024,128]{1,0:T(8,128)(2,1)S(1)} %copy-done.8, ...), custom_call_target="tpu_custom_call" | custom-call | tf_op jit(solution)/shard_map/coupling_and_parts/pallas_call | solution.py:104
  107.2 3.9 %collective-permute-start.20 = (bf16[128,1024]{1,0:T(8,128)(2,1)}, bf16[128,1024]{1,0:T(8,128)(2,1)S(1)}, u32[]{:S(2)}, u32[]{:S(2)}) collective-permute-start(bf16[128,1024]{1,0:T(8,128)(2,1)} %copy-done.21), channel_id=1, source_target_pairs={{0,6},{1,7},{2,0},{3,1},{4,2},{5,3},{6,4},{7,5},{8,14},{9,15},{10,... | collective-permute-start | bytes 786440 | tf_op jit(solution)/shard_map/ppermute | solution.py:25
  112.5 7.6 %collective-permute-done.20 = bf16[128,1024]{1,0:T(8,128)(2,1)S(1)} collective-permute-done((bf16[128,1024]{1,0:T(8,128)(2,1)}, bf16[128,1024]{1,0:T(8,128)(2,1)S(1)}, u32[]{:S(2)}, u32[]{:S(2)}) %collective-permute-start.20) | collective-permute-done | bytes 262176 | tf_op jit(solution)/shard_map/ppermute | solution.py:25
  120.1 2.0 collective-permute-done.21
  122.1 4.1 %collective-permute-done.22 = bf16[128,1024]{1,0:T(8,128)(2,1)S(1)} collective-permute-done((bf16[128,1024]{1,0:T(8,128)(2,1)}, bf16[128,1024]{1,0:T(8,128)(2,1)S(1)}, u32[]{:S(2)}, u32[]{:S(2)}) %collective-permute-start.22) | collective-permute-done | bytes 262176 | tf_op jit(solution)/shard_map/ppermute | solution.py:25
  127.4 2.6 %collective-permute-start.28 = (bf16[128,1024]{1,0:T(8,128)(2,1)S(1)}, bf16[128,1024]{1,0:T(8,128)(2,1)S(1)}, u32[]{:S(2)}, u32[]{:S(2)}) collective-permute-start(bf16[128,1024]{1,0:T(8,128)(2,1)S(1)} %add_convert_fusion.refs_1_.refs_5_), channel_id=1, source_target_pairs={{0,24},{1,25},{2,26},{3,27},{4,28},{5,29},{6,30},{7,31},{8,0},{9,1... | collective-permute-start | bytes 786440 | tf_op jit(solution)/shard_map/ppermute | solution.py:25
  130.5 3.1 %collective-permute-start.24 = (bf16[128,1024]{1,0:T(8,128)(2,1)S(1)}, bf16[128,1024]{1,0:T(8,128)(2,1)S(1)}, u32[]{:S(2)}, u32[]{:S(2)}) collective-permute-start(bf16[128,1024]{1,0:T(8,128)(2,1)S(1)} %add_convert_fusion.refs_1_.refs_5_), channel_id=1, source_target_pairs={{0,4},{1,5},{2,6},{3,7},{4,0},{5,1},{6,2},{7,3},{8,12},{9,13},{10,... | collective-permute-start | bytes 786440 | tf_op jit(solution)/shard_map/ppermute | solution.py:25
  133.7 7.8 %collective-permute-done.26.refs_6_ = bf16[128,1024]{1,0:T(8,128)(2,1)S(1)} collective-permute-done((bf16[128,1024]{1,0:T(8,128)(2,1)S(1)}, bf16[128,1024]{1,0:T(8,128)(2,1)S(1)}, u32[]{:S(2)}, u32[]{:S(2)}) %collective-permute-start.26) | collective-permute-done | bytes 262176 | tf_op jit(solution)/shard_map/ppermute | solution.py:25
  141.5 1.7 collective-permute-start.25
  144.0 2.1 collective-permute-done.24.refs_3_
  146.2 4.3 %collective-permute-done.25.refs_4_ = bf16[128,1024]{1,0:T(8,128)(2,1)S(1)} collective-permute-done((bf16[128,1024]{1,0:T(8,128)(2,1)S(1)}, bf16[128,1024]{1,0:T(8,128)(2,1)S(1)}, u32[]{:S(2)}, u32[]{:S(2)}) %collective-permute-start.25) | collective-permute-done | bytes 262176 | tf_op jit(solution)/shard_map/ppermute | solution.py:25
  150.5 2.6 %gram_terms.1 = (f32[512,256]{1,0:T(8,128)S(1)}, bf16[512,256]{1,0:T(8,128)(2,1)}, bf16[512,256]{1,0:T(8,128)(2,1)}, bf16[512,256]{1,0:T(8,128)(2,1)}) custom-call(s32[1]{0:T(128)} %bitcast.7.refs_0_, bf16[128,1024]{1,0:T(8,128)(2,1)S(1)} %add_convert_fusion.refs_1_.refs_5_, bf16[128,1024]{1,0:T(8,128)(2,1)S(1)} %collective-permute-done.23.refs_2_, ...), custom_call_target="tpu_custom_call" | custom-call | tf_op jit(solution)/shard_map/gram_terms/pallas_call | solution.py:144
  153.2 2.9 %collective-permute-start.34 = (bf16[512,256]{1,0:T(8,128)(2,1)}, bf16[512,256]{1,0:T(8,128)(2,1)}, u32[]{:S(2)}, u32[]{:S(2)}) collective-permute-start(bf16[512,256]{1,0:T(8,128)(2,1)} %get-tuple-element.41), channel_id=1, source_target_pairs={{0,64},{1,65},{2,66},{3,67},{4,68},{5,69},{6,70},{7,71},{8,72},{9,... | collective-permute-start | bytes 786440 | tf_op jit(solution)/shard_map/ppermute | solution.py:25
  156.9 10.9 %band_products.1 = (f32[3,128,4096]{2,1,0:T(8,128)}, bf16[128,4096]{1,0:T(8,128)(2,1)S(1)}, bf16[128,4096]{1,0:T(8,128)(2,1)S(1)}) custom-call(s32[1]{0:T(128)} %bitcast.8.week_ref, bf16[1024,512]{1,0:T(8,128)(2,1)S(1)} %pad_maximum_fusion.left_ref, bf16[2,1024,4096]{2,1,0:T(8,128)(2,1)} %all-gather.5.cloned.1.call-done.wide_ref), custom_call_target="tpu_custom_call" | custom-call | tf_op jit(solution)/shard_map/band_products/pallas_call | solution.py:203
  167.9 3.5 %collective-permute-start.39 = (bf16[128,4096]{1,0:T(8,128)(2,1)S(1)}, bf16[128,4096]{1,0:T(8,128)(2,1)S(1)}, u32[]{:S(2)}, u32[]{:S(2)}) collective-permute-start(bf16[128,4096]{1,0:T(8,128)(2,1)S(1)} %get-tuple-element.51), channel_id=1, source_target_pairs={{32,0},{33,1},{34,2},{35,3},{36,4},{37,5},{38,6},{39,7},{40,8},{41... | collective-permute-start | bytes 3145736 | tf_op jit(solution)/shard_map/ppermute | solution.py:25
  171.3 2.1 week_sum.1
  173.4 1.3 collective-permute-start.40
  174.7 3.9 %collective-permute-start.36 = (bf16[128,256]{1,0:T(8,128)(2,1)}, bf16[128,256]{1,0:T(8,128)(2,1)S(1)}, u32[]{:S(2)}, u32[]{:S(2)}) collective-permute-start(bf16[128,256]{1,0:T(8,128)(2,1)} %get-tuple-element.44), channel_id=1, source_target_pairs={{0,6},{1,7},{2,0},{3,1},{4,2},{5,3},{6,4},{7,5},{8,14},{9,15},{10,... | collective-permute-start | bytes 196616 | tf_op jit(solution)/shard_map/ppermute | solution.py:25
  179.7 2.0 collective-permute-done.36.refs_4_
  181.7 4.4 %collective-permute-done.37.refs_5_ = bf16[128,256]{1,0:T(8,128)(2,1)} collective-permute-done((bf16[128,256]{1,0:T(8,128)(2,1)}, bf16[128,256]{1,0:T(8,128)(2,1)}, u32[]{:S(2)}, u32[]{:S(2)}) %collective-permute-start.37) | collective-permute-done | bytes 65568 | tf_op jit(solution)/shard_map/ppermute | solution.py:25
  186.2 4.0 %all-gather.3.cloned.1.call-done.wide_ref = bf16[1024,4096]{1,0:T(8,128)(2,1)} async-done(((bf16[1024,128]{1,0:T(8,128)(2,1)}), bf16[1024,4096]{1,0:T(8,128)(2,1)}) %all-gather.3.cloned.1.call-update) | async-done | bytes 8388624 | tf_op jit(solution)/shard_map/all_gather | solution.py:374
  190.3 5.6 %collective-permute-done.39.arrived_ref = bf16[128,4096]{1,0:T(8,128)(2,1)S(1)} collective-permute-done((bf16[128,4096]{1,0:T(8,128)(2,1)S(1)}, bf16[128,4096]{1,0:T(8,128)(2,1)S(1)}, u32[]{:S(2)}, u32[]{:S(2)}) %collective-permute-start.39) | collective-permute-done | bytes 1048608 | tf_op jit(solution)/shard_map/ppermute | solution.py:25
  195.9 6.6 %finish_lag_0.1 = (f32[3,128,4096]{2,1,0:T(8,128)}, bf16[128,1024]{1,0:T(8,128)(2,1)S(1)}, bf16[128,1024]{1,0:T(8,128)(2,1)S(1)}, bf16[128,1024]{1,0:T(8,128)(2,1)S(1)}, bf16[128,1024]{1,0:T(8,128)(2,1)S(1)}) custom-call(s32[1]{0:T(128)} %bitcast.first_ref, bf16[1024,128]{1,0:T(8,128)(2,1)S(1)} %copy-done, ...), custom_call_target="tpu_custom_call", output_to_operand_aliasing={{0}: (3, {})} | custom-call | tf_op jit(solution)/shard_map/finish_lag_0/pallas_call | solution.py:273
  203.1 3.6 %collective-permute-start.41 = (bf16[128,1024]{1,0:T(8,128)(2,1)S(1)}, bf16[128,1024]{1,0:T(8,128)(2,1)S(1)}, u32[]{:S(2)}, u32[]{:S(2)}) collective-permute-start(bf16[128,1024]{1,0:T(8,128)(2,1)S(1)} %get-tuple-element.56), channel_id=1, source_target_pairs={{32,64},{33,65},{34,66},{35,67},{36,68},{37,69},{38,70},{39,71},{4... | collective-permute-start | bytes 786440 | tf_op jit(solution)/shard_map/ppermute | solution.py:25
  206.8 1.3 collective-permute-start.42
  208.1 1.3 collective-permute-start.43
  210.1 6.2 %collective-permute-done.40.arrived_ref = bf16[128,4096]{1,0:T(8,128)(2,1)} collective-permute-done((bf16[128,4096]{1,0:T(8,128)(2,1)S(1)}, bf16[128,4096]{1,0:T(8,128)(2,1)}, u32[]{:S(2)}, u32[]{:S(2)}) %collective-permute-start.40) | collective-permute-done | bytes 1048608 | tf_op jit(solution)/shard_map/ppermute | solution.py:25
  216.3 2.9 %add_lag_1.1 = f32[3,128,4096]{2,1,0:T(8,128)} custom-call(f32[3,128,4096]{2,1,0:T(8,128)} %get-tuple-element.52.band_ref, bf16[128,4096]{1,0:T(8,128)(2,1)} %collective-permute-done.40.arrived_ref), custom_call_target="tpu_custom_call", output_to_operand_aliasing={{}: (0, {})} | custom-call | tf_op jit(solution)/shard_map/add_lag_1/pallas_call | solution.py:231
  220.1 2.3 %place_schur.1 = f32[128,1024]{1,0:T(8,128)} custom-call(s32[8]{0:T(128)} %stack.58.ys_ref, s32[1]{0:T(128)} %bitcast.8.week_ref, bf16[128,1024]{1,0:T(8,128)(2,1)} %copy-done.4, bf16[128,1024]{1,0:T(8,128)(2,1)} %copy-done.24, bf16[128,1024]{1,0:T(8,128)(2,1)} %copy-done.25, bf16[128,1024]{1,0:T(8,128)(2,1)} %copy-done.26, ...), custom_call_target="tpu_custom_call" | custom-call | tf_op jit(solution)/shard_map/place_schur/pallas_call | solution.py:309
  (130 shorter events, 26.6 us)
Async XLA Ops:
  7.2 149.7 %all-gather.5.cloned.1.call-start = ((), (), s32[]{:S(2)}) async-start(), calls=%async_computation.1 | async-start | bytes 17301504 | tf_op jit(solution)/shard_map/all_gather | solution.py:349
  9.3 180.9 %all-gather.3.cloned.1.call-start = ((), (), s32[]{:S(2)}) async-start(), calls=%async_computation | async-start | bytes 8650752 | tf_op jit(solution)/shard_map/all_gather | solution.py:374
  10.8 18.4 %collective-permute-start = (bf16[2,1024,128]{2,1,0:T(8,128)(2,1)}, bf16[2,1024,128]{2,1,0:T(8,128)(2,1)S(1)}, u32[]{:S(2)}, u32[]{:S(2)}) collective-permute-start(bf16[2,1024,128]{2,1,0:T(8,128)(2,1)} %pad_maximum_fusion.1), channel_id=1, source_target_pairs={{32,96},{33,97},{34,98},{35,99},{36,100},{37,101},{38,102},{39,103... | collective-permute-start | bytes 1572872 | tf_op jit(solution)/shard_map/ppermute | solution.py:25
  14.9 24.5 %collective-permute-start.8 = (bf16[2,1024,128]{2,1,0:T(8,128)(2,1)}, bf16[2,1024,128]{2,1,0:T(8,128)(2,1)S(1)}, u32[]{:S(2)}, u32[]{:S(2)}) collective-permute-start(bf16[2,1024,128]{2,1,0:T(8,128)(2,1)} %pad_maximum_fusion.1), channel_id=1, source_target_pairs={{32,0},{33,1},{34,2},{35,3},{36,4},{37,5},{38,6},{39,7},{40,8},{41... | collective-permute-start | bytes 1572872 | tf_op jit(solution)/shard_map/ppermute | solution.py:25
  16.8 22.5 %collective-permute-start.9 = (bf16[2,1024,128]{2,1,0:T(8,128)(2,1)}, bf16[2,1024,128]{2,1,0:T(8,128)(2,1)}, u32[]{:S(2)}, u32[]{:S(2)}) collective-permute-start(bf16[2,1024,128]{2,1,0:T(8,128)(2,1)} %pad_maximum_fusion.1), channel_id=1, source_target_pairs={{32,64},{33,65},{34,66},{35,67},{36,68},{37,69},{38,70},{39,71},{4... | collective-permute-start | bytes 1572872 | tf_op jit(solution)/shard_map/ppermute | solution.py:25
  21.5 21.0 %collective-permute-start.1 = (bf16[1024,128]{1,0:T(8,128)(2,1)S(1)}, bf16[1024,128]{1,0:T(8,128)(2,1)S(1)}, u32[]{:S(2)}, u32[]{:S(2)}) collective-permute-start(bf16[1024,128]{1,0:T(8,128)(2,1)S(1)} %copy-done.3), channel_id=1, source_target_pairs={{0,8},{1,9},{2,10},{3,11},{4,12},{5,13},{6,14},{7,15},{8,16},{9,17... | collective-permute-start | bytes 786440 | tf_op jit(solution)/shard_map/ppermute | solution.py:25
  23.4 20.0 %collective-permute-start.2 = (bf16[1024,128]{1,0:T(8,128)(2,1)S(1)}, bf16[1024,128]{1,0:T(8,128)(2,1)S(1)}, u32[]{:S(2)}, u32[]{:S(2)}) collective-permute-start(bf16[1024,128]{1,0:T(8,128)(2,1)S(1)} %copy-done.3), channel_id=1, source_target_pairs={{0,16},{1,17},{2,18},{3,19},{4,20},{5,21},{6,22},{7,23},{8,24},{9,... | collective-permute-start | bytes 786440 | tf_op jit(solution)/shard_map/ppermute | solution.py:25
  29.3 14.2 %collective-permute-start.3 = (bf16[1024,128]{1,0:T(8,128)(2,1)S(1)}, bf16[1024,128]{1,0:T(8,128)(2,1)S(1)}, u32[]{:S(2)}, u32[]{:S(2)}) collective-permute-start(bf16[1024,128]{1,0:T(8,128)(2,1)S(1)} %copy-done.3), channel_id=1, source_target_pairs={{0,24},{1,25},{2,26},{3,27},{4,28},{5,29},{6,30},{7,31},{8,0},{9,1... | collective-permute-start | bytes 786440 | tf_op jit(solution)/shard_map/ppermute | solution.py:25
  40.5 17.3 %collective-permute-start.13 = (bf16[2,1024,128]{2,1,0:T(8,128)(2,1)S(1)}, bf16[2,1024,128]{2,1,0:T(8,128)(2,1)}, u32[]{:S(2)}, u32[]{:S(2)}) collective-permute-start(bf16[2,1024,128]{2,1,0:T(8,128)(2,1)S(1)} %pad_maximum_fusion.3.refs_12_), channel_id=1, source_target_pairs={{0,8},{1,9},{2,10},{3,11},{4,12},{5,13},{6,14},{7,15},{8,16},{9,17... | collective-permute-start | bytes 1572872 | tf_op jit(solution)/shard_map/ppermute | solution.py:25
  42.5 4.3 %collective-permute-start.4 = (bf16[1024,128]{1,0:T(8,128)(2,1)S(1)}, bf16[1024,128]{1,0:T(8,128)(2,1)S(1)}, u32[]{:S(2)}, u32[]{:S(2)}) collective-permute-start(bf16[1024,128]{1,0:T(8,128)(2,1)S(1)} %copy-done.3), channel_id=1, source_target_pairs={{0,1},{1,0},{2,3},{3,2},{4,5},{5,4},{6,7},{7,6},{8,9},{9,8},{10,11... | collective-permute-start | bytes 786440 | tf_op jit(solution)/shard_map/ppermute | solution.py:25
  42.5 6.0 %collective-permute-start.5 = (bf16[1024,128]{1,0:T(8,128)(2,1)S(1)}, bf16[1024,128]{1,0:T(8,128)(2,1)S(1)}, u32[]{:S(2)}, u32[]{:S(2)}) collective-permute-start(bf16[1024,128]{1,0:T(8,128)(2,1)S(1)} %collective-permute-done.1.refs_1_), channel_id=1, source_target_pairs={{0,1},{1,0},{2,3},{3,2},{4,5},{5,4},{6,7},{7,6},{8,9},{9,8},{10,11... | collective-permute-start | bytes 786440 | tf_op jit(solution)/shard_map/ppermute | solution.py:25
  43.5 7.4 %collective-permute-start.6 = (bf16[1024,128]{1,0:T(8,128)(2,1)S(1)}, bf16[1024,128]{1,0:T(8,128)(2,1)S(1)}, u32[]{:S(2)}, u32[]{:S(2)}) collective-permute-start(bf16[1024,128]{1,0:T(8,128)(2,1)S(1)} %collective-permute-done.2.refs_2_), channel_id=1, source_target_pairs={{0,1},{1,0},{2,3},{3,2},{4,5},{5,4},{6,7},{7,6},{8,9},{9,8},{10,11... | collective-permute-start | bytes 786440 | tf_op jit(solution)/shard_map/ppermute | solution.py:25
  43.5 38.3 %collective-permute-start.14 = (bf16[2,1024,128]{2,1,0:T(8,128)(2,1)S(1)}, bf16[2,1024,128]{2,1,0:T(8,128)(2,1)}, u32[]{:S(2)}, u32[]{:S(2)}) collective-permute-start(bf16[2,1024,128]{2,1,0:T(8,128)(2,1)S(1)} %pad_maximum_fusion.3.refs_12_), channel_id=1, source_target_pairs={{0,16},{1,17},{2,18},{3,19},{4,20},{5,21},{6,22},{7,23},{8,24},{9,... | collective-permute-start | bytes 1572872 | tf_op jit(solution)/shard_map/ppermute | solution.py:25
  47.5 34.3 %collective-permute-start.15 = (bf16[2,1024,128]{2,1,0:T(8,128)(2,1)S(1)}, bf16[2,1024,128]{2,1,0:T(8,128)(2,1)}, u32[]{:S(2)}, u32[]{:S(2)}) collective-permute-start(bf16[2,1024,128]{2,1,0:T(8,128)(2,1)S(1)} %pad_maximum_fusion.3.refs_12_), channel_id=1, source_target_pairs={{0,24},{1,25},{2,26},{3,27},{4,28},{5,29},{6,30},{7,31},{8,0},{9,1... | collective-permute-start | bytes 1572872 | tf_op jit(solution)/shard_map/ppermute | solution.py:25
  49.2 33.1 %collective-permute-start.10 = (bf16[2,1024,128]{2,1,0:T(8,128)(2,1)S(1)}, bf16[2,1024,128]{2,1,0:T(8,128)(2,1)S(1)}, u32[]{:S(2)}, u32[]{:S(2)}) collective-permute-start(bf16[2,1024,128]{2,1,0:T(8,128)(2,1)S(1)} %pad_maximum_fusion.2.refs_8_), channel_id=1, source_target_pairs={{0,2},{1,3},{2,4},{3,5},{4,6},{5,7},{6,0},{7,1},{8,10},{9,11},{10,... | collective-permute-start | bytes 1572872 | tf_op jit(solution)/shard_map/ppermute | solution.py:25
  51.5 36.4 %collective-permute-start.11 = (bf16[2,1024,128]{2,1,0:T(8,128)(2,1)S(1)}, bf16[2,1024,128]{2,1,0:T(8,128)(2,1)S(1)}, u32[]{:S(2)}, u32[]{:S(2)}) collective-permute-start(bf16[2,1024,128]{2,1,0:T(8,128)(2,1)S(1)} %pad_maximum_fusion.2.refs_8_), channel_id=1, source_target_pairs={{0,4},{1,5},{2,6},{3,7},{4,0},{5,1},{6,2},{7,3},{8,12},{9,13},{10,... | collective-permute-start | bytes 1572872 | tf_op jit(solution)/shard_map/ppermute | solution.py:25
  57.8 1.6 collective-permute-start.7
  60.1 30.2 %collective-permute-start.12 = (bf16[2,1024,128]{2,1,0:T(8,128)(2,1)S(1)}, bf16[2,1024,128]{2,1,0:T(8,128)(2,1)S(1)}, u32[]{:S(2)}, u32[]{:S(2)}) collective-permute-start(bf16[2,1024,128]{2,1,0:T(8,128)(2,1)S(1)} %pad_maximum_fusion.2.refs_8_), channel_id=1, source_target_pairs={{0,6},{1,7},{2,0},{3,1},{4,2},{5,3},{6,4},{7,5},{8,14},{9,15},{10,... | collective-permute-start | bytes 1572872 | tf_op jit(solution)/shard_map/ppermute | solution.py:25
  81.8 8.5 %collective-permute-start.16 = (bf16[2,1024,128]{2,1,0:T(8,128)(2,1)S(1)}, bf16[2,1024,128]{2,1,0:T(8,128)(2,1)}, u32[]{:S(2)}, u32[]{:S(2)}) collective-permute-start(bf16[2,1024,128]{2,1,0:T(8,128)(2,1)S(1)} %pad_maximum_fusion.3.refs_12_), channel_id=1, source_target_pairs={{0,1},{1,0},{2,3},{3,2},{4,5},{5,4},{6,7},{7,6},{8,9},{9,8},{10,11... | collective-permute-start | bytes 1572872 | tf_op jit(solution)/shard_map/ppermute | solution.py:25
  81.8 8.5 %collective-permute-start.17 = (bf16[2,1024,128]{2,1,0:T(8,128)(2,1)}, bf16[2,1024,128]{2,1,0:T(8,128)(2,1)}, u32[]{:S(2)}, u32[]{:S(2)}) collective-permute-start(bf16[2,1024,128]{2,1,0:T(8,128)(2,1)} %collective-permute-done.13.refs_13_), channel_id=1, source_target_pairs={{0,1},{1,0},{2,3},{3,2},{4,5},{5,4},{6,7},{7,6},{8,9},{9,8},{10,11... | collective-permute-start | bytes 1572872 | tf_op jit(solution)/shard_map/ppermute | solution.py:25
  82.3 8.0 %collective-permute-start.18 = (bf16[2,1024,128]{2,1,0:T(8,128)(2,1)}, bf16[2,1024,128]{2,1,0:T(8,128)(2,1)}, u32[]{:S(2)}, u32[]{:S(2)}) collective-permute-start(bf16[2,1024,128]{2,1,0:T(8,128)(2,1)} %collective-permute-done.14.refs_14_), channel_id=1, source_target_pairs={{0,1},{1,0},{2,3},{3,2},{4,5},{5,4},{6,7},{7,6},{8,9},{9,8},{10,11... | collective-permute-start | bytes 1572872 | tf_op jit(solution)/shard_map/ppermute | solution.py:25
  87.9 2.4 %collective-permute-start.19 = (bf16[2,1024,128]{2,1,0:T(8,128)(2,1)}, bf16[2,1024,128]{2,1,0:T(8,128)(2,1)}, u32[]{:S(2)}, u32[]{:S(2)}) collective-permute-start(bf16[2,1024,128]{2,1,0:T(8,128)(2,1)} %collective-permute-done.15.refs_15_), channel_id=1, source_target_pairs={{0,1},{1,0},{2,3},{3,2},{4,5},{5,4},{6,7},{7,6},{8,9},{9,8},{10,11... | collective-permute-start | bytes 1572872 | tf_op jit(solution)/shard_map/ppermute | solution.py:25
  107.2 12.9 %collective-permute-start.20 = (bf16[128,1024]{1,0:T(8,128)(2,1)}, bf16[128,1024]{1,0:T(8,128)(2,1)S(1)}, u32[]{:S(2)}, u32[]{:S(2)}) collective-permute-start(bf16[128,1024]{1,0:T(8,128)(2,1)} %copy-done.21), channel_id=1, source_target_pairs={{0,6},{1,7},{2,0},{3,1},{4,2},{5,3},{6,4},{7,5},{8,14},{9,15},{10,... | collective-permute-start | bytes 786440 | tf_op jit(solution)/shard_map/ppermute | solution.py:25
  111.1 11.0 %collective-permute-start.21 = (bf16[128,1024]{1,0:T(8,128)(2,1)}, bf16[128,1024]{1,0:T(8,128)(2,1)S(1)}, u32[]{:S(2)}, u32[]{:S(2)}) collective-permute-start(bf16[128,1024]{1,0:T(8,128)(2,1)} %copy-done.20), channel_id=1, source_target_pairs={{0,4},{1,5},{2,6},{3,7},{4,0},{5,1},{6,2},{7,3},{8,12},{9,13},{10,... | collective-permute-start | bytes 786440 | tf_op jit(solution)/shard_map/ppermute | solution.py:25
  111.9 14.3 %collective-permute-start.22 = (bf16[128,1024]{1,0:T(8,128)(2,1)}, bf16[128,1024]{1,0:T(8,128)(2,1)S(1)}, u32[]{:S(2)}, u32[]{:S(2)}) collective-permute-start(bf16[128,1024]{1,0:T(8,128)(2,1)} %copy-done.19), channel_id=1, source_target_pairs={{0,2},{1,3},{2,4},{3,5},{4,6},{5,7},{6,0},{7,1},{8,10},{9,11},{10,... | collective-permute-start | bytes 786440 | tf_op jit(solution)/shard_map/ppermute | solution.py:25
  126.4 30.4 %copy-start.1 = (bf16[128,1024]{1,0:T(8,128)(2,1)}, bf16[128,1024]{1,0:T(8,128)(2,1)S(1)}, u32[]{:S(2)}) copy-start(bf16[128,1024]{1,0:T(8,128)(2,1)S(1)} %add_convert_fusion.refs_1_.refs_5_) | copy-start | bytes 786436
  126.4 15.1 %collective-permute-start.26 = (bf16[128,1024]{1,0:T(8,128)(2,1)S(1)}, bf16[128,1024]{1,0:T(8,128)(2,1)S(1)}, u32[]{:S(2)}, u32[]{:S(2)}) collective-permute-start(bf16[128,1024]{1,0:T(8,128)(2,1)S(1)} %add_convert_fusion.refs_1_.refs_5_), channel_id=1, source_target_pairs={{0,8},{1,9},{2,10},{3,11},{4,12},{5,13},{6,14},{7,15},{8,16},{9,17... | collective-permute-start | bytes 786440 | tf_op jit(solution)/shard_map/ppermute | solution.py:25
  127.2 16.0 %collective-permute-start.27 = (bf16[128,1024]{1,0:T(8,128)(2,1)S(1)}, bf16[128,1024]{1,0:T(8,128)(2,1)S(1)}, u32[]{:S(2)}, u32[]{:S(2)}) collective-permute-start(bf16[128,1024]{1,0:T(8,128)(2,1)S(1)} %add_convert_fusion.refs_1_.refs_5_), channel_id=1, source_target_pairs={{0,16},{1,17},{2,18},{3,19},{4,20},{5,21},{6,22},{7,23},{8,24},{9,... | collective-permute-start | bytes 786440 | tf_op jit(solution)/shard_map/ppermute | solution.py:25
  127.4 16.2 %collective-permute-start.28 = (bf16[128,1024]{1,0:T(8,128)(2,1)S(1)}, bf16[128,1024]{1,0:T(8,128)(2,1)S(1)}, u32[]{:S(2)}, u32[]{:S(2)}) collective-permute-start(bf16[128,1024]{1,0:T(8,128)(2,1)S(1)} %add_convert_fusion.refs_1_.refs_5_), channel_id=1, source_target_pairs={{0,24},{1,25},{2,26},{3,27},{4,28},{5,29},{6,30},{7,31},{8,0},{9,1... | collective-permute-start | bytes 786440 | tf_op jit(solution)/shard_map/ppermute | solution.py:25
  130.0 13.8 %collective-permute-start.23 = (bf16[128,1024]{1,0:T(8,128)(2,1)S(1)}, bf16[128,1024]{1,0:T(8,128)(2,1)S(1)}, u32[]{:S(2)}, u32[]{:S(2)}) collective-permute-start(bf16[128,1024]{1,0:T(8,128)(2,1)S(1)} %add_convert_fusion.refs_1_.refs_5_), channel_id=1, source_target_pairs={{0,2},{1,3},{2,4},{3,5},{4,6},{5,7},{6,0},{7,1},{8,10},{9,11},{10,... | collective-permute-start | bytes 786440 | tf_op jit(solution)/shard_map/ppermute | solution.py:25
  130.5 15.6 %collective-permute-start.24 = (bf16[128,1024]{1,0:T(8,128)(2,1)S(1)}, bf16[128,1024]{1,0:T(8,128)(2,1)S(1)}, u32[]{:S(2)}, u32[]{:S(2)}) collective-permute-start(bf16[128,1024]{1,0:T(8,128)(2,1)S(1)} %add_convert_fusion.refs_1_.refs_5_), channel_id=1, source_target_pairs={{0,4},{1,5},{2,6},{3,7},{4,0},{5,1},{6,2},{7,3},{8,12},{9,13},{10,... | collective-permute-start | bytes 786440 | tf_op jit(solution)/shard_map/ppermute | solution.py:25
  141.5 9.0 %collective-permute-start.25 = (bf16[128,1024]{1,0:T(8,128)(2,1)S(1)}, bf16[128,1024]{1,0:T(8,128)(2,1)S(1)}, u32[]{:S(2)}, u32[]{:S(2)}) collective-permute-start(bf16[128,1024]{1,0:T(8,128)(2,1)S(1)} %add_convert_fusion.refs_1_.refs_5_), channel_id=1, source_target_pairs={{0,6},{1,7},{2,0},{3,1},{4,2},{5,3},{6,4},{7,5},{8,14},{9,15},{10,... | collective-permute-start | bytes 786440 | tf_op jit(solution)/shard_map/ppermute | solution.py:25
  143.2 7.3 %collective-permute-start.29 = (bf16[128,1024]{1,0:T(8,128)(2,1)S(1)}, bf16[128,1024]{1,0:T(8,128)(2,1)S(1)}, u32[]{:S(2)}, u32[]{:S(2)}) collective-permute-start(bf16[128,1024]{1,0:T(8,128)(2,1)S(1)} %add_convert_fusion.refs_1_.refs_5_), channel_id=1, source_target_pairs={{0,1},{1,0},{2,3},{3,2},{4,5},{5,4},{6,7},{7,6},{8,9},{9,8},{10,11... | collective-permute-start | bytes 786440 | tf_op jit(solution)/shard_map/ppermute | solution.py:25
  143.5 7.0 %collective-permute-start.30 = (bf16[128,1024]{1,0:T(8,128)(2,1)S(1)}, bf16[128,1024]{1,0:T(8,128)(2,1)S(1)}, u32[]{:S(2)}, u32[]{:S(2)}) collective-permute-start(bf16[128,1024]{1,0:T(8,128)(2,1)S(1)} %collective-permute-done.26.refs_6_), channel_id=1, source_target_pairs={{0,1},{1,0},{2,3},{3,2},{4,5},{5,4},{6,7},{7,6},{8,9},{9,8},{10,11... | collective-permute-start | bytes 786440 | tf_op jit(solution)/shard_map/ppermute | solution.py:25
  143.7 6.8 %collective-permute-start.31 = (bf16[128,1024]{1,0:T(8,128)(2,1)S(1)}, bf16[128,1024]{1,0:T(8,128)(2,1)S(1)}, u32[]{:S(2)}, u32[]{:S(2)}) collective-permute-start(bf16[128,1024]{1,0:T(8,128)(2,1)S(1)} %collective-permute-done.27.refs_7_), channel_id=1, source_target_pairs={{0,1},{1,0},{2,3},{3,2},{4,5},{5,4},{6,7},{7,6},{8,9},{9,8},{10,11... | collective-permute-start | bytes 786440 | tf_op jit(solution)/shard_map/ppermute | solution.py:25
  146.2 4.3 %collective-permute-start.32 = (bf16[128,1024]{1,0:T(8,128)(2,1)S(1)}, bf16[128,1024]{1,0:T(8,128)(2,1)S(1)}, u32[]{:S(2)}, u32[]{:S(2)}) collective-permute-start(bf16[128,1024]{1,0:T(8,128)(2,1)S(1)} %collective-permute-done.28.refs_8_), channel_id=1, source_target_pairs={{0,1},{1,0},{2,3},{3,2},{4,5},{5,4},{6,7},{7,6},{8,9},{9,8},{10,11... | collective-permute-start | bytes 786440 | tf_op jit(solution)/shard_map/ppermute | solution.py:25
  153.1 14.7 %collective-permute-start.33 = (bf16[512,256]{1,0:T(8,128)(2,1)}, bf16[512,256]{1,0:T(8,128)(2,1)}, u32[]{:S(2)}, u32[]{:S(2)}) collective-permute-start(bf16[512,256]{1,0:T(8,128)(2,1)} %get-tuple-element.40), channel_id=1, source_target_pairs={{0,32},{1,33},{2,34},{3,35},{4,36},{5,37},{6,38},{7,39},{8,40},{9,... | collective-permute-start | bytes 786440 | tf_op jit(solution)/shard_map/ppermute | solution.py:25
  153.2 14.7 %collective-permute-start.34 = (bf16[512,256]{1,0:T(8,128)(2,1)}, bf16[512,256]{1,0:T(8,128)(2,1)}, u32[]{:S(2)}, u32[]{:S(2)}) collective-permute-start(bf16[512,256]{1,0:T(8,128)(2,1)} %get-tuple-element.41), channel_id=1, source_target_pairs={{0,64},{1,65},{2,66},{3,67},{4,68},{5,69},{6,70},{7,71},{8,72},{9,... | collective-permute-start | bytes 786440 | tf_op jit(solution)/shard_map/ppermute | solution.py:25
  156.1 11.8 %collective-permute-start.35 = (bf16[512,256]{1,0:T(8,128)(2,1)}, bf16[512,256]{1,0:T(8,128)(2,1)}, u32[]{:S(2)}, u32[]{:S(2)}) collective-permute-start(bf16[512,256]{1,0:T(8,128)(2,1)} %get-tuple-element.42), channel_id=1, source_target_pairs={{0,96},{1,97},{2,98},{3,99},{4,100},{5,101},{6,102},{7,103},{8,104... | collective-permute-start | bytes 786440 | tf_op jit(solution)/shard_map/ppermute | solution.py:25
  156.9 38.9 %copy-start = (bf16[1024,128]{1,0:T(8,128)(2,1)S(1)}, bf16[1024,128]{1,0:T(8,128)(2,1)}, u32[]{:S(2)}) copy-start(bf16[1024,128]{1,0:T(8,128)(2,1)} %fusion.11.left_ref) | copy-start | bytes 786436
  167.9 28.0 %collective-permute-start.39 = (bf16[128,4096]{1,0:T(8,128)(2,1)S(1)}, bf16[128,4096]{1,0:T(8,128)(2,1)S(1)}, u32[]{:S(2)}, u32[]{:S(2)}) collective-permute-start(bf16[128,4096]{1,0:T(8,128)(2,1)S(1)} %get-tuple-element.51), channel_id=1, source_target_pairs={{32,0},{33,1},{34,2},{35,3},{36,4},{37,5},{38,6},{39,7},{40,8},{41... | collective-permute-start | bytes 3145736 | tf_op jit(solution)/shard_map/ppermute | solution.py:25
  173.4 42.9 %collective-permute-start.40 = (bf16[128,4096]{1,0:T(8,128)(2,1)S(1)}, bf16[128,4096]{1,0:T(8,128)(2,1)}, u32[]{:S(2)}, u32[]{:S(2)}) collective-permute-start(bf16[128,4096]{1,0:T(8,128)(2,1)S(1)} %get-tuple-element.54), channel_id=1, source_target_pairs={{64,32},{65,33},{66,34},{67,35},{68,36},{69,37},{70,38},{71,39},{7... | collective-permute-start | bytes 3145736 | tf_op jit(solution)/shard_map/ppermute | solution.py:25
  174.7 7.0 %collective-permute-start.36 = (bf16[128,256]{1,0:T(8,128)(2,1)}, bf16[128,256]{1,0:T(8,128)(2,1)S(1)}, u32[]{:S(2)}, u32[]{:S(2)}) collective-permute-start(bf16[128,256]{1,0:T(8,128)(2,1)} %get-tuple-element.44), channel_id=1, source_target_pairs={{0,6},{1,7},{2,0},{3,1},{4,2},{5,3},{6,4},{7,5},{8,14},{9,15},{10,... | collective-permute-start | bytes 196616 | tf_op jit(solution)/shard_map/ppermute | solution.py:25
  178.6 7.5 %collective-permute-start.37 = (bf16[128,256]{1,0:T(8,128)(2,1)}, bf16[128,256]{1,0:T(8,128)(2,1)}, u32[]{:S(2)}, u32[]{:S(2)}) collective-permute-start(bf16[128,256]{1,0:T(8,128)(2,1)} %get-tuple-element.45), channel_id=1, source_target_pairs={{0,4},{1,5},{2,6},{3,7},{4,0},{5,1},{6,2},{7,3},{8,12},{9,13},{10,... | collective-permute-start | bytes 196616 | tf_op jit(solution)/shard_map/ppermute | solution.py:25
  178.6 7.6 %collective-permute-start.38 = (bf16[128,256]{1,0:T(8,128)(2,1)}, bf16[128,256]{1,0:T(8,128)(2,1)}, u32[]{:S(2)}, u32[]{:S(2)}) collective-permute-start(bf16[128,256]{1,0:T(8,128)(2,1)} %get-tuple-element.46), channel_id=1, source_target_pairs={{0,2},{1,3},{2,4},{3,5},{4,6},{5,7},{6,0},{7,1},{8,10},{9,11},{10,... | collective-permute-start | bytes 196616 | tf_op jit(solution)/shard_map/ppermute | solution.py:25
  203.1 16.1 %collective-permute-start.41 = (bf16[128,1024]{1,0:T(8,128)(2,1)S(1)}, bf16[128,1024]{1,0:T(8,128)(2,1)S(1)}, u32[]{:S(2)}, u32[]{:S(2)}) collective-permute-start(bf16[128,1024]{1,0:T(8,128)(2,1)S(1)} %get-tuple-element.56), channel_id=1, source_target_pairs={{32,64},{33,65},{34,66},{35,67},{36,68},{37,69},{38,70},{39,71},{4... | collective-permute-start | bytes 786440 | tf_op jit(solution)/shard_map/ppermute | solution.py:25
  206.8 12.4 %collective-permute-start.42 = (bf16[128,1024]{1,0:T(8,128)(2,1)S(1)}, bf16[128,1024]{1,0:T(8,128)(2,1)S(1)}, u32[]{:S(2)}, u32[]{:S(2)}) collective-permute-start(bf16[128,1024]{1,0:T(8,128)(2,1)S(1)} %get-tuple-element.57), channel_id=1, source_target_pairs={{32,96},{33,97},{34,98},{35,99},{36,100},{37,101},{38,102},{39,103... | collective-permute-start | bytes 786440 | tf_op jit(solution)/shard_map/ppermute | solution.py:25
  208.1 11.1 %collective-permute-start.43 = (bf16[128,1024]{1,0:T(8,128)(2,1)S(1)}, bf16[128,1024]{1,0:T(8,128)(2,1)S(1)}, u32[]{:S(2)}, u32[]{:S(2)}) collective-permute-start(bf16[128,1024]{1,0:T(8,128)(2,1)S(1)} %get-tuple-element.58), channel_id=1, source_target_pairs={{32,0},{33,1},{34,2},{35,3},{36,4},{37,5},{38,6},{39,7},{40,8},{41... | collective-permute-start | bytes 786440 | tf_op jit(solution)/shard_map/ppermute | solution.py:25
  (29 other events, 119.5 us)
Sparse Core Ops, SparseCore 0:
  10.8 109.2 all-gather.4
  122.3 67.9 all-gather.2

commit v4 on v3

--- a/solution.py
+++ b/solution.py
@@ -402,12 +402,12 @@
     bands, *here = finish_lag_0(first, last, wide_last, bands, got_b, prior_precision, n_week)
 
     arrived = [move(here[(1 + j) % n_week], dw=j, weeks=(1,)) for j in range(1, n_week)]
-    bands = add_lag_1(bands, got_a)
 
     ys = [((y + t) % n_y) * 2 + (k + e) % 2 for t in range(n_y) for e in range(2)]
     ys = jnp.stack(ys).astype(jnp.int32)
     schur = place_schur(ys, week, here[1], arrived, totals)
 
+    bands = add_lag_1(after(bands, schur), got_a)
     return (bands[None], panel, schur)
 
 

time: 230 us -> 231 us (level); the launches traced: 229 us -> 227 us
  transfers between devices with their start and end apart: 46 -> 46, of which waited for: 21 -> 23; matrix products, arithmetic and copies ran while one was open for 3% -> 3% of each run, Pallas kernels for 14% -> 14%
where the time goes in v4:
time: 231 us; the launch traced here: 227 us
  waiting for transfers between devices  87.8 us (38%)
  starting transfers between devices  68.8 us (30%)
  Pallas kernels  35.4 us (15%)
  between operations  14.5 us (6%)
  local copies, waits for them, and re-layouts  13.8 us (6%)
  other arithmetic  7.16 us (3%)
    ppermute x44, waiting for transfers between devices, moved(): return lax.ppermute(block, AXES, route)  83.7 us
    ppermute x44, starting transfers between devices, moved(): return lax.ppermute(block, AXES, route)  68.7 us
    unnamed x62, local copies, waits for them, and re-layouts  13 us
    pallas_call x1, Pallas kernels, band_products(): pl.pallas_call(kernel, grid=(regions // tile,), in_specs=[SMEM, VMEM, pl....  10.9 us
    pallas_call x1, Pallas kernels, coupling_and_parts(): pl.pallas_call(kernel, in_specs=[VMEM] * n_in, out_specs=[VMEM] * n_r, ou...  8.03 us
    pallas_call x1, Pallas kernels, finish_lag_0(): pl.pallas_call(kernel, grid=(regions // tile,), in_specs=[SMEM, VMEM, pl....  6.56 us
    select_n x5, other arithmetic, by_week(): return lax.select_n(week, *choices)  4.7 us
  transfers between devices with their start and end apart: 46, of which 23 were waited for; matrix products, arithmetic and copies ran while one was open for 3% of the time, Pallas kernels for 14%

profile of v4, /device:TPU:2, one launch (start us, length us, event | category | flops | bytes accessed | tf_op | source)
XLA Modules:
  0.0 227.5 jit_solution(312370482792313850)
XLA Ops:
  10.8 4.0 %collective-permute-start = (bf16[2,1024,128]{2,1,0:T(8,128)(2,1)}, bf16[2,1024,128]{2,1,0:T(8,128)(2,1)S(1)}, u32[]{:S(2)}, u32[]{:S(2)}) collective-permute-start(bf16[2,1024,128]{2,1,0:T(8,128)(2,1)} %pad_maximum_fusion.1), channel_id=1, source_target_pairs={{32,96},{33,97},{34,98},{35,99},{36,100},{37,101},{38,102},{39,103... | collective-permute-start | bytes 1572872 | tf_op jit(solution)/shard_map/ppermute | solution.py:25
  14.9 1.9 collective-permute-start.8
  16.8 4.7 %collective-permute-start.9 = (bf16[2,1024,128]{2,1,0:T(8,128)(2,1)}, bf16[2,1024,128]{2,1,0:T(8,128)(2,1)}, u32[]{:S(2)}, u32[]{:S(2)}) collective-permute-start(bf16[2,1024,128]{2,1,0:T(8,128)(2,1)} %pad_maximum_fusion.1), channel_id=1, source_target_pairs={{32,64},{33,65},{34,66},{35,67},{36,68},{37,69},{38,70},{39,71},{4... | collective-permute-start | bytes 1572872 | tf_op jit(solution)/shard_map/ppermute | solution.py:25
  21.5 1.9 collective-permute-start.1
  23.4 3.6 %collective-permute-start.2 = (bf16[1024,128]{1,0:T(8,128)(2,1)S(1)}, bf16[1024,128]{1,0:T(8,128)(2,1)S(1)}, u32[]{:S(2)}, u32[]{:S(2)}) collective-permute-start(bf16[1024,128]{1,0:T(8,128)(2,1)S(1)} %copy-done.3), channel_id=1, source_target_pairs={{0,16},{1,17},{2,18},{3,19},{4,20},{5,21},{6,22},{7,23},{8,24},{9,... | collective-permute-start | bytes 786440 | tf_op jit(solution)/shard_map/ppermute | solution.py:25
  27.0 2.2 collective-permute-done
  29.3 4.0 %collective-permute-start.3 = (bf16[1024,128]{1,0:T(8,128)(2,1)S(1)}, bf16[1024,128]{1,0:T(8,128)(2,1)S(1)}, u32[]{:S(2)}, u32[]{:S(2)}) collective-permute-start(bf16[1024,128]{1,0:T(8,128)(2,1)S(1)} %copy-done.3), channel_id=1, source_target_pairs={{0,24},{1,25},{2,26},{3,27},{4,28},{5,29},{6,30},{7,31},{8,0},{9,1... | collective-permute-start | bytes 786440 | tf_op jit(solution)/shard_map/ppermute | solution.py:25
  33.3 6.0 %collective-permute-done.8 = bf16[2,1024,128]{2,1,0:T(8,128)(2,1)S(1)} collective-permute-done((bf16[2,1024,128]{2,1,0:T(8,128)(2,1)}, bf16[2,1024,128]{2,1,0:T(8,128)(2,1)S(1)}, u32[]{:S(2)}, u32[]{:S(2)}) %collective-permute-start.8) | collective-permute-done | bytes 524320 | tf_op jit(solution)/shard_map/ppermute | solution.py:25
  40.5 2.0 collective-permute-start.13
  43.5 3.3 %collective-permute-start.14 = (bf16[2,1024,128]{2,1,0:T(8,128)(2,1)S(1)}, bf16[2,1024,128]{2,1,0:T(8,128)(2,1)}, u32[]{:S(2)}, u32[]{:S(2)}) collective-permute-start(bf16[2,1024,128]{2,1,0:T(8,128)(2,1)S(1)} %pad_maximum_fusion.3.refs_12_), channel_id=1, source_target_pairs={{0,16},{1,17},{2,18},{3,19},{4,20},{5,21},{6,22},{7,23},{8,24},{9,... | collective-permute-start | bytes 1572872 | tf_op jit(solution)/shard_map/ppermute | solution.py:25
  49.2 1.6 collective-permute-start.10
  51.5 2.9 %collective-permute-start.11 = (bf16[2,1024,128]{2,1,0:T(8,128)(2,1)S(1)}, bf16[2,1024,128]{2,1,0:T(8,128)(2,1)S(1)}, u32[]{:S(2)}, u32[]{:S(2)}) collective-permute-start(bf16[2,1024,128]{2,1,0:T(8,128)(2,1)S(1)} %pad_maximum_fusion.2.refs_8_), channel_id=1, source_target_pairs={{0,4},{1,5},{2,6},{3,7},{4,0},{5,1},{6,2},{7,3},{8,12},{9,13},{10,... | collective-permute-start | bytes 1572872 | tf_op jit(solution)/shard_map/ppermute | solution.py:25
  54.4 3.4 %collective-permute-done.13.refs_13_ = bf16[2,1024,128]{2,1,0:T(8,128)(2,1)} collective-permute-done((bf16[2,1024,128]{2,1,0:T(8,128)(2,1)S(1)}, bf16[2,1024,128]{2,1,0:T(8,128)(2,1)}, u32[]{:S(2)}, u32[]{:S(2)}) %collective-permute-start.13) | collective-permute-done | bytes 524320 | tf_op jit(solution)/shard_map/ppermute | solution.py:25
  57.8 1.6 collective-permute-done.7.refs_7_
  60.1 2.7 %collective-permute-start.12 = (bf16[2,1024,128]{2,1,0:T(8,128)(2,1)S(1)}, bf16[2,1024,128]{2,1,0:T(8,128)(2,1)S(1)}, u32[]{:S(2)}, u32[]{:S(2)}) collective-permute-start(bf16[2,1024,128]{2,1,0:T(8,128)(2,1)S(1)} %pad_maximum_fusion.2.refs_8_), channel_id=1, source_target_pairs={{0,6},{1,7},{2,0},{3,1},{4,2},{5,3},{6,4},{7,5},{8,14},{9,15},{10,... | collective-permute-start | bytes 1572872 | tf_op jit(solution)/shard_map/ppermute | solution.py:25
  62.9 18.9 %collective-permute-done.14.refs_14_ = bf16[2,1024,128]{2,1,0:T(8,128)(2,1)} collective-permute-done((bf16[2,1024,128]{2,1,0:T(8,128)(2,1)S(1)}, bf16[2,1024,128]{2,1,0:T(8,128)(2,1)}, u32[]{:S(2)}, u32[]{:S(2)}) %collective-permute-start.14) | collective-permute-done | bytes 524320 | tf_op jit(solution)/shard_map/ppermute | solution.py:25
  82.4 5.5 %collective-permute-done.11.refs_10_ = bf16[2,1024,128]{2,1,0:T(8,128)(2,1)S(1)} collective-permute-done((bf16[2,1024,128]{2,1,0:T(8,128)(2,1)S(1)}, bf16[2,1024,128]{2,1,0:T(8,128)(2,1)S(1)}, u32[]{:S(2)}, u32[]{:S(2)}) %collective-permute-start.11) | collective-permute-done | bytes 524320 | tf_op jit(solution)/shard_map/ppermute | solution.py:25
  87.9 1.9 fusion.11.left_ref
  97.0 8.0 %coupling_and_parts.1 = (f32[128,1024]{1,0:T(8,128)S(1)}, bf16[128,1024]{1,0:T(8,128)(2,1)S(1)}, bf16[128,1024]{1,0:T(8,128)(2,1)S(1)}, bf16[128,1024]{1,0:T(8,128)(2,1)S(1)}) custom-call(bf16[1024,128]{1,0:T(8,128)(2,1)S(1)} %copy-done.3, bf16[1024,128]{1,0:T(8,128)(2,1)S(1)} %copy-done.6, bf16[1024,128]{1,0:T(8,128)(2,1)S(1)} %copy-done.8, ...), custom_call_target="tpu_custom_call" | custom-call | tf_op jit(solution)/shard_map/coupling_and_parts/pallas_call | solution.py:104
  107.2 3.9 %collective-permute-start.20 = (bf16[128,1024]{1,0:T(8,128)(2,1)}, bf16[128,1024]{1,0:T(8,128)(2,1)S(1)}, u32[]{:S(2)}, u32[]{:S(2)}) collective-permute-start(bf16[128,1024]{1,0:T(8,128)(2,1)} %copy-done.21), channel_id=1, source_target_pairs={{0,6},{1,7},{2,0},{3,1},{4,2},{5,3},{6,4},{7,5},{8,14},{9,15},{10,... | collective-permute-start | bytes 786440 | tf_op jit(solution)/shard_map/ppermute | solution.py:25
  112.5 7.6 %collective-permute-done.20 = bf16[128,1024]{1,0:T(8,128)(2,1)S(1)} collective-permute-done((bf16[128,1024]{1,0:T(8,128)(2,1)}, bf16[128,1024]{1,0:T(8,128)(2,1)S(1)}, u32[]{:S(2)}, u32[]{:S(2)}) %collective-permute-start.20) | collective-permute-done | bytes 262176 | tf_op jit(solution)/shard_map/ppermute | solution.py:25
  120.1 2.0 collective-permute-done.21
  122.1 4.1 %collective-permute-done.22 = bf16[128,1024]{1,0:T(8,128)(2,1)S(1)} collective-permute-done((bf16[128,1024]{1,0:T(8,128)(2,1)}, bf16[128,1024]{1,0:T(8,128)(2,1)S(1)}, u32[]{:S(2)}, u32[]{:S(2)}) %collective-permute-start.22) | collective-permute-done | bytes 262176 | tf_op jit(solution)/shard_map/ppermute | solution.py:25
  127.4 2.6 %collective-permute-start.28 = (bf16[128,1024]{1,0:T(8,128)(2,1)S(1)}, bf16[128,1024]{1,0:T(8,128)(2,1)S(1)}, u32[]{:S(2)}, u32[]{:S(2)}) collective-permute-start(bf16[128,1024]{1,0:T(8,128)(2,1)S(1)} %add_convert_fusion.refs_1_.refs_5_), channel_id=1, source_target_pairs={{0,24},{1,25},{2,26},{3,27},{4,28},{5,29},{6,30},{7,31},{8,0},{9,1... | collective-permute-start | bytes 786440 | tf_op jit(solution)/shard_map/ppermute | solution.py:25
  130.5 3.1 %collective-permute-start.24 = (bf16[128,1024]{1,0:T(8,128)(2,1)S(1)}, bf16[128,1024]{1,0:T(8,128)(2,1)S(1)}, u32[]{:S(2)}, u32[]{:S(2)}) collective-permute-start(bf16[128,1024]{1,0:T(8,128)(2,1)S(1)} %add_convert_fusion.refs_1_.refs_5_), channel_id=1, source_target_pairs={{0,4},{1,5},{2,6},{3,7},{4,0},{5,1},{6,2},{7,3},{8,12},{9,13},{10,... | collective-permute-start | bytes 786440 | tf_op jit(solution)/shard_map/ppermute | solution.py:25
  133.7 7.8 %collective-permute-done.26.refs_6_ = bf16[128,1024]{1,0:T(8,128)(2,1)S(1)} collective-permute-done((bf16[128,1024]{1,0:T(8,128)(2,1)S(1)}, bf16[128,1024]{1,0:T(8,128)(2,1)S(1)}, u32[]{:S(2)}, u32[]{:S(2)}) %collective-permute-start.26) | collective-permute-done | bytes 262176 | tf_op jit(solution)/shard_map/ppermute | solution.py:25
  141.5 1.7 collective-permute-start.25
  144.0 2.1 collective-permute-done.24.refs_3_
  146.2 4.3 %collective-permute-done.25.refs_4_ = bf16[128,1024]{1,0:T(8,128)(2,1)S(1)} collective-permute-done((bf16[128,1024]{1,0:T(8,128)(2,1)S(1)}, bf16[128,1024]{1,0:T(8,128)(2,1)S(1)}, u32[]{:S(2)}, u32[]{:S(2)}) %collective-permute-start.25) | collective-permute-done | bytes 262176 | tf_op jit(solution)/shard_map/ppermute | solution.py:25
  150.5 2.6 %gram_terms.1 = (f32[512,256]{1,0:T(8,128)S(1)}, bf16[512,256]{1,0:T(8,128)(2,1)}, bf16[512,256]{1,0:T(8,128)(2,1)}, bf16[512,256]{1,0:T(8,128)(2,1)}) custom-call(s32[1]{0:T(128)} %bitcast.7.refs_0_, bf16[128,1024]{1,0:T(8,128)(2,1)S(1)} %add_convert_fusion.refs_1_.refs_5_, bf16[128,1024]{1,0:T(8,128)(2,1)S(1)} %collective-permute-done.23.refs_2_, ...), custom_call_target="tpu_custom_call" | custom-call | tf_op jit(solution)/shard_map/gram_terms/pallas_call | solution.py:144
  153.2 2.9 %collective-permute-start.34 = (bf16[512,256]{1,0:T(8,128)(2,1)}, bf16[512,256]{1,0:T(8,128)(2,1)}, u32[]{:S(2)}, u32[]{:S(2)}) collective-permute-start(bf16[512,256]{1,0:T(8,128)(2,1)} %get-tuple-element.42), channel_id=1, source_target_pairs={{0,64},{1,65},{2,66},{3,67},{4,68},{5,69},{6,70},{7,71},{8,72},{9,... | collective-permute-start | bytes 786440 | tf_op jit(solution)/shard_map/ppermute | solution.py:25
  156.9 10.9 %band_products.1 = (f32[3,128,4096]{2,1,0:T(8,128)}, bf16[128,4096]{1,0:T(8,128)(2,1)S(1)}, bf16[128,4096]{1,0:T(8,128)(2,1)S(1)}) custom-call(s32[1]{0:T(128)} %bitcast.8.week_ref, bf16[1024,512]{1,0:T(8,128)(2,1)S(1)} %pad_maximum_fusion.left_ref, bf16[2,1024,4096]{2,1,0:T(8,128)(2,1)} %all-gather.5.cloned.1.call-done.wide_ref), custom_call_target="tpu_custom_call" | custom-call | tf_op jit(solution)/shard_map/band_products/pallas_call | solution.py:203
  167.9 3.5 %collective-permute-start.39 = (bf16[128,4096]{1,0:T(8,128)(2,1)S(1)}, bf16[128,4096]{1,0:T(8,128)(2,1)S(1)}, u32[]{:S(2)}, u32[]{:S(2)}) collective-permute-start(bf16[128,4096]{1,0:T(8,128)(2,1)S(1)} %get-tuple-element.52), channel_id=1, source_target_pairs={{32,0},{33,1},{34,2},{35,3},{36,4},{37,5},{38,6},{39,7},{40,8},{41... | collective-permute-start | bytes 3145736 | tf_op jit(solution)/shard_map/ppermute | solution.py:25
  171.3 2.1 week_sum.1
  173.4 1.3 collective-permute-start.43
  174.7 3.9 %collective-permute-start.36 = (bf16[128,256]{1,0:T(8,128)(2,1)}, bf16[128,256]{1,0:T(8,128)(2,1)S(1)}, u32[]{:S(2)}, u32[]{:S(2)}) collective-permute-start(bf16[128,256]{1,0:T(8,128)(2,1)} %get-tuple-element.45), channel_id=1, source_target_pairs={{0,6},{1,7},{2,0},{3,1},{4,2},{5,3},{6,4},{7,5},{8,14},{9,15},{10,... | collective-permute-start | bytes 196616 | tf_op jit(solution)/shard_map/ppermute | solution.py:25
  179.7 2.0 collective-permute-done.36.refs_4_
  181.7 4.4 %collective-permute-done.37.refs_5_ = bf16[128,256]{1,0:T(8,128)(2,1)} collective-permute-done((bf16[128,256]{1,0:T(8,128)(2,1)}, bf16[128,256]{1,0:T(8,128)(2,1)}, u32[]{:S(2)}, u32[]{:S(2)}) %collective-permute-start.37) | collective-permute-done | bytes 65568 | tf_op jit(solution)/shard_map/ppermute | solution.py:25
  186.2 4.0 %all-gather.3.cloned.1.call-done.wide_ref = bf16[1024,4096]{1,0:T(8,128)(2,1)} async-done(((bf16[1024,128]{1,0:T(8,128)(2,1)}), bf16[1024,4096]{1,0:T(8,128)(2,1)}) %all-gather.3.cloned.1.call-update) | async-done | bytes 8388624 | tf_op jit(solution)/shard_map/all_gather | solution.py:374
  190.3 5.6 %collective-permute-done.39.arrived_ref = bf16[128,4096]{1,0:T(8,128)(2,1)S(1)} collective-permute-done((bf16[128,4096]{1,0:T(8,128)(2,1)S(1)}, bf16[128,4096]{1,0:T(8,128)(2,1)S(1)}, u32[]{:S(2)}, u32[]{:S(2)}) %collective-permute-start.39) | collective-permute-done | bytes 1048608 | tf_op jit(solution)/shard_map/ppermute | solution.py:25
  195.9 6.6 %finish_lag_0.1 = (f32[3,128,4096]{2,1,0:T(8,128)}, bf16[128,1024]{1,0:T(8,128)(2,1)S(1)}, bf16[128,1024]{1,0:T(8,128)(2,1)S(1)}, bf16[128,1024]{1,0:T(8,128)(2,1)S(1)}, bf16[128,1024]{1,0:T(8,128)(2,1)S(1)}) custom-call(s32[1]{0:T(128)} %bitcast.first_ref, bf16[1024,128]{1,0:T(8,128)(2,1)S(1)} %copy-done, ...), custom_call_target="tpu_custom_call", output_to_operand_aliasing={{0}: (3, {})} | custom-call | tf_op jit(solution)/shard_map/finish_lag_0/pallas_call | solution.py:273
  203.1 3.6 %collective-permute-start.40 = (bf16[128,1024]{1,0:T(8,128)(2,1)S(1)}, bf16[128,1024]{1,0:T(8,128)(2,1)S(1)}, u32[]{:S(2)}, u32[]{:S(2)}) collective-permute-start(bf16[128,1024]{1,0:T(8,128)(2,1)S(1)} %get-tuple-element.55), channel_id=1, source_target_pairs={{32,64},{33,65},{34,66},{35,67},{36,68},{37,69},{38,70},{39,71},{4... | collective-permute-start | bytes 786440 | tf_op jit(solution)/shard_map/ppermute | solution.py:25
  206.8 1.3 collective-permute-start.41
  208.1 1.3 collective-permute-start.42
  210.6 1.3 collective-permute-done.41.refs_1_
  211.9 2.8 %collective-permute-done.42.refs_2_ = bf16[128,1024]{1,0:T(8,128)(2,1)S(1)} collective-permute-done((bf16[128,1024]{1,0:T(8,128)(2,1)S(1)}, bf16[128,1024]{1,0:T(8,128)(2,1)S(1)}, u32[]{:S(2)}, u32[]{:S(2)}) %collective-permute-start.42) | collective-permute-done | bytes 262176 | tf_op jit(solution)/shard_map/ppermute | solution.py:25
  215.4 2.3 %place_schur.1 = f32[128,1024]{1,0:T(8,128)} custom-call(s32[8]{0:T(128)} %stack.58.ys_ref, s32[1]{0:T(128)} %bitcast.8.week_ref, bf16[128,1024]{1,0:T(8,128)(2,1)} %copy-done.4, bf16[128,1024]{1,0:T(8,128)(2,1)} %copy-done.24, bf16[128,1024]{1,0:T(8,128)(2,1)} %copy-done.25, bf16[128,1024]{1,0:T(8,128)(2,1)} %copy-done.26, ...), custom_call_target="tpu_custom_call" | custom-call | tf_op jit(solution)/shard_map/place_schur/pallas_call | solution.py:309
  217.7 2.9 %add_lag_1.1 = f32[3,128,4096]{2,1,0:T(8,128)} custom-call(f32[3,128,4096]{2,1,0:T(8,128)} %get-tuple-element.58.band_ref, bf16[128,4096]{1,0:T(8,128)(2,1)} %collective-permute-done.43.arrived_ref), custom_call_target="tpu_custom_call", output_to_operand_aliasing={{}: (0, {})} | custom-call | tf_op jit(solution)/shard_map/add_lag_1/pallas_call | solution.py:231
  (130 shorter events, 28.1 us)
Async XLA Ops:
  7.2 149.7 %all-gather.5.cloned.1.call-start = ((), (), s32[]{:S(2)}) async-start(), calls=%async_computation.1 | async-start | bytes 17301504 | tf_op jit(solution)/shard_map/all_gather | solution.py:349
  9.3 180.9 %all-gather.3.cloned.1.call-start = ((), (), s32[]{:S(2)}) async-start(), calls=%async_computation | async-start | bytes 8650752 | tf_op jit(solution)/shard_map/all_gather | solution.py:374
  10.8 18.4 %collective-permute-start = (bf16[2,1024,128]{2,1,0:T(8,128)(2,1)}, bf16[2,1024,128]{2,1,0:T(8,128)(2,1)S(1)}, u32[]{:S(2)}, u32[]{:S(2)}) collective-permute-start(bf16[2,1024,128]{2,1,0:T(8,128)(2,1)} %pad_maximum_fusion.1), channel_id=1, source_target_pairs={{32,96},{33,97},{34,98},{35,99},{36,100},{37,101},{38,102},{39,103... | collective-permute-start | bytes 1572872 | tf_op jit(solution)/shard_map/ppermute | solution.py:25
  14.9 24.5 %collective-permute-start.8 = (bf16[2,1024,128]{2,1,0:T(8,128)(2,1)}, bf16[2,1024,128]{2,1,0:T(8,128)(2,1)S(1)}, u32[]{:S(2)}, u32[]{:S(2)}) collective-permute-start(bf16[2,1024,128]{2,1,0:T(8,128)(2,1)} %pad_maximum_fusion.1), channel_id=1, source_target_pairs={{32,0},{33,1},{34,2},{35,3},{36,4},{37,5},{38,6},{39,7},{40,8},{41... | collective-permute-start | bytes 1572872 | tf_op jit(solution)/shard_map/ppermute | solution.py:25
  16.8 22.5 %collective-permute-start.9 = (bf16[2,1024,128]{2,1,0:T(8,128)(2,1)}, bf16[2,1024,128]{2,1,0:T(8,128)(2,1)}, u32[]{:S(2)}, u32[]{:S(2)}) collective-permute-start(bf16[2,1024,128]{2,1,0:T(8,128)(2,1)} %pad_maximum_fusion.1), channel_id=1, source_target_pairs={{32,64},{33,65},{34,66},{35,67},{36,68},{37,69},{38,70},{39,71},{4... | collective-permute-start | bytes 1572872 | tf_op jit(solution)/shard_map/ppermute | solution.py:25
  21.5 21.0 %collective-permute-start.1 = (bf16[1024,128]{1,0:T(8,128)(2,1)S(1)}, bf16[1024,128]{1,0:T(8,128)(2,1)S(1)}, u32[]{:S(2)}, u32[]{:S(2)}) collective-permute-start(bf16[1024,128]{1,0:T(8,128)(2,1)S(1)} %copy-done.3), channel_id=1, source_target_pairs={{0,8},{1,9},{2,10},{3,11},{4,12},{5,13},{6,14},{7,15},{8,16},{9,17... | collective-permute-start | bytes 786440 | tf_op jit(solution)/shard_map/ppermute | solution.py:25
  23.4 20.0 %collective-permute-start.2 = (bf16[1024,128]{1,0:T(8,128)(2,1)S(1)}, bf16[1024,128]{1,0:T(8,128)(2,1)S(1)}, u32[]{:S(2)}, u32[]{:S(2)}) collective-permute-start(bf16[1024,128]{1,0:T(8,128)(2,1)S(1)} %copy-done.3), channel_id=1, source_target_pairs={{0,16},{1,17},{2,18},{3,19},{4,20},{5,21},{6,22},{7,23},{8,24},{9,... | collective-permute-start | bytes 786440 | tf_op jit(solution)/shard_map/ppermute | solution.py:25
  29.3 14.2 %collective-permute-start.3 = (bf16[1024,128]{1,0:T(8,128)(2,1)S(1)}, bf16[1024,128]{1,0:T(8,128)(2,1)S(1)}, u32[]{:S(2)}, u32[]{:S(2)}) collective-permute-start(bf16[1024,128]{1,0:T(8,128)(2,1)S(1)} %copy-done.3), channel_id=1, source_target_pairs={{0,24},{1,25},{2,26},{3,27},{4,28},{5,29},{6,30},{7,31},{8,0},{9,1... | collective-permute-start | bytes 786440 | tf_op jit(solution)/shard_map/ppermute | solution.py:25
  40.5 17.3 %collective-permute-start.13 = (bf16[2,1024,128]{2,1,0:T(8,128)(2,1)S(1)}, bf16[2,1024,128]{2,1,0:T(8,128)(2,1)}, u32[]{:S(2)}, u32[]{:S(2)}) collective-permute-start(bf16[2,1024,128]{2,1,0:T(8,128)(2,1)S(1)} %pad_maximum_fusion.3.refs_12_), channel_id=1, source_target_pairs={{0,8},{1,9},{2,10},{3,11},{4,12},{5,13},{6,14},{7,15},{8,16},{9,17... | collective-permute-start | bytes 1572872 | tf_op jit(solution)/shard_map/ppermute | solution.py:25
  42.5 4.3 %collective-permute-start.4 = (bf16[1024,128]{1,0:T(8,128)(2,1)S(1)}, bf16[1024,128]{1,0:T(8,128)(2,1)S(1)}, u32[]{:S(2)}, u32[]{:S(2)}) collective-permute-start(bf16[1024,128]{1,0:T(8,128)(2,1)S(1)} %copy-done.3), channel_id=1, source_target_pairs={{0,1},{1,0},{2,3},{3,2},{4,5},{5,4},{6,7},{7,6},{8,9},{9,8},{10,11... | collective-permute-start | bytes 786440 | tf_op jit(solution)/shard_map/ppermute | solution.py:25
  42.5 6.0 %collective-permute-start.5 = (bf16[1024,128]{1,0:T(8,128)(2,1)S(1)}, bf16[1024,128]{1,0:T(8,128)(2,1)S(1)}, u32[]{:S(2)}, u32[]{:S(2)}) collective-permute-start(bf16[1024,128]{1,0:T(8,128)(2,1)S(1)} %collective-permute-done.1.refs_1_), channel_id=1, source_target_pairs={{0,1},{1,0},{2,3},{3,2},{4,5},{5,4},{6,7},{7,6},{8,9},{9,8},{10,11... | collective-permute-start | bytes 786440 | tf_op jit(solution)/shard_map/ppermute | solution.py:25
  43.5 7.4 %collective-permute-start.6 = (bf16[1024,128]{1,0:T(8,128)(2,1)S(1)}, bf16[1024,128]{1,0:T(8,128)(2,1)S(1)}, u32[]{:S(2)}, u32[]{:S(2)}) collective-permute-start(bf16[1024,128]{1,0:T(8,128)(2,1)S(1)} %collective-permute-done.2.refs_2_), channel_id=1, source_target_pairs={{0,1},{1,0},{2,3},{3,2},{4,5},{5,4},{6,7},{7,6},{8,9},{9,8},{10,11... | collective-permute-start | bytes 786440 | tf_op jit(solution)/shard_map/ppermute | solution.py:25
  43.5 38.3 %collective-permute-start.14 = (bf16[2,1024,128]{2,1,0:T(8,128)(2,1)S(1)}, bf16[2,1024,128]{2,1,0:T(8,128)(2,1)}, u32[]{:S(2)}, u32[]{:S(2)}) collective-permute-start(bf16[2,1024,128]{2,1,0:T(8,128)(2,1)S(1)} %pad_maximum_fusion.3.refs_12_), channel_id=1, source_target_pairs={{0,16},{1,17},{2,18},{3,19},{4,20},{5,21},{6,22},{7,23},{8,24},{9,... | collective-permute-start | bytes 1572872 | tf_op jit(solution)/shard_map/ppermute | solution.py:25
  47.5 34.3 %collective-permute-start.15 = (bf16[2,1024,128]{2,1,0:T(8,128)(2,1)S(1)}, bf16[2,1024,128]{2,1,0:T(8,128)(2,1)}, u32[]{:S(2)}, u32[]{:S(2)}) collective-permute-start(bf16[2,1024,128]{2,1,0:T(8,128)(2,1)S(1)} %pad_maximum_fusion.3.refs_12_), channel_id=1, source_target_pairs={{0,24},{1,25},{2,26},{3,27},{4,28},{5,29},{6,30},{7,31},{8,0},{9,1... | collective-permute-start | bytes 1572872 | tf_op jit(solution)/shard_map/ppermute | solution.py:25
  49.2 33.1 %collective-permute-start.10 = (bf16[2,1024,128]{2,1,0:T(8,128)(2,1)S(1)}, bf16[2,1024,128]{2,1,0:T(8,128)(2,1)S(1)}, u32[]{:S(2)}, u32[]{:S(2)}) collective-permute-start(bf16[2,1024,128]{2,1,0:T(8,128)(2,1)S(1)} %pad_maximum_fusion.2.refs_8_), channel_id=1, source_target_pairs={{0,2},{1,3},{2,4},{3,5},{4,6},{5,7},{6,0},{7,1},{8,10},{9,11},{10,... | collective-permute-start | bytes 1572872 | tf_op jit(solution)/shard_map/ppermute | solution.py:25
  51.5 36.4 %collective-permute-start.11 = (bf16[2,1024,128]{2,1,0:T(8,128)(2,1)S(1)}, bf16[2,1024,128]{2,1,0:T(8,128)(2,1)S(1)}, u32[]{:S(2)}, u32[]{:S(2)}) collective-permute-start(bf16[2,1024,128]{2,1,0:T(8,128)(2,1)S(1)} %pad_maximum_fusion.2.refs_8_), channel_id=1, source_target_pairs={{0,4},{1,5},{2,6},{3,7},{4,0},{5,1},{6,2},{7,3},{8,12},{9,13},{10,... | collective-permute-start | bytes 1572872 | tf_op jit(solution)/shard_map/ppermute | solution.py:25
  57.8 1.6 collective-permute-start.7
  60.1 30.2 %collective-permute-start.12 = (bf16[2,1024,128]{2,1,0:T(8,128)(2,1)S(1)}, bf16[2,1024,128]{2,1,0:T(8,128)(2,1)S(1)}, u32[]{:S(2)}, u32[]{:S(2)}) collective-permute-start(bf16[2,1024,128]{2,1,0:T(8,128)(2,1)S(1)} %pad_maximum_fusion.2.refs_8_), channel_id=1, source_target_pairs={{0,6},{1,7},{2,0},{3,1},{4,2},{5,3},{6,4},{7,5},{8,14},{9,15},{10,... | collective-permute-start | bytes 1572872 | tf_op jit(solution)/shard_map/ppermute | solution.py:25
  81.8 8.5 %collective-permute-start.16 = (bf16[2,1024,128]{2,1,0:T(8,128)(2,1)S(1)}, bf16[2,1024,128]{2,1,0:T(8,128)(2,1)}, u32[]{:S(2)}, u32[]{:S(2)}) collective-permute-start(bf16[2,1024,128]{2,1,0:T(8,128)(2,1)S(1)} %pad_maximum_fusion.3.refs_12_), channel_id=1, source_target_pairs={{0,1},{1,0},{2,3},{3,2},{4,5},{5,4},{6,7},{7,6},{8,9},{9,8},{10,11... | collective-permute-start | bytes 1572872 | tf_op jit(solution)/shard_map/ppermute | solution.py:25
  81.8 8.5 %collective-permute-start.17 = (bf16[2,1024,128]{2,1,0:T(8,128)(2,1)}, bf16[2,1024,128]{2,1,0:T(8,128)(2,1)}, u32[]{:S(2)}, u32[]{:S(2)}) collective-permute-start(bf16[2,1024,128]{2,1,0:T(8,128)(2,1)} %collective-permute-done.13.refs_13_), channel_id=1, source_target_pairs={{0,1},{1,0},{2,3},{3,2},{4,5},{5,4},{6,7},{7,6},{8,9},{9,8},{10,11... | collective-permute-start | bytes 1572872 | tf_op jit(solution)/shard_map/ppermute | solution.py:25
  82.3 8.0 %collective-permute-start.18 = (bf16[2,1024,128]{2,1,0:T(8,128)(2,1)}, bf16[2,1024,128]{2,1,0:T(8,128)(2,1)}, u32[]{:S(2)}, u32[]{:S(2)}) collective-permute-start(bf16[2,1024,128]{2,1,0:T(8,128)(2,1)} %collective-permute-done.14.refs_14_), channel_id=1, source_target_pairs={{0,1},{1,0},{2,3},{3,2},{4,5},{5,4},{6,7},{7,6},{8,9},{9,8},{10,11... | collective-permute-start | bytes 1572872 | tf_op jit(solution)/shard_map/ppermute | solution.py:25
  87.9 2.4 %collective-permute-start.19 = (bf16[2,1024,128]{2,1,0:T(8,128)(2,1)}, bf16[2,1024,128]{2,1,0:T(8,128)(2,1)}, u32[]{:S(2)}, u32[]{:S(2)}) collective-permute-start(bf16[2,1024,128]{2,1,0:T(8,128)(2,1)} %collective-permute-done.15.refs_15_), channel_id=1, source_target_pairs={{0,1},{1,0},{2,3},{3,2},{4,5},{5,4},{6,7},{7,6},{8,9},{9,8},{10,11... | collective-permute-start | bytes 1572872 | tf_op jit(solution)/shard_map/ppermute | solution.py:25
  107.2 12.9 %collective-permute-start.20 = (bf16[128,1024]{1,0:T(8,128)(2,1)}, bf16[128,1024]{1,0:T(8,128)(2,1)S(1)}, u32[]{:S(2)}, u32[]{:S(2)}) collective-permute-start(bf16[128,1024]{1,0:T(8,128)(2,1)} %copy-done.21), channel_id=1, source_target_pairs={{0,6},{1,7},{2,0},{3,1},{4,2},{5,3},{6,4},{7,5},{8,14},{9,15},{10,... | collective-permute-start | bytes 786440 | tf_op jit(solution)/shard_map/ppermute | solution.py:25
  111.1 11.0 %collective-permute-start.21 = (bf16[128,1024]{1,0:T(8,128)(2,1)}, bf16[128,1024]{1,0:T(8,128)(2,1)S(1)}, u32[]{:S(2)}, u32[]{:S(2)}) collective-permute-start(bf16[128,1024]{1,0:T(8,128)(2,1)} %copy-done.20), channel_id=1, source_target_pairs={{0,4},{1,5},{2,6},{3,7},{4,0},{5,1},{6,2},{7,3},{8,12},{9,13},{10,... | collective-permute-start | bytes 786440 | tf_op jit(solution)/shard_map/ppermute | solution.py:25
  111.9 14.3 %collective-permute-start.22 = (bf16[128,1024]{1,0:T(8,128)(2,1)}, bf16[128,1024]{1,0:T(8,128)(2,1)S(1)}, u32[]{:S(2)}, u32[]{:S(2)}) collective-permute-start(bf16[128,1024]{1,0:T(8,128)(2,1)} %copy-done.19), channel_id=1, source_target_pairs={{0,2},{1,3},{2,4},{3,5},{4,6},{5,7},{6,0},{7,1},{8,10},{9,11},{10,... | collective-permute-start | bytes 786440 | tf_op jit(solution)/shard_map/ppermute | solution.py:25
  126.4 30.4 %copy-start.1 = (bf16[128,1024]{1,0:T(8,128)(2,1)}, bf16[128,1024]{1,0:T(8,128)(2,1)S(1)}, u32[]{:S(2)}) copy-start(bf16[128,1024]{1,0:T(8,128)(2,1)S(1)} %add_convert_fusion.refs_1_.refs_5_) | copy-start | bytes 786436
  126.4 15.1 %collective-permute-start.26 = (bf16[128,1024]{1,0:T(8,128)(2,1)S(1)}, bf16[128,1024]{1,0:T(8,128)(2,1)S(1)}, u32[]{:S(2)}, u32[]{:S(2)}) collective-permute-start(bf16[128,1024]{1,0:T(8,128)(2,1)S(1)} %add_convert_fusion.refs_1_.refs_5_), channel_id=1, source_target_pairs={{0,8},{1,9},{2,10},{3,11},{4,12},{5,13},{6,14},{7,15},{8,16},{9,17... | collective-permute-start | bytes 786440 | tf_op jit(solution)/shard_map/ppermute | solution.py:25
  127.2 16.0 %collective-permute-start.27 = (bf16[128,1024]{1,0:T(8,128)(2,1)S(1)}, bf16[128,1024]{1,0:T(8,128)(2,1)S(1)}, u32[]{:S(2)}, u32[]{:S(2)}) collective-permute-start(bf16[128,1024]{1,0:T(8,128)(2,1)S(1)} %add_convert_fusion.refs_1_.refs_5_), channel_id=1, source_target_pairs={{0,16},{1,17},{2,18},{3,19},{4,20},{5,21},{6,22},{7,23},{8,24},{9,... | collective-permute-start | bytes 786440 | tf_op jit(solution)/shard_map/ppermute | solution.py:25
  127.4 16.2 %collective-permute-start.28 = (bf16[128,1024]{1,0:T(8,128)(2,1)S(1)}, bf16[128,1024]{1,0:T(8,128)(2,1)S(1)}, u32[]{:S(2)}, u32[]{:S(2)}) collective-permute-start(bf16[128,1024]{1,0:T(8,128)(2,1)S(1)} %add_convert_fusion.refs_1_.refs_5_), channel_id=1, source_target_pairs={{0,24},{1,25},{2,26},{3,27},{4,28},{5,29},{6,30},{7,31},{8,0},{9,1... | collective-permute-start | bytes 786440 | tf_op jit(solution)/shard_map/ppermute | solution.py:25
  130.0 13.8 %collective-permute-start.23 = (bf16[128,1024]{1,0:T(8,128)(2,1)S(1)}, bf16[128,1024]{1,0:T(8,128)(2,1)S(1)}, u32[]{:S(2)}, u32[]{:S(2)}) collective-permute-start(bf16[128,1024]{1,0:T(8,128)(2,1)S(1)} %add_convert_fusion.refs_1_.refs_5_), channel_id=1, source_target_pairs={{0,2},{1,3},{2,4},{3,5},{4,6},{5,7},{6,0},{7,1},{8,10},{9,11},{10,... | collective-permute-start | bytes 786440 | tf_op jit(solution)/shard_map/ppermute | solution.py:25
  130.5 15.6 %collective-permute-start.24 = (bf16[128,1024]{1,0:T(8,128)(2,1)S(1)}, bf16[128,1024]{1,0:T(8,128)(2,1)S(1)}, u32[]{:S(2)}, u32[]{:S(2)}) collective-permute-start(bf16[128,1024]{1,0:T(8,128)(2,1)S(1)} %add_convert_fusion.refs_1_.refs_5_), channel_id=1, source_target_pairs={{0,4},{1,5},{2,6},{3,7},{4,0},{5,1},{6,2},{7,3},{8,12},{9,13},{10,... | collective-permute-start | bytes 786440 | tf_op jit(solution)/shard_map/ppermute | solution.py:25
  141.5 9.0 %collective-permute-start.25 = (bf16[128,1024]{1,0:T(8,128)(2,1)S(1)}, bf16[128,1024]{1,0:T(8,128)(2,1)S(1)}, u32[]{:S(2)}, u32[]{:S(2)}) collective-permute-start(bf16[128,1024]{1,0:T(8,128)(2,1)S(1)} %add_convert_fusion.refs_1_.refs_5_), channel_id=1, source_target_pairs={{0,6},{1,7},{2,0},{3,1},{4,2},{5,3},{6,4},{7,5},{8,14},{9,15},{10,... | collective-permute-start | bytes 786440 | tf_op jit(solution)/shard_map/ppermute | solution.py:25
  143.2 7.3 %collective-permute-start.29 = (bf16[128,1024]{1,0:T(8,128)(2,1)S(1)}, bf16[128,1024]{1,0:T(8,128)(2,1)S(1)}, u32[]{:S(2)}, u32[]{:S(2)}) collective-permute-start(bf16[128,1024]{1,0:T(8,128)(2,1)S(1)} %add_convert_fusion.refs_1_.refs_5_), channel_id=1, source_target_pairs={{0,1},{1,0},{2,3},{3,2},{4,5},{5,4},{6,7},{7,6},{8,9},{9,8},{10,11... | collective-permute-start | bytes 786440 | tf_op jit(solution)/shard_map/ppermute | solution.py:25
  143.5 7.0 %collective-permute-start.30 = (bf16[128,1024]{1,0:T(8,128)(2,1)S(1)}, bf16[128,1024]{1,0:T(8,128)(2,1)S(1)}, u32[]{:S(2)}, u32[]{:S(2)}) collective-permute-start(bf16[128,1024]{1,0:T(8,128)(2,1)S(1)} %collective-permute-done.26.refs_6_), channel_id=1, source_target_pairs={{0,1},{1,0},{2,3},{3,2},{4,5},{5,4},{6,7},{7,6},{8,9},{9,8},{10,11... | collective-permute-start | bytes 786440 | tf_op jit(solution)/shard_map/ppermute | solution.py:25
  143.7 6.8 %collective-permute-start.31 = (bf16[128,1024]{1,0:T(8,128)(2,1)S(1)}, bf16[128,1024]{1,0:T(8,128)(2,1)S(1)}, u32[]{:S(2)}, u32[]{:S(2)}) collective-permute-start(bf16[128,1024]{1,0:T(8,128)(2,1)S(1)} %collective-permute-done.27.refs_7_), channel_id=1, source_target_pairs={{0,1},{1,0},{2,3},{3,2},{4,5},{5,4},{6,7},{7,6},{8,9},{9,8},{10,11... | collective-permute-start | bytes 786440 | tf_op jit(solution)/shard_map/ppermute | solution.py:25
  146.2 4.3 %collective-permute-start.32 = (bf16[128,1024]{1,0:T(8,128)(2,1)S(1)}, bf16[128,1024]{1,0:T(8,128)(2,1)S(1)}, u32[]{:S(2)}, u32[]{:S(2)}) collective-permute-start(bf16[128,1024]{1,0:T(8,128)(2,1)S(1)} %collective-permute-done.28.refs_8_), channel_id=1, source_target_pairs={{0,1},{1,0},{2,3},{3,2},{4,5},{5,4},{6,7},{7,6},{8,9},{9,8},{10,11... | collective-permute-start | bytes 786440 | tf_op jit(solution)/shard_map/ppermute | solution.py:25
  153.1 14.7 %collective-permute-start.33 = (bf16[512,256]{1,0:T(8,128)(2,1)}, bf16[512,256]{1,0:T(8,128)(2,1)}, u32[]{:S(2)}, u32[]{:S(2)}) collective-permute-start(bf16[512,256]{1,0:T(8,128)(2,1)} %get-tuple-element.41), channel_id=1, source_target_pairs={{0,32},{1,33},{2,34},{3,35},{4,36},{5,37},{6,38},{7,39},{8,40},{9,... | collective-permute-start | bytes 786440 | tf_op jit(solution)/shard_map/ppermute | solution.py:25
  153.2 14.7 %collective-permute-start.34 = (bf16[512,256]{1,0:T(8,128)(2,1)}, bf16[512,256]{1,0:T(8,128)(2,1)}, u32[]{:S(2)}, u32[]{:S(2)}) collective-permute-start(bf16[512,256]{1,0:T(8,128)(2,1)} %get-tuple-element.42), channel_id=1, source_target_pairs={{0,64},{1,65},{2,66},{3,67},{4,68},{5,69},{6,70},{7,71},{8,72},{9,... | collective-permute-start | bytes 786440 | tf_op jit(solution)/shard_map/ppermute | solution.py:25
  156.1 11.8 %collective-permute-start.35 = (bf16[512,256]{1,0:T(8,128)(2,1)}, bf16[512,256]{1,0:T(8,128)(2,1)}, u32[]{:S(2)}, u32[]{:S(2)}) collective-permute-start(bf16[512,256]{1,0:T(8,128)(2,1)} %get-tuple-element.43), channel_id=1, source_target_pairs={{0,96},{1,97},{2,98},{3,99},{4,100},{5,101},{6,102},{7,103},{8,104... | collective-permute-start | bytes 786440 | tf_op jit(solution)/shard_map/ppermute | solution.py:25
  156.9 38.9 %copy-start = (bf16[1024,128]{1,0:T(8,128)(2,1)S(1)}, bf16[1024,128]{1,0:T(8,128)(2,1)}, u32[]{:S(2)}) copy-start(bf16[1024,128]{1,0:T(8,128)(2,1)} %fusion.11.left_ref) | copy-start | bytes 786436
  167.9 28.0 %collective-permute-start.39 = (bf16[128,4096]{1,0:T(8,128)(2,1)S(1)}, bf16[128,4096]{1,0:T(8,128)(2,1)S(1)}, u32[]{:S(2)}, u32[]{:S(2)}) collective-permute-start(bf16[128,4096]{1,0:T(8,128)(2,1)S(1)} %get-tuple-element.52), channel_id=1, source_target_pairs={{32,0},{33,1},{34,2},{35,3},{36,4},{37,5},{38,6},{39,7},{40,8},{41... | collective-permute-start | bytes 3145736 | tf_op jit(solution)/shard_map/ppermute | solution.py:25
  173.4 44.3 %collective-permute-start.43 = (bf16[128,4096]{1,0:T(8,128)(2,1)S(1)}, bf16[128,4096]{1,0:T(8,128)(2,1)}, u32[]{:S(2)}, u32[]{:S(2)}) collective-permute-start(bf16[128,4096]{1,0:T(8,128)(2,1)S(1)} %get-tuple-element.60), channel_id=1, source_target_pairs={{64,32},{65,33},{66,34},{67,35},{68,36},{69,37},{70,38},{71,39},{7... | collective-permute-start | bytes 3145736 | tf_op jit(solution)/shard_map/ppermute | solution.py:25
  174.7 7.0 %collective-permute-start.36 = (bf16[128,256]{1,0:T(8,128)(2,1)}, bf16[128,256]{1,0:T(8,128)(2,1)S(1)}, u32[]{:S(2)}, u32[]{:S(2)}) collective-permute-start(bf16[128,256]{1,0:T(8,128)(2,1)} %get-tuple-element.45), channel_id=1, source_target_pairs={{0,6},{1,7},{2,0},{3,1},{4,2},{5,3},{6,4},{7,5},{8,14},{9,15},{10,... | collective-permute-start | bytes 196616 | tf_op jit(solution)/shard_map/ppermute | solution.py:25
  178.6 7.5 %collective-permute-start.37 = (bf16[128,256]{1,0:T(8,128)(2,1)}, bf16[128,256]{1,0:T(8,128)(2,1)}, u32[]{:S(2)}, u32[]{:S(2)}) collective-permute-start(bf16[128,256]{1,0:T(8,128)(2,1)} %get-tuple-element.46), channel_id=1, source_target_pairs={{0,4},{1,5},{2,6},{3,7},{4,0},{5,1},{6,2},{7,3},{8,12},{9,13},{10,... | collective-permute-start | bytes 196616 | tf_op jit(solution)/shard_map/ppermute | solution.py:25
  178.6 7.6 %collective-permute-start.38 = (bf16[128,256]{1,0:T(8,128)(2,1)}, bf16[128,256]{1,0:T(8,128)(2,1)}, u32[]{:S(2)}, u32[]{:S(2)}) collective-permute-start(bf16[128,256]{1,0:T(8,128)(2,1)} %get-tuple-element.47), channel_id=1, source_target_pairs={{0,2},{1,3},{2,4},{3,5},{4,6},{5,7},{6,0},{7,1},{8,10},{9,11},{10,... | collective-permute-start | bytes 196616 | tf_op jit(solution)/shard_map/ppermute | solution.py:25
  203.1 7.5 %collective-permute-start.40 = (bf16[128,1024]{1,0:T(8,128)(2,1)S(1)}, bf16[128,1024]{1,0:T(8,128)(2,1)S(1)}, u32[]{:S(2)}, u32[]{:S(2)}) collective-permute-start(bf16[128,1024]{1,0:T(8,128)(2,1)S(1)} %get-tuple-element.55), channel_id=1, source_target_pairs={{32,64},{33,65},{34,66},{35,67},{36,68},{37,69},{38,70},{39,71},{4... | collective-permute-start | bytes 786440 | tf_op jit(solution)/shard_map/ppermute | solution.py:25
  206.8 5.2 %collective-permute-start.41 = (bf16[128,1024]{1,0:T(8,128)(2,1)S(1)}, bf16[128,1024]{1,0:T(8,128)(2,1)S(1)}, u32[]{:S(2)}, u32[]{:S(2)}) collective-permute-start(bf16[128,1024]{1,0:T(8,128)(2,1)S(1)} %get-tuple-element.56), channel_id=1, source_target_pairs={{32,96},{33,97},{34,98},{35,99},{36,100},{37,101},{38,102},{39,103... | collective-permute-start | bytes 786440 | tf_op jit(solution)/shard_map/ppermute | solution.py:25
  208.1 6.7 %collective-permute-start.42 = (bf16[128,1024]{1,0:T(8,128)(2,1)S(1)}, bf16[128,1024]{1,0:T(8,128)(2,1)S(1)}, u32[]{:S(2)}, u32[]{:S(2)}) collective-permute-start(bf16[128,1024]{1,0:T(8,128)(2,1)S(1)} %get-tuple-element.57), channel_id=1, source_target_pairs={{32,0},{33,1},{34,2},{35,3},{36,4},{37,5},{38,6},{39,7},{40,8},{41... | collective-permute-start | bytes 786440 | tf_op jit(solution)/shard_map/ppermute | solution.py:25
  (29 other events, 124.7 us)
Sparse Core Ops, SparseCore 0:
  10.8 109.2 all-gather.4
  122.3 67.9 all-gather.2
